TPU v7x, 128 devices: a whole 4x4x4 slice. The times are simulated.
128 devices in a mesh: scene: 16 (over y, z_hi, core), batch: 8 (over x, z_lo).
Axes of the slice: x: 4, y: 4, z: 4 (z_hi: 2, z_lo: 2; z = z_hi * 2 + z_lo), core: 2. Of those that a mesh axis runs over, the one named last changes fastest.
Arguments:
- tokens: float32 [8, 6144, 384], P('batch', 'scene'), may hold values from -6 to 6
- nbr_offset: int32 [27, 8, 6144], P(None, 'batch', 'scene'), may hold values from -64 to 65, as said below
- cotangent: float32 [8, 6144, 384], P('batch', 'scene'), may hold values from -6 to 6
- conv_weight: float32 [27, 384], replicated, may hold values from -1.25 to 1.25
- w_qkv: float32 [384, 1152], replicated, may hold values from -0.3125 to 0.3125
- w_out: float32 [384, 384], replicated, may hold values from -0.3125 to 0.3125
- score_bias: float32 [24, 32, 32], replicated, may hold values from -6 to 400
- w_up: float32 [384, 1536], replicated, may hold values from -0.3125 to 0.3125
- w_down: float32 [1536, 384], replicated, may hold values from -0.15625 to 0.15625
Outputs:
- block_out: float32 [8, 6144, 384], P('batch', 'scene')
- grad_mid: float32 [8, 6144, 384], P('batch', 'scene')
- grad_up: float32 [384, 1536], P('scene', 'batch')
- grad_down: float32 [1536, 384], P('scene', 'batch')
Inputs may be any that keep to these rules, and one draw needn't show every extreme that they name: `nbr_offset`: the middle tap is 0 for every token; the value 64 + 1 marks a missing neighbour.
All inputs are finite; a program needn't handle non-finite values.
Results may differ from a plain program's by a relative error of at most 0.000075.
Values sent between devices are 32-bit elements; how exact they have to be, the bound alone decides.
No kernel may reach another device: no remote copies, remote signals or barrier semaphores. Data moves between devices by JAX's collectives and lax.ppermute only.
A program may use at most 128 MiB of HBM per device.

v0:
```python
import jax
import jax.numpy as jnp
from jax import lax
from jax.sharding import PartitionSpec as P

GROUP = 32
HALO = 64


def extended_2(block, sides, width):
    for axis, dim in sides:
        count = lax.axis_size(axis)
        forward = [(i, i + 1) for i in range(count - 1)]
        backward = [(target, source) for source, target in forward]
        low = lax.ppermute(
            lax.slice_in_dim(block, block.shape[dim] - width, None, axis=dim), axis, forward
        )
        high = lax.ppermute(lax.slice_in_dim(block, 0, width, axis=dim), axis, backward)
        block = jnp.concatenate([low, block, high], axis=dim)
    return block


def layer_norm(values):
    average = jnp.mean(values, axis=-1, keepdims=True)
    centered = values - average
    variance = jnp.mean(centered * centered, axis=-1, keepdims=True)
    return centered * lax.rsqrt(variance + 1e-05)


def attend_groups(arrived, score_bias):
    per_group, scene_count, group_count, channels = arrived.shape
    feature_width = channels // 3
    head_count = score_bias.shape[0]
    head_dim = feature_width // head_count
    shape_five = (per_group, scene_count, group_count, head_count, head_dim)
    query = arrived[..., :feature_width].reshape(shape_five)
    keys = arrived[..., feature_width : 2 * feature_width].reshape(shape_five)
    values = arrived[..., 2 * feature_width :].reshape(shape_five)
    bias = score_bias.reshape(head_count, scene_count, per_group, scene_count, per_group)
    scores = jnp.einsum(
        "ksghd,ltghd->ghsktl", query, keys, precision=lax.Precision.HIGHEST
    ) * head_dim ** (-0.5)
    scores = scores + bias[None]
    flat_shape = (group_count, head_count, scene_count, per_group, scene_count * per_group)
    weights = jax.nn.softmax(scores.reshape(flat_shape), axis=-1).reshape(scores.shape)
    mixed = jnp.einsum("ghsktl,ltghd->ksghd", weights, values, precision=lax.Precision.HIGHEST)
    return mixed.reshape(per_group, scene_count, group_count, feature_width)


def mlp_branch(middle, w_up, w_down):
    normed = layer_norm(middle)
    hidden = jnp.dot(
        normed, w_up, precision=lax.Precision.HIGHEST, preferred_element_type=jnp.float32
    )
    activation = jax.nn.gelu(hidden, approximate=False)
    return middle + jnp.dot(
        activation, w_down, precision=lax.Precision.HIGHEST, preferred_element_type=jnp.float32
    )


def on_device(tokens, nbr_offset, cotangent, conv_weight, w_qkv, w_out, score_bias, w_up, w_down):
    local = tokens[0]
    tok_dev, feature_width = local.shape
    scene_count = lax.axis_size("scene")
    batch_count = lax.axis_size("batch")
    extended = extended_2(local, (("scene", 0),), HALO)
    extended = jnp.concatenate([extended, jnp.zeros((1, feature_width), jnp.float32)], axis=0)
    row_ids = jnp.arange(tok_dev, dtype=jnp.int32)
    offsets = nbr_offset[:, 0, :]
    row_index = jnp.where(offsets > HALO, tok_dev + 2 * HALO, row_ids[None, :] + HALO + offsets)
    neighbours = jnp.take(extended, row_index, axis=0)
    stencil = jnp.sum(neighbours * conv_weight[:, None, :], axis=0)
    first = local + stencil
    normed = layer_norm(first)
    per_group = GROUP // scene_count
    group_count = tok_dev // GROUP
    qkv = jnp.dot(
        normed, w_qkv, precision=lax.Precision.HIGHEST, preferred_element_type=jnp.float32
    )
    qkv = qkv.reshape(per_group, scene_count, group_count, 3 * feature_width)
    attended = attend_groups(
        lax.all_to_all(qkv, "scene", split_axis=1, concat_axis=1, tiled=True), score_bias
    )
    returned = lax.all_to_all(attended, "scene", split_axis=1, concat_axis=1, tiled=True).reshape(
        tok_dev, feature_width
    )
    middle = first + jnp.dot(
        returned, w_out, precision=lax.Precision.HIGHEST, preferred_element_type=jnp.float32
    )
    block_out, pullback = jax.vjp(mlp_branch, middle, w_up, w_down)
    grad_mid, grad_up, grad_down = pullback(cotangent[0])
    grad_scale = lax.rsqrt(jnp.asarray(tok_dev * scene_count * batch_count, jnp.float32))
    grad_up = grad_up * grad_scale
    grad_down = grad_down * grad_scale
    part_up, part_down = (
        lax.psum_scatter(grad_up, "scene", scatter_dimension=0, tiled=True),
        lax.psum_scatter(grad_down, "scene", scatter_dimension=0, tiled=True),
    )
    shard_up, shard_down = (
        lax.psum_scatter(part_up, "batch", scatter_dimension=1, tiled=True),
        lax.psum_scatter(part_down, "batch", scatter_dimension=1, tiled=True),
    )
    return (block_out[None], grad_mid[None], shard_up, shard_down)


def solution(mesh):
    placed = (
        P("batch", "scene", None),
        P(None, "batch", "scene"),
        P("batch", "scene", None),
        P(),
        P(),
        P(),
        P(),
        P(),
        P(),
    )
    return jax.shard_map(
        on_device,
        mesh=mesh,
        in_specs=placed,
        out_specs=(
            P("batch", "scene", None),
            P("batch", "scene", None),
            P("scene", "batch"),
            P("scene", "batch"),
        ),
        check_vma=False,
    )
```

profile of v0, /device:TPU:0, one launch (start us, length us, event | category | flops | bytes accessed | tf_op | source)
XLA Modules:
  0.0 481.8 jit_solution(2089269034716840844)
XLA Ops:
  7.2 1.5 copy.72
  8.7 0.9 slice_bitcast_fusion.1
  9.6 2.0 collective-permute-start
  11.5 1.3 collective-permute-start.1
  12.8 1.6 fusion.46
  14.4 1.4 reshape.165
  15.8 1.4 pad_clamp_fusion
  17.2 0.8 compare_and_fusion
  18.0 1.0 squeeze.16
  19.0 2.3 maximum_maximum_fusion
  21.4 1.5 copy.75
  22.9 26.4 %gather_fusion = f32[10368,384]{1,0:T(8,128)} fusion(f32[513,384]{1,0:T(8,128)S(1)} %copy.75, s32[11264]{0:T(1024)S(1)} %copy-done.12), kind=kCustom, calls=%fused_computation | custom fusion | bytes 31891968 | tf_op jit(solution)/shard_map/jit(_take)/gather | solution.py:71
  49.3 7.8 %multiply_reduce_fusion = f32[384,384]{1,0:T(8,128)} fusion(f32[27,384,384]{2,1,0:T(8,128)} %bitcast.94, f32[27,384]{1,0:T(8,128)} %param.12, pred[27,384]{1,0:T(8,128)(4,1)S(1)} %compare_and_fusion), kind=kLoop, calls=%fused_computation.1 | loop fusion | flops 11796480 | bytes 16566912 | tf_op jit(solution)/shard_map/reduce_sum | solution.py:72
  57.1 1.3 copy.76
  58.4 0.1 fusion.50
  58.5 0.6 copy-done.13
  59.2 0.7 multiply_reduce_fusion.3
  59.9 0.8 div.36
  60.6 2.0 reduce_sum.83
  62.6 1.3 add_rsqrt_fusion
  63.9 1.4 rsqrt.22
  65.3 6.3 %fusion.20 = f32[2,16,12,1152]{3,2,1,0:T(8,128)S(1)} fusion(f32[384,1152]{1,0:T(8,128)} %param.13, f32[2,16,12,384]{3,2,1,0:T(8,128)} %squeeze.16, f32[2,16,12,384]{3,2,1,0:T(8,128)} %reduce_sum.83, f32[2,16,12]{2,1,0:T(8,128)} %rsqrt.22, f32[2,16,12]{2,1,0:T(8,128)S(1)} %div.36), kind=kOutput, calls=%fused_computation.33 | convolution fusion | flops 2038874112 | bytes 4721664 | tf_op jit(solution)/shard_map/dot_general | solution.py:77
  71.6 2.6 copy.78
  74.2 11.9 %all-to-all-start = ((f32[2,16,12,1152]{3,0,2,1:T(2,128)}), f32[2,16,12,1152]{3,0,2,1:T(2,128)}, u32[]{:S(2)}, u32[]{:S(2)}) async-start(f32[2,16,12,1152]{3,0,2,1:T(2,128)} %copy.78), calls=%async_computation | async-start | bytes 3538944 | tf_op jit(solution)/shard_map/all_to_all | solution.py:82
  86.0 0.3 reduce-scatter.9.cloned.1.call-start
  86.3 1.3 copy.84
  87.6 1.6 copy.85
  89.2 22.6 %all-to-all-done = f32[2,16,12,1152]{3,0,2,1:T(2,128)} async-done(((f32[2,16,12,1152]{3,0,2,1:T(2,128)}), f32[2,16,12,1152]{3,0,2,1:T(2,128)}, u32[]{:S(2)}, u32[]{:S(2)}) %all-to-all-start) | async-done | bytes 1769504 | tf_op jit(solution)/shard_map/all_to_all | solution.py:82
  111.8 3.1 fusion.51
  114.8 4.3 reshape.178
  119.1 4.4 reshape.179
  123.5 3.2 reshape.177
  126.7 53.3 %fusion.4 = (f32[12,24,16,2]{2,3,1,0:T(2,128)S(1)}, f32[12,24,2,16,2,16]{5,3,4,2,1,0:T(8,128)S(1)}) fusion(f32[24,16,2,16,2]{1,3,2,4,0:T(8,128)} %copy.85, f32[2,16,12,24,16,1]{4,3,0,2,1,5:T(8,128)} %bitcast.97, f32[2,16,12,24,16,1]{4,3,0,2,1,5:T(8,128)} %bitcast.96), kind=kOutput, calls=%fused_computation.8 | convolution fusion | flops 57498624 | bytes 2494464 | tf_op jit(solution)/shard_map/ksghd,ltghd->ghsktl/dot_general | solution.py:40
  180.0 3.5 fusion.3
  183.5 12.6 %fusion.15 = f32[2,16,12,24,16]{1,4,0,3,2:T(8,128)} fusion(f32[2,16,12,24,16,1]{4,3,0,2,1,5:T(8,128)S(1)} %bitcast.98, f32[12,24,2,16,2,16]{5,3,4,2,1,0:T(8,128)S(1)} %get-tuple-element.26, f32[12,24,16,2]{2,3,1,0:T(2,128)S(1)} %fusion.3, f32[12,24,16,2]{2,3,1,0:T(2,128)S(1)} %get-tuple-element.25, f32[24,16,2,16,2]{1,3,2,4,0:T(8,128)S(1)} %copy-done.7), kind=kOutput, calls=%fused_computation.31 | convolution fusion | flops 57802752 | bytes 2531328 | tf_op jit(solution)/shard_map/ghsktl,ltghd->ksghd/dot_general | solution.py:46
  196.1 6.7 %copy.119 = f32[2,16,12,24,16]{4,3,0,2,1:T(8,128)} copy(f32[2,16,12,24,16]{1,4,0,3,2:T(8,128)} %fusion.15) | data formatting | bytes 1179648 | tf_op jit(solution)/shard_map/reshape | solution.py:47
  202.8 4.3 reshape.180
  207.1 17.1 %all_to_all.10 = f32[2,16,12,384]{3,0,2,1:T(2,128)S(1)} all-to-all(f32[2,16,12,384]{3,0,2,1:T(2,128)S(1)} %reshape.180), channel_id=1, replica_groups=mesh['scene'=16,'batch'=8] {'scene'}, dimensions={1} | all-to-all | bytes 1179648 | tf_op jit(solution)/shard_map/all_to_all | solution.py:84
  224.2 0.9 copy.90
  225.2 2.0 reshape.162
  227.2 2.8 fusion.52
  230.0 0.1 multiply_reduce_fusion.2
  230.1 8.7 %fusion.9 = (f32[384,1536]{1,0:T(8,128)S(1)}, f32[384,1536]{1,0:T(8,128)S(1)}) fusion(f32[384,1536]{1,0:T(8,128)S(1)} %copy-done, f32[384,384]{0,1:T(8,128)S(1)} %get-tuple-element.28, f32[384]{0:T(512)S(1)} %fusion.47, f32[384]{0:T(512)S(1)} %broadcast_multiply_fusion), kind=kOutput, calls=%fused_computation.16 | convolution fusion | flops 2754772992 | bytes 7670784 | tf_op jit(solution)/shard_map/jvp()/dot_general | solution.py:52
  238.8 5.0 %multiply_add_fusion = f32[384,1536]{1,0:T(8,128)S(1)} fusion(f32[384,1536]{1,0:T(8,128)S(1)} %get-tuple-element.29, f32[384,1536]{1,0:T(8,128)S(1)} %get-tuple-element.30, f32[1536,384]{1,0:T(8,128)S(1)} %copy-done.10, f32[1,384,384]{2,1,0:T(8,128)S(1)} %copy-done.11), kind=kOutput, calls=%fused_computation.17 | convolution fusion | flops 2725576704 | bytes 10027008 | tf_op jit(solution)/shard_map/transpose(jvp())/dot_general | solution.py:56
  243.9 1.5 copy-done.4
  245.3 5.3 %convolution_multiply_fusion.1 = f32[384,1536]{1,0:T(8,128)} fusion(f32[384,1536]{1,0:T(8,128)S(1)} %multiply_add_fusion, f32[384,384]{0,1:T(8,128)S(1)} %get-tuple-element.28, f32[384]{0:T(512)S(1)} %fusion.47, f32[384]{0:T(512)S(1)} %broadcast_multiply_fusion), kind=kOutput, calls=%fused_computation.15 | convolution fusion | flops 2718793728 | bytes 5311488 | tf_op jit(solution)/shard_map/transpose(jvp())/dot_general | solution.py:52
  250.7 0.0 reduce-scatter.11.cloned.1.call-start
  250.7 7.4 %convolution_multiply_fusion = f32[1536,384]{1,0:T(8,128)} fusion(f32[384,1536]{1,0:T(8,128)} %copy-done.5, f32[384,1536]{1,0:T(8,128)} %copy-done.6, f32[1,384,384]{2,1,0:T(8,128)S(1)} %copy-done.11), kind=kOutput, calls=%fused_computation.14 | convolution fusion | flops 2719678464 | bytes 7667712 | tf_op jit(solution)/shard_map/transpose(jvp())/dot_general | solution.py:56
  258.2 0.2 reduce-scatter.13.cloned.1.call-start
  258.4 1.1 copy.92
  259.5 5.6 %multiply_reduce_fusion.1 = (f32[384]{0:T(512)S(1)}, f32[384,384]{0,1:T(8,128)S(1)}) fusion(f32[384,384]{0,1:T(8,128)S(1)} %get-tuple-element.28, f32[384]{0:T(512)S(1)} %broadcast_multiply_fusion, f32[384,1536]{1,0:T(8,128)} %copy-done.4, f32[384,1536]{1,0:T(8,128)S(1)} %copy-done), kind=kOutput, calls=%fused_computation.49 | convolution fusion | flops 2718350848 | bytes 5901312 | tf_op jit(solution)/shard_map/transpose(jvp())/dot_general | solution.py:52
  265.1 0.2 fusion.44
  265.2 55.4 %reduce-scatter.9.cloned.1.call-done = f32[24,1536]{1,0:T(8,128)} async-done(((f32[384,1536]{1,0:T(8,128)}), f32[24,1536]{1,0:T(8,128)}) %reduce-scatter.9.cloned.1.call-update) | async-done | bytes 147472 | tf_op jit(solution)/shard_map/reduce_scatter | solution.py:96
  320.6 2.1 copy.120
  322.7 0.0 reduce-scatter.15.cloned.1.call-start
  322.8 2.0 fusion.32
  324.8 2.1 copy.94
  326.9 69.0 %reduce-scatter.11.cloned.1.call-done = f32[96,384]{1,0:T(8,128)} async-done(((f32[1536,384]{1,0:T(8,128)}), f32[96,384]{1,0:T(8,128)}) %reduce-scatter.11.cloned.1.call-update) | async-done | bytes 147472 | tf_op jit(solution)/shard_map/reduce_scatter | solution.py:97
  395.9 1.7 copy.122
  397.6 7.1 %fusion.22 = f32[1,384,384]{1,2,0:T(8,128)S(1)} fusion(f32[384,384]{0,1:T(8,128)S(1)} %get-tuple-element.28, f32[1536,384]{1,0:T(8,128)} %param.17, f32[384,1536]{1,0:T(8,128)} %copy-done.5, f32[384,1536]{1,0:T(8,128)} %copy-done.6), kind=kOutput, calls=%fused_computation.37 | convolution fusion | flops 2719236096 | bytes 8257536 | tf_op jit(solution)/shard_map/jvp()/dot_general | solution.py:56
  404.7 1.1 copy.93
  405.8 30.2 %reduce-scatter.13.cloned.1.call-done = f32[192,24]{1,0:T(8,128)} async-done(((f32[1536,24]{1,0:T(8,128)}), f32[192,24]{1,0:T(8,128)}) %reduce-scatter.13.cloned.1.call-update) | async-done | bytes 18448
  436.0 1.6 copy.121
  437.6 37.5 %reduce-scatter.15.cloned.1.call-done = f32[48,96]{1,0:T(8,128)} async-done(((f32[384,96]{1,0:T(8,128)}), f32[48,96]{1,0:T(8,128)}) %reduce-scatter.15.cloned.1.call-update) | async-done | bytes 18448
  (39 shorter events, 0.2 us)
Async XLA Ops:
  7.2 222.9 %copy-start = (f32[384,1536]{1,0:T(8,128)S(1)}, f32[384,1536]{1,0:T(8,128)}, u32[]{:S(2)}) copy-start(f32[384,1536]{1,0:T(8,128)} %param.16) | copy-start | bytes 7077892
  7.2 10.8 %copy-start.9 = (f32[1,384,384]{2,1,0:T(8,128)S(1)}, f32[1,384,384]{2,1,0:T(8,128)}, u32[]{:S(2)}) copy-start(f32[1,384,384]{2,1,0:T(8,128)} %param.9) | copy-start | bytes 1769476
  8.6 10.4 %copy-start.1 = (f32[1,384,384]{1,2,0:T(8,128)}, f32[1,384,384]{1,2,0:T(8,128)S(1)}, u32[]{:S(2)}) copy-start(f32[1,384,384]{1,2,0:T(8,128)S(1)} %copy.72) | copy-start | bytes 1769476
  9.6 9.4 %collective-permute-start = (f32[64,384]{0,1:T(8,128)}, f32[64,384]{0,1:T(8,128)}, u32[]{:S(2)}, u32[]{:S(2)}) collective-permute-start(f32[64,384]{0,1:T(8,128)} %get-tuple-element.23), channel_id=1, source_target_pairs={{0,8},{8,16},{16,24},{24,32},{32,40},{40,48},{48,56},{56,64},{64,7... | collective-permute-start | bytes 294920 | tf_op jit(solution)/shard_map/ppermute | solution.py:15
  11.5 7.5 %collective-permute-start.1 = (f32[64,384]{0,1:T(8,128)}, f32[64,384]{0,1:T(8,128)}, u32[]{:S(2)}, u32[]{:S(2)}) collective-permute-start(f32[64,384]{0,1:T(8,128)} %get-tuple-element.24), channel_id=1, source_target_pairs={{8,0},{16,8},{24,16},{32,24},{40,32},{48,40},{56,48},{64,56},{72,6... | collective-permute-start | bytes 294920 | tf_op jit(solution)/shard_map/ppermute | solution.py:18
  19.0 3.9 copy-start.12
  49.3 9.1 %copy-start.2 = (f32[1,384,384]{1,2,0:T(8,128)S(1)}, f32[1,384,384]{1,2,0:T(8,128)}, u32[]{:S(2)}) copy-start(f32[1,384,384]{1,2,0:T(8,128)} %copy-done.1) | copy-start | bytes 1769476
  58.4 13.2 %copy-start.3 = (f32[384,384]{0,1:T(8,128)}, f32[384,384]{0,1:T(8,128)S(1)}, u32[]{:S(2)}) copy-start(f32[384,384]{0,1:T(8,128)S(1)} %copy.76) | copy-start | bytes 1769476
  58.5 0.7 copy-start.13
  74.2 37.6 %all-to-all-start = ((f32[2,16,12,1152]{3,0,2,1:T(2,128)}), f32[2,16,12,1152]{3,0,2,1:T(2,128)}, u32[]{:S(2)}, u32[]{:S(2)}) async-start(f32[2,16,12,1152]{3,0,2,1:T(2,128)} %copy.78), calls=%async_computation | async-start | bytes 3538944 | tf_op jit(solution)/shard_map/all_to_all | solution.py:82
  86.0 234.6 %reduce-scatter.9.cloned.1.call-start = ((), (), s32[]{:S(2)}) async-start(), calls=%async_computation.6 | async-start | bytes 2506752 | tf_op jit(solution)/shard_map/reduce_scatter | solution.py:96
  126.7 53.3 %copy-start.7 = (f32[24,16,2,16,2]{1,3,2,4,0:T(8,128)S(1)}, f32[24,16,2,16,2]{1,3,2,4,0:T(8,128)}, u32[]{:S(2)}) copy-start(f32[24,16,2,16,2]{1,3,2,4,0:T(8,128)} %copy.85) | copy-start | bytes 294916
  180.0 3.5 copy-start.8
  230.1 8.7 %copy-start.10 = (f32[1536,384]{1,0:T(8,128)S(1)}, f32[1536,384]{1,0:T(8,128)}, u32[]{:S(2)}) copy-start(f32[1536,384]{1,0:T(8,128)} %param.17) | copy-start | bytes 7077892
  230.1 8.7 %copy-start.11 = (f32[1,384,384]{2,1,0:T(8,128)S(1)}, f32[1,384,384]{2,1,0:T(8,128)}, u32[]{:S(2)}) copy-start(f32[1,384,384]{2,1,0:T(8,128)} %param.11) | copy-start | bytes 1769476
  238.8 5.1 %copy-start.5 = (f32[384,1536]{1,0:T(8,128)}, f32[384,1536]{1,0:T(8,128)S(1)}, u32[]{:S(2)}) copy-start(f32[384,1536]{1,0:T(8,128)S(1)} %get-tuple-element.29) | copy-start | bytes 7077892
  238.8 5.1 %copy-start.6 = (f32[384,1536]{1,0:T(8,128)}, f32[384,1536]{1,0:T(8,128)S(1)}, u32[]{:S(2)}) copy-start(f32[384,1536]{1,0:T(8,128)S(1)} %get-tuple-element.30) | copy-start | bytes 7077892
  243.9 1.5 copy-start.4
  250.7 145.2 %reduce-scatter.11.cloned.1.call-start = ((), (), s32[]{:S(2)}) async-start(), calls=%async_computation.7 | async-start | bytes 2506752 | tf_op jit(solution)/shard_map/reduce_scatter | solution.py:97
  258.2 177.8 %reduce-scatter.13.cloned.1.call-start = ((), (), s32[]{:S(2)}) async-start(), calls=%async_computation.8 | async-start | bytes 884736
  322.7 152.3 %reduce-scatter.15.cloned.1.call-start = ((), (), s32[]{:S(2)}) async-start(), calls=%async_computation.9 | async-start | bytes 221184
Sparse Core Ops, SparseCore 0:
  250.8 69.8 reduce-scatter.8
  324.6 71.2 reduce-scatter.10
  398.3 37.6 reduce-scatter.12
  438.8 36.2 reduce-scatter.14
where the time goes:
time: 485 us; the launch traced here: 482 us
  waiting for transfers between devices  215 us (44%)
  matrix products  114 us (24%)
  local copies, waits for them, and re-layouts  84.2 us (17%)
  other arithmetic  21.7 us (4%)
  blocking collectives  17.1 us (4%)
  starting transfers between devices  15.7 us (3%)
  between operations  14.3 us (3%)
    reduce_scatter x1, waiting for transfers between devices, on_device(): lax.psum_scatter(grad_down, 'scene', scatter_dimension=0, tiled=True)  69 us
    unnamed x6, waiting for transfers between devices  67.8 us
    reduce_scatter x1, waiting for transfers between devices, on_device(): lax.psum_scatter(grad_up, 'scene', scatter_dimension=0, tiled=True)  55.4 us
    dot_general x1, matrix products, attend_groups(): jnp.einsum('ksghd,ltghd->ghsktl', query, keys, precision=lax.Precision.HI...  53.3 us
    gather x1, local copies, waits for them, and re-layouts, on_device(): neighbours = jnp.take(extended, row_index, axis=0)  26.4 us
    all_to_all x1, waiting for transfers between devices, on_device(): lax.all_to_all(qkv, 'scene', split_axis=1, concat_axis=1, tiled=True)  22.6 us
    dot_general x3, matrix products, mlp_branch(): jnp.dot(activation, w_down, precision=lax.Precision.HIGHEST, preferred_el...  19.6 us
    dot_general x3, matrix products, mlp_branch(): jnp.dot(normed, w_up, precision=lax.Precision.HIGHEST, preferred_element_...  19.6 us
  transfers between devices with their start and end apart: 7, of which 5 were waited for; matrix products, arithmetic and copies ran while one was open for 8% of the time, Pallas kernels for 0%

commit v1 on v0

v1 whole, which is shorter than its diff:
```python
import functools

import jax
import jax.numpy as jnp
from jax import lax
from jax.experimental import pallas as pl
from jax.experimental.pallas import tpu as pltpu
from jax.sharding import Mesh
from jax.sharding import PartitionSpec as P

D = 384
FF = 1536
TAPS = 27
HALO = 64
TOK = 384
SCENE = 16
UNITS = 24
HALF = FF // 2
SCENE_AXES = ("y", "zh", "c")
BATCH_AXES = ("x", "zl")
CHIP_AXES = ("y", "zh", "x", "zl")
F32 = jnp.float32
BF16 = jnp.bfloat16
NN = (((1,), (0,)), ((), ()))
NT = (((1,), (1,)), ((), ()))
VMEM_SPEC = pl.BlockSpec(memory_space=pltpu.VMEM)
PARAMS = pltpu.CompilerParams(vmem_limit_bytes=58 * 1024 * 1024)


def parts_of(values):
    high = values.astype(BF16)
    return high, (values - high.astype(F32)).astype(BF16)


def dot(a, b, dims=NN):
    return lax.dot_general(a, b, dims, preferred_element_type=F32)


def dot3(a, b, dims=NN):
    return dot(a[0], b[0], dims) + (dot(a[0], b[1], dims) + dot(a[1], b[0], dims))


def normalise(values):
    average = jnp.mean(values, axis=-1, keepdims=True)
    centered = values - average
    variance = jnp.mean(centered * centered, axis=-1, keepdims=True)
    scale = lax.rsqrt(variance + 1e-05)
    return centered * scale, scale


def by_unit(ref):
    rows = []
    for unit in range(UNITS):
        tiles = [ref[pl.ds(UNITS * t + unit, SCENE, stride=3 * UNITS), :] for t in range(3)]
        rows.append(jnp.concatenate(tiles, axis=1))
    return jnp.concatenate(rows, axis=0)


def by_member(ref, values):
    for unit in range(UNITS):
        for t in range(3):
            ref[pl.ds(UNITS * t + unit, SCENE, stride=3 * UNITS), :] = values[
                SCENE * unit : SCENE * (unit + 1), 128 * t : 128 * (t + 1)
            ]


def conv_kernel(tok_ref, low_ref, high_ref, nbr_ref, weight_ref, sent_ref):
    middle_tap = TAPS // 2
    taps = [a for a in range(TAPS) if a != middle_tap]
    chunk = 13
    tok = tok_ref[...]
    ext = jnp.concatenate([low_ref[...], tok, high_ref[...]], axis=0)
    ext_high, ext_low = parts_of(ext)
    offsets = jnp.concatenate([nbr_ref[:, 0, :], jnp.zeros((5, TOK), jnp.int32)], axis=0).T
    row = lax.broadcasted_iota(jnp.int32, (128, 32), 0)
    lanes = lax.broadcasted_iota(jnp.int32, (128, 256), 1)
    done = []
    for block in range(3):
        rows = slice(128 * block, 128 * (block + 1))
        window = slice(128 * block, 128 * block + 256)
        table = jnp.concatenate([ext_high[window], ext_low[window]], axis=1)
        off = offsets[rows]
        index = jnp.where(off > HALO, -1, off + row + HALO)
        acc = tok[rows] + tok[rows] * weight_ref[middle_tap : middle_tap + 1, :]
        for start in range(0, len(taps), chunk):
            hits = [
                jnp.where(index[:, a : a + 1] == lanes, 1.0, 0.0).astype(BF16)
                for a in taps[start : start + chunk]
            ]
            picked = dot(jnp.concatenate(hits, axis=0), table)
            for i, a in enumerate(taps[start : start + chunk]):
                piece = picked[128 * i : 128 * (i + 1)]
                acc = acc + (piece[:, :D] + piece[:, D:]) * weight_ref[a : a + 1, :]
        done.append(acc)
    by_member(sent_ref, jnp.concatenate(done, axis=0))


def attention_kernel(got_ref, qkv_ref, wout_ref, bias_ref, sent_ref, scores_ref):
    normed, _ = normalise(by_unit(got_ref))
    qkv = dot3(parts_of(normed), parts_of(qkv_ref[...]))
    bias = bias_ref[...]
    lane = lax.broadcasted_iota(jnp.int32, (16, 128), 1)
    head_of = lane // 16
    row_head = (lax.broadcasted_iota(jnp.int32, (256, 128), 0) // 16) % 8
    ones = jnp.where(row_head == lax.broadcasted_iota(jnp.int32, (256, 128), 1) // 16, 1.0, 0.0).astype(BF16)
    lane_all = lax.broadcasted_iota(jnp.int32, (TOK, 128), 1)

    def members(values, group):
        return values[16 * group : 16 * group + 16], values[192 + 16 * group : 208 + 16 * group]

    def spread(values, group):
        pieces = []
        for piece in members(values, group):
            pieces += [jnp.where(head_of == h, piece, 0.0) for h in range(8)]
        return parts_of(jnp.concatenate(pieces, axis=0))

    attended = []
    for t in range(3):
        cols = slice(128 * t, 128 * (t + 1))
        query = qkv[:, :D][:, cols] * 0.25
        keys = qkv[:, D : 2 * D][:, cols]
        vals = qkv[:, 2 * D :][:, cols]
        for g in range(12):
            q_high, q_low = parts_of(jnp.concatenate(members(query, g), axis=0))
            k_high, k_low = spread(keys, g)
            both = dot(jnp.concatenate([q_high, q_low], axis=0), k_high, NT)
            score = both[:32] + (both[32:] + dot(q_high, k_low, NT))
            scores_ref[32 * g : 32 * g + 32, :] = score + bias[:, 256 * t : 256 * (t + 1)]
        score = scores_ref[...]
        top = jnp.maximum(score[:, :128], score[:, 128:])
        for shift in (8, 4, 2, 1):
            other = jnp.where(
                lane_all % (2 * shift) < shift,
                pltpu.roll(top, 128 - shift, 1),
                pltpu.roll(top, shift, 1),
            )
            top = jnp.maximum(top, other)
        weight = jnp.exp(score - jnp.concatenate([top, top], axis=1))
        w_high, w_low = parts_of(weight)
        pieces = []
        for g in range(12):
            v_high, v_low = spread(vals, g)
            wide = jnp.concatenate([v_high, ones], axis=1)
            rows = slice(32 * g, 32 * g + 32)
            both = dot(jnp.concatenate([w_high[rows], w_low[rows]], axis=0), wide)
            total = both[:32] + both[32:]
            mixed = total[:, :128] + dot(w_high[rows], v_low)
            pieces.append(mixed / total[:, 128:])
        attended.append(
            jnp.concatenate([p[:16] for p in pieces] + [p[16:] for p in pieces], axis=0)
        )
    attended = jnp.concatenate(attended, axis=1)
    by_member(sent_ref, dot3(parts_of(attended), parts_of(wout_ref[...])))


def gauss(x):
    z = jnp.clip(x * 0.7071067811865476, -3.832506856900711, 3.832506856900711)
    s = z * z
    top = 0.00022905065861350646
    for c in (0.0034082910107109506, 0.050955695062380861, 0.18520832239976145, 1.128379143519084):
        top = top * s + c
    low = -1.1791602954361697e-7
    for c in (
        0.000023547966471313185,
        0.0010179625278914885,
        0.014070470171167667,
        0.11098505178285362,
        0.49746925110067538,
        1.0,
    ):
        low = low * s + c
    return 0.5 + 0.5 * (z * top / low), 0.3989422804014327 * jnp.exp(-0.5 * (x * x))


def branch_kernel(
    first_ref, ret_ref, cot_ref, up_ref, down_ref,
    out_ref, mid_grad_ref, keep_ref, send_ref,
    mid_ref, normed_ref, scale_ref, nt_ref, cot_ref3, ct_ref, grad_up_ref, grad_down_ref,
):
    step = pl.program_id(0)

    @pl.when(step == 0)
    def _():
        mid = by_unit(first_ref) + by_unit(ret_ref)
        normed, scale = normalise(mid)
        mid_ref[...] = mid
        normed_ref[...] = normed
        scale_ref[...] = jnp.broadcast_to(scale, scale_ref.shape)
        n_high, n_low = parts_of(normed.T)
        nt_ref[0], nt_ref[1] = n_high, n_low
        cot = cot_ref[...]
        cot_ref3[0], cot_ref3[1] = parts_of(cot)
        ct_ref[0], ct_ref[1] = parts_of(cot.T)

    cot = (cot_ref3[0], cot_ref3[1])
    up = parts_of(up_ref[...])
    down = parts_of(down_ref[...])
    hidden = dot3(parts_of(normed_ref[...]), up)
    chance, density = gauss(hidden)
    active = parts_of(hidden * chance)
    d_hidden = parts_of(dot3(cot, down, NT) * (chance + hidden * density))
    cols = pl.ds(pl.multiple_of(step * HALF, HALF), HALF)
    grad_down_ref[:, cols] = dot3((ct_ref[0], ct_ref[1]), active)
    grad_up_ref[:, cols] = dot3((nt_ref[0], nt_ref[1]), d_hidden)
    out_part = dot3(active, down)
    norm_part = dot3(d_hidden, up, NT)

    @pl.when(step == 0)
    def _():
        out_ref[...] = mid_ref[...] + out_part
        mid_grad_ref[...] = norm_part

    @pl.when(step == 1)
    def _():
        out_ref[...] += out_part
        d_normed = mid_grad_ref[...] + norm_part
        normed = normed_ref[...]
        shift = jnp.mean(d_normed, axis=-1, keepdims=True)
        slope = jnp.mean(d_normed * normed, axis=-1, keepdims=True)
        mid_grad_ref[...] = cot_ref[...] + scale_ref[:, :1] * (d_normed - shift - normed * slope)
        pack(grad_up_ref, grad_down_ref, keep_ref, send_ref)


def pack(grad_up_ref, grad_down_ref, keep_ref, send_ref):
    core = lax.axis_index("c")
    lane = lax.broadcasted_iota(jnp.int32, (8, 128), 1)
    left = lane < 64
    segment = lane // 32
    first_core = jnp.full((72, 128), core, jnp.int32) == 0

    def piece(quarter, sigma, b):
        g, beta = b // 2, b % 2
        row = pl.multiple_of((4 * quarter + sigma) * 24, 8)

        def up_tile(i, t):
            return grad_up_ref[pl.ds(row + 8 * i, 8), 384 * g + 128 * t : 384 * g + 128 * (t + 1)]

        def down_tile(i, t):
            col = pl.multiple_of(384 * quarter + 128 * t, 128)
            return grad_down_ref[48 * b + 8 * i : 48 * b + 8 * (i + 1), pl.ds(col, 128)]

        full = [up_tile(i, 2 * beta) for i in range(3)]
        m0, m1, m2 = [up_tile(i, 1) for i in range(3)]
        own = left if beta == 0 else jnp.logical_not(left)
        if sigma == 0:
            c = [down_tile(i, 0) for i in range(6)]
        elif sigma == 1:
            c = [jnp.where(segment == 3, down_tile(i, 0), down_tile(i, 1)) for i in range(6)]
        elif sigma == 2:
            c = [jnp.where(segment == 0, down_tile(i, 2), down_tile(i, 1)) for i in range(6)]
        else:
            c = [down_tile(i, 2) for i in range(6)]
        free = 3 - sigma
        hole = segment == free
        start = 2 if beta == 0 else 0
        turn = 32 * ((start - (free + 2)) % 4)
        extra = pltpu.roll(c[4], turn, 1) if turn else c[4]
        rows = full + [
            jnp.where(own, m0, pltpu.roll(m1, 64, 1)),
            jnp.where(own, m2, extra),
            jnp.where(hole, pltpu.roll(c[5], 96, 1), c[0]),
            jnp.where(hole, pltpu.roll(c[5], 64, 1), c[1]),
            jnp.where(hole, pltpu.roll(c[5], 32, 1), c[2]),
            jnp.where(hole, pltpu.roll(c[4], 96, 1), c[3]),
        ]
        return jnp.concatenate(rows, axis=0)

    def quarter_body(quarter, carry):
        for pair in range(2):
            for b in range(8):
                even = piece(quarter, 2 * pair, b)
                odd = piece(quarter, 2 * pair + 1, b)
                where = (2 * quarter + pair) * 8 + b
                keep_ref[where] = jnp.where(first_core, even, odd)
                send_ref[where] = jnp.where(first_core, odd, even)
        return carry

    lax.fori_loop(0, 4, quarter_body, 0)


def finish_kernel(pieces_ref, up_ref, down_ref):
    scale = (TOK * 128) ** -0.5
    z = pieces_ref[0]
    for i in range(1, 64):
        z = z + pieces_ref[i]
    z = z * scale
    beta = lax.axis_index("zl")
    sigma = 2 * lax.axis_index("zh") + lax.axis_index("c")
    lane = lax.broadcasted_iota(jnp.int32, (8, 128), 1)
    lane24 = lax.broadcasted_iota(jnp.int32, (24, 128), 1)
    even24 = jnp.full((24, 128), beta, jnp.int32) == 0
    even = jnp.full((8, 128), beta, jnp.int32) == 0
    full, a, b = z[:24], z[24:32], z[32:40]
    turned = pltpu.roll(a, 64, 1)
    half = jnp.concatenate(
        [
            jnp.where(even, a, turned),
            jnp.where(even, turned, a),
            jnp.where(even, b, pltpu.roll(b, 64, 1)),
        ],
        axis=0,
    )
    swapped = pltpu.roll(full, 64, 1)
    up_ref[:, :128] = jnp.where(even24, full, jnp.where(lane24 < 64, half, swapped))
    up_ref[:, 128:] = jnp.where(even24, half, swapped)[:, :64]
    rest = z[40:]
    turned_rest = rest
    for k in range(1, 4):
        chosen = jnp.full((32, 128), sigma, jnp.int32) == k
        turned_rest = jnp.where(chosen, pltpu.roll(rest, 32 * k, 1), turned_rest)
    p0, p1, p2, p3 = [turned_rest[8 * i : 8 * (i + 1)] for i in range(4)]
    segment = lane // 32
    c5 = jnp.where(
        segment == 0,
        pltpu.roll(p0, 32, 1),
        jnp.where(segment == 1, pltpu.roll(p1, 64, 1), pltpu.roll(p2, 96, 1)),
    )
    tail = jnp.where(even, pltpu.roll(b, 96, 1), pltpu.roll(b, 32, 1))
    c4 = jnp.where(segment == 0, pltpu.roll(p3, 32, 1), tail)
    square = jnp.concatenate([p0, p1, p2, p3, c4, c5, jnp.zeros((80, 128), F32)], axis=0)
    down_ref[...] = square.T[:96, :48]


def shape(*dims):
    return jax.ShapeDtypeStruct(dims, F32)


def on_device(tokens, nbr_offset, cotangent, conv_weight, w_qkv, w_out, score_bias, w_up, w_down):
    local = tokens[0]
    forward = [(i, i + 1) for i in range(SCENE - 1)]
    backward = [(target, source) for source, target in forward]
    low = lax.ppermute(local[TOK - HALO :], SCENE_AXES, forward)
    high = lax.ppermute(local[:HALO], SCENE_AXES, backward)
    bias = score_bias.reshape(3, 8, 16, 2, 16, 2).transpose(3, 2, 0, 5, 1, 4).reshape(32, 768)

    sent = pl.pallas_call(
        conv_kernel,
        out_shape=shape(3 * TOK, 128),
        in_specs=[VMEM_SPEC] * 5,
        out_specs=VMEM_SPEC,
        compiler_params=PARAMS,
        name="conv",
    )(local, low, high, nbr_offset, conv_weight)

    def exchange(values):
        swapped = lax.all_to_all(
            values.reshape(SCENE, 3 * UNITS, 128), SCENE_AXES, split_axis=0, concat_axis=0, tiled=True
        )
        return swapped.reshape(3 * TOK, 128)

    mixed = pl.pallas_call(
        attention_kernel,
        out_shape=shape(3 * TOK, 128),
        in_specs=[VMEM_SPEC] * 4,
        out_specs=VMEM_SPEC,
        scratch_shapes=[pltpu.VMEM((TOK, 256), F32)],
        compiler_params=PARAMS,
        name="attention",
    )(exchange(sent), w_qkv, w_out, bias)
    returned = exchange(mixed)

    whole = lambda *dims: pl.BlockSpec(dims, lambda n: (0,) * len(dims))
    block_out, grad_mid, keep, send = pl.pallas_call(
        branch_kernel,
        grid=(2,),
        out_shape=(shape(TOK, D), shape(TOK, D), shape(64, 72, 128), shape(64, 72, 128)),
        in_specs=[
            whole(3 * TOK, 128),
            whole(3 * TOK, 128),
            whole(TOK, D),
            pl.BlockSpec((D, HALF), lambda n: (0, n)),
            pl.BlockSpec((HALF, D), lambda n: (n, 0)),
        ],
        out_specs=(whole(TOK, D), whole(TOK, D), whole(64, 72, 128), whole(64, 72, 128)),
        scratch_shapes=[
            pltpu.VMEM((TOK, D), F32),
            pltpu.VMEM((TOK, D), F32),
            pltpu.VMEM((TOK, 128), F32),
            pltpu.VMEM((2, D, TOK), BF16),
            pltpu.VMEM((2, TOK, D), BF16),
            pltpu.VMEM((2, D, TOK), BF16),
            pltpu.VMEM((D, FF), F32),
            pltpu.VMEM((D, FF), F32),
        ],
        compiler_params=PARAMS,
        name="branch",
    )(sent, returned, cotangent[0], w_up, w_down)

    got = lax.ppermute(send, "c", [(0, 1), (1, 0)])
    pieces = lax.all_to_all(keep + got, CHIP_AXES, split_axis=0, concat_axis=0, tiled=True)
    grad_up, grad_down = pl.pallas_call(
        finish_kernel,
        out_shape=(shape(24, 192), shape(96, 48)),
        in_specs=[VMEM_SPEC],
        out_specs=(VMEM_SPEC, VMEM_SPEC),
        compiler_params=PARAMS,
        name="finish",
    )(pieces)
    return block_out[None], grad_mid[None], grad_up, grad_down


def solution(mesh):
    fine = Mesh(mesh.devices.reshape(4, 2, 2, 4, 2), (*SCENE_AXES, *BATCH_AXES))
    slab = P(BATCH_AXES, SCENE_AXES, None)
    shard = P(SCENE_AXES, BATCH_AXES)
    return jax.shard_map(
        on_device,
        mesh=fine,
        in_specs=(slab, P(None, BATCH_AXES, SCENE_AXES), slab, P(), P(), P(), P(), P(), P()),
        out_specs=(slab, slab, shard, shard),
        check_vma=False,
    )
```

time: 485 us -> 138 us (0.28)
  waiting for transfers between devices: 215 us -> 15.8 us
  matrix products: 114 us -> 0 us
  local copies, waits for them, and re-layouts: 84.2 us -> 6.68 us
  blocking collectives: 17.1 us -> 56.9 us
  Pallas kernels: 0 us -> 37.5 us
  other arithmetic: 21.7 us -> 2 us
  between operations: 14.3 us -> 0.72 us
    reduce_scatter x2 -> x0, waiting for transfers between devices: 124 us -> none  [the longest x1 69 us: on_device(): lax.psum_scatter(grad_down, 'scene', scatter_dimension=0, tiled=True)]
    dot_general x10 -> x0, matrix products: 114 us -> none  [the longest x1 53.3 us: attend_groups(): jnp.einsum('ksghd,ltghd->ghsktl', query, keys, precision=lax.Precision.HI...]
    unnamed x6 -> x0, waiting for transfers between devices: 67.8 us -> none
    all_to_all x1 -> x2, blocking collectives: 17.1 us -> 56.9 us  [the longest x1 39.6 us: on_device(): lax.all_to_all(keep + got, CHIP_AXES, split_axis=0, concat_axis=0, tiled=...]
    pallas_call x0 -> x4, Pallas kernels: none -> 37.5 us  [the longest x1 20 us: on_device(): pl.pallas_call(branch_kernel, grid=(2,), out_shape=(shape(TOK, D), shape(...]
    gather x1 -> x0, local copies, waits for them, and re-layouts: 26.4 us -> none  [on_device(): neighbours = jnp.take(extended, row_index, axis=0)]
    reshape x6 -> x2, local copies, waits for them, and re-layouts: 24.9 us -> 1.75 us  [on_device(): score_bias.reshape(3, 8, 16, 2, 16, 2).transpose(3, 2, 0, 5, 1, 4)]
    all_to_all x1, waiting for transfers between devices: 22.6 us -> 10.3 us  [exchange(): lax.all_to_all(values.reshape(SCENE, 3 * UNITS, 128), SCENE_AXES, split_a...]
  transfers between devices with their start and end apart: 7 -> 4, of which waited for: 5 -> 3; matrix products, arithmetic and copies ran while one was open for 8% -> 2% of each run, Pallas kernels for 0% -> 0%
where the time goes in v1:
time: 138 us; the launch traced here: 137 us
  blocking collectives  56.9 us (41%)
  Pallas kernels  37.5 us (27%)
  starting transfers between devices  17.4 us (13%)
  waiting for transfers between devices  15.8 us (11%)
  local copies, waits for them, and re-layouts  6.68 us (5%)
  other arithmetic  2 us (1%)
    all_to_all x1, blocking collectives, on_device(): lax.all_to_all(keep + got, CHIP_AXES, split_axis=0, concat_axis=0, tiled=...  39.6 us
    pallas_call x1, Pallas kernels, on_device(): pl.pallas_call(branch_kernel, grid=(2,), out_shape=(shape(TOK, D), shape(...  20 us
    all_to_all x1, blocking collectives, exchange(): lax.all_to_all(values.reshape(SCENE, 3 * UNITS, 128), SCENE_AXES, split_a...  17.3 us
    all_to_all x1, starting transfers between devices, exchange(): lax.all_to_all(values.reshape(SCENE, 3 * UNITS, 128), SCENE_AXES, split_a...  13 us
    all_to_all x1, waiting for transfers between devices, exchange(): lax.all_to_all(values.reshape(SCENE, 3 * UNITS, 128), SCENE_AXES, split_a...  10.3 us
    pallas_call x1, Pallas kernels, on_device(): pl.pallas_call(attention_kernel, out_shape=shape(3 * TOK, 128), in_specs=...  8.42 us
    pallas_call x1, Pallas kernels, on_device(): pl.pallas_call(conv_kernel, out_shape=shape(3 * TOK, 128), in_specs=[VMEM...  6.54 us
    ppermute x1, waiting for transfers between devices, on_device(): got = lax.ppermute(send, 'c', [(0, 1), (1, 0)])  4.63 us
  transfers between devices with their start and end apart: 4, of which 3 were waited for; matrix products, arithmetic and copies ran while one was open for 2% of the time, Pallas kernels for 0%

profile of v1, /device:TPU:0, one launch (start us, length us, event | category | flops | bytes accessed | tf_op | source)
XLA Modules:
  0.0 137.1 jit_solution(762274023947308585)
XLA Ops:
  0.6 0.0 copy-start.1
  0.6 1.0 slice_bitcast_fusion
  1.6 1.3 collective-permute-start.1
  2.9 3.0 %collective-permute-start = (f32[64,384]{1,0:T(8,128)S(1)}, f32[64,384]{1,0:T(8,128)S(1)}, u32[]{:S(2)}, u32[]{:S(2)}) collective-permute-start(f32[64,384]{1,0:T(8,128)S(1)} %get-tuple-element.25), channel_id=1, source_target_pairs={{0,8},{8,16},{16,24},{24,32},{32,40},{40,48},{48,56},{56,64},{64,7... | collective-permute-start | bytes 294920 | tf_op jit(solution)/shard_map/ppermute | solution.py:332
  6.0 0.0 collective-permute-done.1.high_ref
  6.0 0.0 copy-start.2
  6.0 0.9 collective-permute-done.low_ref
  6.9 0.0 copy-start.3
  6.9 0.0 copy-done.2
  6.9 0.6 copy-done.3
  7.6 6.5 %conv.1.first_ref = f32[1152,128]{1,0:T(8,128)} custom-call(f32[384,384]{1,0:T(8,128)} %bitcast.22, f32[64,384]{1,0:T(8,128)} %copy-done.3, f32[64,384]{1,0:T(8,128)} %copy-done.2, s32[27,1,384]{2,1,0:T(1,128)} %nbr_ref.1, f32[27,384]{1,0:T(8,128)} %weight_ref.1), custom_call_target="tpu_custom_call" | custom-call | tf_op jit(solution)/shard_map/conv/pallas_call | solution.py:336
  14.1 13.0 %all-to-all-start = ((f32[16,72,128]{2,1,0:T(8,128)}), f32[16,72,128]{2,1,0:T(8,128)S(1)}, u32[]{:S(2)}, u32[]{:S(2)}) async-start(f32[16,72,128]{2,1,0:T(8,128)} %bitcast.18), calls=%async_computation | async-start | bytes 1179648 | tf_op jit(solution)/shard_map/all_to_all | solution.py:346
  27.1 0.0 copy-done.1
  27.1 0.3 copy.15
  27.4 0.8 reshape.30
  28.2 0.7 copy.16
  28.9 0.9 reshape.31.bias_ref
  29.8 10.3 %all-to-all-done = f32[16,72,128]{2,1,0:T(8,128)S(1)} async-done(((f32[16,72,128]{2,1,0:T(8,128)}), f32[16,72,128]{2,1,0:T(8,128)S(1)}, u32[]{:S(2)}, u32[]{:S(2)}) %all-to-all-start) | async-done | bytes 589856 | tf_op jit(solution)/shard_map/all_to_all | solution.py:346
  40.1 0.0 copy-start
  40.1 0.8 copy-done
  40.9 8.4 %attention.1 = f32[1152,128]{1,0:T(8,128)} custom-call(f32[1152,128]{1,0:T(8,128)} %bitcast.20, f32[384,1152]{1,0:T(8,128)} %qkv_ref.1, f32[384,384]{1,0:T(8,128)} %wout_ref.1, f32[32,768]{1,0:T(8,128)} %reshape.31.bias_ref), custom_call_target="tpu_custom_call" | custom-call | tf_op jit(solution)/shard_map/attention/pallas_call | solution.py:351
  49.4 17.3 %all_to_all.15 = f32[16,72,128]{2,1,0:T(8,128)} all-to-all(f32[16,72,128]{2,1,0:T(8,128)} %bitcast.21), channel_id=1, replica_groups=mesh['y'=4,'zh'=2,'c'=2,'x'=4,'zl'=2] {'y','zh','c'}, dimensions={0} | all-to-all | bytes 1179648 | tf_op jit(solution)/shard_map/all_to_all | solution.py:346
  66.6 20.0 %branch.1 = (f32[384,384]{1,0:T(8,128)}, f32[384,384]{1,0:T(8,128)}, f32[64,72,128]{2,1,0:T(8,128)}, f32[64,72,128]{2,1,0:T(8,128)}) custom-call(f32[1152,128]{1,0:T(8,128)} %conv.1.first_ref, f32[1152,128]{1,0:T(8,128)} %bitcast.19, f32[384,384]{1,0:T(8,128)} %bitcast.23, f32[384,1536]{1,0:T(8,128)} %up_ref.1, f32[1536,384]{1,0:T(8,128)} %down_ref.1), custom_call_target="tpu_custom_call" | custom-call | tf_op jit(solution)/shard_map/branch/pallas_call | solution.py:363
  86.6 0.1 collective-permute-start.2
  86.7 4.6 %collective-permute-done.2 = f32[64,72,128]{2,1,0:T(8,128)S(1)} collective-permute-done((f32[64,72,128]{2,1,0:T(8,128)}, f32[64,72,128]{2,1,0:T(8,128)S(1)}, u32[]{:S(2)}, u32[]{:S(2)}) %collective-permute-start.2) | collective-permute-done | bytes 2359328 | tf_op jit(solution)/shard_map/ppermute | solution.py:389
  91.3 2.0 %add.3 = f32[64,72,128]{2,1,0:T(8,128)S(1)} add(f32[64,72,128]{2,1,0:T(8,128)} %get-tuple-element.12, f32[64,72,128]{2,1,0:T(8,128)S(1)} %collective-permute-done.2) | non-fusion elementwise | flops 589824 | bytes 7077888 | tf_op jit(solution)/shard_map/add | solution.py:390
  93.4 39.6 %all_to_all.16.pieces_ref = f32[64,72,128]{2,1,0:T(8,128)} all-to-all(f32[64,72,128]{2,1,0:T(8,128)S(1)} %add.3), channel_id=1, replica_groups=mesh['y'=4,'zh'=2,'c'=2,'x'=4,'zl'=2] {'y','zh','x','zl'}, dimensions={0} | all-to-all | bytes 4718592 | tf_op jit(solution)/shard_map/all_to_all | solution.py:390
  133.0 2.6 %finish.1 = (f32[24,192]{1,0:T(8,128)}, f32[96,48]{1,0:T(8,128)}) custom-call(f32[64,72,128]{2,1,0:T(8,128)} %all_to_all.16.pieces_ref), custom_call_target="tpu_custom_call" | custom-call | tf_op jit(solution)/shard_map/finish/pallas_call | solution.py:391
  135.6 1.5 %copy.17 = f32[96,48]{0,1:T(8,128)} copy(f32[96,48]{1,0:T(8,128)} %get-tuple-element.23) | data formatting | bytes 36864
Async XLA Ops:
  0.6 26.5 %copy-start.1 = (f32[24,32,32]{2,1,0:T(8,128)S(1)}, f32[24,32,32]{2,1,0:T(8,128)}, u32[]{:S(2)}) copy-start(f32[24,32,32]{2,1,0:T(8,128)} %param.15) | copy-start | bytes 294916
  1.6 4.3 %collective-permute-start.1 = (f32[64,384]{1,0:T(8,128)S(1)}, f32[64,384]{1,0:T(8,128)S(1)}, u32[]{:S(2)}, u32[]{:S(2)}) collective-permute-start(f32[64,384]{1,0:T(8,128)S(1)} %get-tuple-element.24), channel_id=1, source_target_pairs={{8,0},{16,8},{24,16},{32,24},{40,32},{48,40},{56,48},{64,56},{72,6... | collective-permute-start | bytes 294920 | tf_op jit(solution)/shard_map/ppermute | solution.py:333
  2.9 4.0 %collective-permute-start = (f32[64,384]{1,0:T(8,128)S(1)}, f32[64,384]{1,0:T(8,128)S(1)}, u32[]{:S(2)}, u32[]{:S(2)}) collective-permute-start(f32[64,384]{1,0:T(8,128)S(1)} %get-tuple-element.25), channel_id=1, source_target_pairs={{0,8},{8,16},{16,24},{24,32},{32,40},{40,48},{48,56},{56,64},{64,7... | collective-permute-start | bytes 294920 | tf_op jit(solution)/shard_map/ppermute | solution.py:332
  6.0 0.9 copy-start.2
  6.9 0.6 copy-start.3
  14.1 26.0 %all-to-all-start = ((f32[16,72,128]{2,1,0:T(8,128)}), f32[16,72,128]{2,1,0:T(8,128)S(1)}, u32[]{:S(2)}, u32[]{:S(2)}) async-start(f32[16,72,128]{2,1,0:T(8,128)} %bitcast.18), calls=%async_computation | async-start | bytes 1179648 | tf_op jit(solution)/shard_map/all_to_all | solution.py:346
  40.1 0.8 copy-start
  86.6 4.7 %collective-permute-start.2 = (f32[64,72,128]{2,1,0:T(8,128)}, f32[64,72,128]{2,1,0:T(8,128)S(1)}, u32[]{:S(2)}, u32[]{:S(2)}) collective-permute-start(f32[64,72,128]{2,1,0:T(8,128)} %get-tuple-element.13), channel_id=1, source_target_pairs={{0,8},{8,0},{1,9},{9,1},{2,10},{10,2},{3,11},{11,3},{4,12},{12,4},... | collective-permute-start | bytes 7077896 | tf_op jit(solution)/shard_map/ppermute | solution.py:389

commit v2 on v1

v2 whole, which is shorter than its diff:
```python
import functools

import jax
import jax.numpy as jnp
from jax import lax
from jax.experimental import pallas as pl
from jax.experimental.pallas import tpu as pltpu
from jax.sharding import Mesh
from jax.sharding import PartitionSpec as P

D = 384
FF = 1536
TAPS = 27
HALO = 64
TOK = 384
SCENE = 16
UNITS = 24
HALF = FF // 2
SCENE_AXES = ("y", "zh", "c")
BATCH_AXES = ("x", "zl")
YZ_AXES = ("y", "zh", "zl")
F32 = jnp.float32
BF16 = jnp.bfloat16
NN = (((1,), (0,)), ((), ()))
NT = (((1,), (1,)), ((), ()))
VMEM_SPEC = pl.BlockSpec(memory_space=pltpu.VMEM)
SUB = 256


def params(mebibytes):
    return pltpu.CompilerParams(vmem_limit_bytes=mebibytes * 1024 * 1024)


def cost(flops, moved):
    return pl.CostEstimate(flops=int(flops), bytes_accessed=int(moved), transcendentals=0)


def parts_of(values):
    high = values.astype(BF16)
    return high, (values - high.astype(F32)).astype(BF16)


def dot(a, b, dims=NN):
    return lax.dot_general(a, b, dims, preferred_element_type=F32)


def dot3(a, b, dims=NN):
    return dot(a[0], b[0], dims) + (dot(a[0], b[1], dims) + dot(a[1], b[0], dims))


def stack(values):
    return jnp.concatenate(parts_of(values), axis=0)


def dot_stacked(a, b, dims=NN):
    rows = a.shape[0] // 2
    both = dot(a, b[0], dims)
    return both[:rows] + (both[rows:] + dot(a[:rows], b[1], dims))


def normalise(values):
    average = jnp.mean(values, axis=-1, keepdims=True)
    centered = values - average
    variance = jnp.mean(centered * centered, axis=-1, keepdims=True)
    scale = lax.rsqrt(variance + 1e-05)
    return centered * scale, scale


def slots():
    return [2 * j + k for k in range(2) for j in range(12)]


def from_members(ref):
    rows = []
    for place in slots():
        tiles = [ref[pl.ds(UNITS * t + place, SCENE, stride=3 * UNITS), :] for t in range(3)]
        rows.append(jnp.concatenate(tiles, axis=1))
    return jnp.concatenate(rows, axis=0)


def to_members(ref, values):
    for unit, place in enumerate(slots()):
        for t in range(3):
            ref[pl.ds(UNITS * t + place, SCENE, stride=3 * UNITS), :] = values[
                SCENE * unit : SCENE * (unit + 1), 128 * t : 128 * (t + 1)
            ]


def convolve(tok, ext, offsets, weight_ref):
    middle_tap = TAPS // 2
    taps = [a for a in range(TAPS) if a != middle_tap]
    chunk = 13
    row = lax.broadcasted_iota(jnp.int32, (128, 32), 0)
    lanes = lax.broadcasted_iota(jnp.int32, (128, 256), 1)
    table = jnp.concatenate(parts_of(ext), axis=1)
    index = jnp.where(offsets > HALO, -1, offsets + row + HALO)
    acc = tok + tok * weight_ref[middle_tap : middle_tap + 1, :]
    for start in range(0, len(taps), chunk):
        hits = [
            jnp.where(index[:, a : a + 1] == lanes, 1.0, 0.0).astype(BF16)
            for a in taps[start : start + chunk]
        ]
        picked = dot(jnp.concatenate(hits, axis=0), table)
        for i, a in enumerate(taps[start : start + chunk]):
            piece = picked[128 * i : 128 * (i + 1)]
            acc = acc + (piece[:, :D] + piece[:, D:]) * weight_ref[a : a + 1, :]
    return acc


def offsets_of(nbr_ref, block):
    rows = nbr_ref[:, 0, 128 * block : 128 * (block + 1)]
    return jnp.concatenate([rows, jnp.zeros((5, 128), jnp.int32)], axis=0).T


def inner_kernel(tok_ref, nbr_ref, weight_ref, out_ref):
    out_ref[...] = convolve(
        tok_ref[128:256, :], tok_ref[64:320, :], offsets_of(nbr_ref, 1), weight_ref
    )


def edge_kernel(tok_ref, mate_ref, other_ref, nbr_ref, weight_ref, inner_ref, sent_ref):
    even = jnp.full((HALO, D), lax.axis_index("c"), jnp.int32) == 0
    low = jnp.where(even, other_ref[...], mate_ref[...])
    high = jnp.where(even, mate_ref[...], other_ref[...])
    head = convolve(
        tok_ref[:128, :],
        jnp.concatenate([low, tok_ref[:192, :]], axis=0),
        offsets_of(nbr_ref, 0),
        weight_ref,
    )
    tail = convolve(
        tok_ref[256:, :],
        jnp.concatenate([tok_ref[192:, :], high], axis=0),
        offsets_of(nbr_ref, 2),
        weight_ref,
    )
    to_members(sent_ref, jnp.concatenate([head, inner_ref[...], tail], axis=0))


def attention_kernel(got_ref, qkv_ref, wout_ref, bias_ref, sent_ref, rows_ref, scores_ref):
    for place in range(UNITS):
        group, half = place // 2, place % 2
        for t in range(3):
            rows_ref[pl.ds(TOK * t + 32 * group + half, SCENE, stride=2), :] = got_ref[
                pl.ds(UNITS * t + place, SCENE, stride=3 * UNITS), :
            ]
    normed, _ = normalise(
        jnp.concatenate([rows_ref[TOK * t : TOK * (t + 1), :] for t in range(3)], axis=1)
    )
    qkv = dot_stacked(stack(normed), parts_of(qkv_ref[...]))
    head_of = lax.broadcasted_iota(jnp.int32, (16, 128), 1) // 16
    row_head = (lax.broadcasted_iota(jnp.int32, (256, 128), 0) // 16) % 8
    ones = jnp.where(
        row_head == lax.broadcasted_iota(jnp.int32, (256, 128), 1) // 16, 1.0, 0.0
    ).astype(BF16)
    lane_all = lax.broadcasted_iota(jnp.int32, (TOK, 128), 1)

    def spread(values, group):
        pieces = []
        for half in range(2):
            piece = values[32 * group + 16 * half : 32 * group + 16 * half + 16]
            pieces += [jnp.where(head_of == h, piece, 0.0) for h in range(8)]
        return parts_of(jnp.concatenate(pieces, axis=0))

    attended = []
    for t in range(3):
        cols = slice(128 * t, 128 * (t + 1))
        query = qkv[:, :D][:, cols] * 0.25
        keys = qkv[:, D : 2 * D][:, cols]
        vals = qkv[:, 2 * D :][:, cols]
        bias = jnp.concatenate(
            [bias_ref[8 * t + h][:, 16 * half : 16 * half + 16] for half in range(2) for h in range(8)],
            axis=1,
        )
        for g in range(12):
            rows = slice(32 * g, 32 * g + 32)
            scores_ref[rows, :] = dot_stacked(stack(query[rows]), spread(keys, g), NT) + bias
        score = scores_ref[...]
        top = jnp.maximum(score[:, :128], score[:, 128:])
        for shift in (8, 4, 2, 1):
            other = jnp.where(
                lane_all % (2 * shift) < shift,
                pltpu.roll(top, 128 - shift, 1),
                pltpu.roll(top, shift, 1),
            )
            top = jnp.maximum(top, other)
        weight = jnp.exp(score - jnp.concatenate([top, top], axis=1))
        w_high, w_low = parts_of(weight)
        pieces = []
        for g in range(12):
            v_high, v_low = spread(vals, g)
            wide = jnp.concatenate([v_high, ones], axis=1)
            rows = slice(32 * g, 32 * g + 32)
            both = dot(jnp.concatenate([w_high[rows], w_low[rows]], axis=0), wide)
            total = both[:32] + both[32:]
            mixed = total[:, :128] + dot(w_high[rows], v_low)
            pieces.append(mixed / total[:, 128:])
        attended.append(jnp.concatenate(pieces, axis=0))
    attended = jnp.concatenate(attended, axis=1)
    mixed = dot_stacked(stack(attended), parts_of(wout_ref[...]))
    for t in range(3):
        rows_ref[TOK * t : TOK * (t + 1), :] = mixed[:, 128 * t : 128 * (t + 1)]
    for place in range(UNITS):
        group, half = place // 2, place % 2
        for t in range(3):
            sent_ref[pl.ds(UNITS * t + place, SCENE, stride=3 * UNITS), :] = rows_ref[
                pl.ds(TOK * t + 32 * group + half, SCENE, stride=2), :
            ]


def gauss(x):
    z = jnp.clip(x * 0.7071067811865476, -3.832506856900711, 3.832506856900711)
    s = z * z
    top = 0.00022905065861350646
    for c in (0.0034082910107109506, 0.050955695062380861, 0.18520832239976145, 1.128379143519084):
        top = top * s + c
    low = -1.1791602954361697e-7
    for c in (
        0.000023547966471313185,
        0.0010179625278914885,
        0.014070470171167667,
        0.11098505178285362,
        0.49746925110067538,
        1.0,
    ):
        low = low * s + c
    return 0.5 + 0.5 * (z * top / low), 0.3989422804014327 * jnp.exp(-0.5 * (x * x))


def gradient_kernel(
    first_ref, ret_ref, cot_ref, up_ref, down_ref,
    mid_ref, act_ref, dh_ref, keep_ref, send_ref,
    normed_ref, nt_ref, cot_pair_ref, ct_ref, grad_up_ref, grad_down_ref,
):
    step = pl.program_id(0)

    @pl.when(step == 0)
    def _():
        mid = from_members(first_ref) + from_members(ret_ref)
        mid_ref[...] = mid
        normed, _ = normalise(mid)
        cot = cot_ref[...]
        normed_ref[...] = stack(normed)
        nt_ref[...] = stack(normed.T)
        cot_pair_ref[...] = stack(cot)
        ct_ref[...] = stack(cot.T)

    def enter(i):
        cols = slice(SUB * i, SUB * (i + 1))
        hidden = dot_stacked(normed_ref[...], parts_of(up_ref[:, cols]))
        return hidden, dot_stacked(cot_pair_ref[...], parts_of(down_ref[cols, :]), NT)

    count = HALF // SUB
    ahead = enter(0)
    for i in range(count):
        hidden, d_active = ahead
        if i + 1 < count:
            ahead = enter(i + 1)
        chance, density = gauss(hidden)
        active = parts_of(hidden * chance)
        d_hidden = parts_of(d_active * (chance + hidden * density))
        here = slice(SUB * i, SUB * (i + 1))
        act_ref[:TOK, here], act_ref[TOK:, here] = active
        dh_ref[:TOK, here], dh_ref[TOK:, here] = d_hidden
        cols = pl.ds(pl.multiple_of(step * HALF + SUB * i, SUB), SUB)
        grad_down_ref[:, cols] = dot_stacked(ct_ref[...], active)
        grad_up_ref[:, cols] = dot_stacked(nt_ref[...], d_hidden)

    @pl.when(step == 1)
    def _():
        pack(grad_up_ref, grad_down_ref, keep_ref, send_ref)


def output_kernel(mid_ref, cot_ref, act_ref, dh_ref, up_ref, down_ref, out_ref, mid_grad_ref):
    step = pl.program_id(0)
    out_part = dot_stacked(act_ref[...], parts_of(down_ref[...]))
    norm_part = dot_stacked(dh_ref[...], parts_of(up_ref[...]), NT)

    @pl.when(step == 0)
    def _():
        out_ref[...] = mid_ref[...] + out_part
        mid_grad_ref[...] = norm_part

    @pl.when(step > 0)
    def _():
        out_ref[...] += out_part
        mid_grad_ref[...] += norm_part

    @pl.when(step == pl.num_programs(0) - 1)
    def _():
        normed, scale = normalise(mid_ref[...])
        d_normed = mid_grad_ref[...]
        shift = jnp.mean(d_normed, axis=-1, keepdims=True)
        slope = jnp.mean(d_normed * normed, axis=-1, keepdims=True)
        mid_grad_ref[...] = cot_ref[...] + scale * (d_normed - shift - normed * slope)


def pack(grad_up_ref, grad_down_ref, keep_ref, send_ref):
    core = lax.axis_index("c")
    lane = lax.broadcasted_iota(jnp.int32, (8, 128), 1)
    left = lane < 64
    segment = lane // 32
    first_core = jnp.full((72, 128), core, jnp.int32) == 0

    def piece(quarter, sigma, b):
        g, beta = b // 2, b % 2
        row = pl.multiple_of((4 * quarter + sigma) * 24, 8)

        def up_tile(i, t):
            return grad_up_ref[pl.ds(row + 8 * i, 8), 384 * g + 128 * t : 384 * g + 128 * (t + 1)]

        def down_tile(i, t):
            col = pl.multiple_of(384 * quarter + 128 * t, 128)
            return grad_down_ref[48 * b + 8 * i : 48 * b + 8 * (i + 1), pl.ds(col, 128)]

        full = [up_tile(i, 2 * beta) for i in range(3)]
        m0, m1, m2 = [up_tile(i, 1) for i in range(3)]
        own = left if beta == 0 else jnp.logical_not(left)
        if sigma == 0:
            c = [down_tile(i, 0) for i in range(6)]
        elif sigma == 1:
            c = [jnp.where(segment == 3, down_tile(i, 0), down_tile(i, 1)) for i in range(6)]
        elif sigma == 2:
            c = [jnp.where(segment == 0, down_tile(i, 2), down_tile(i, 1)) for i in range(6)]
        else:
            c = [down_tile(i, 2) for i in range(6)]
        free = 3 - sigma
        hole = segment == free
        start = 2 if beta == 0 else 0
        turn = 32 * ((start - (free + 2)) % 4)
        extra = pltpu.roll(c[4], turn, 1) if turn else c[4]
        rows = full + [
            jnp.where(own, m0, pltpu.roll(m1, 64, 1)),
            jnp.where(own, m2, extra),
            jnp.where(hole, pltpu.roll(c[5], 96, 1), c[0]),
            jnp.where(hole, pltpu.roll(c[5], 64, 1), c[1]),
            jnp.where(hole, pltpu.roll(c[5], 32, 1), c[2]),
            jnp.where(hole, pltpu.roll(c[4], 96, 1), c[3]),
        ]
        return jnp.concatenate(rows, axis=0)

    def quarter_body(quarter, carry):
        for pair in range(2):
            for b in range(8):
                even = piece(quarter, 2 * pair, b)
                odd = piece(quarter, 2 * pair + 1, b)
                where = (2 * quarter + pair) * 8 + (b % 2) * 4 + b // 2
                keep_ref[where] = jnp.where(first_core, even, odd)
                send_ref[where] = jnp.where(first_core, odd, even)
        return carry

    lax.fori_loop(0, 4, quarter_body, 0)


def add_kernel(a_ref, b_ref, out_ref):
    out_ref[...] = a_ref[...] + b_ref[...]


def sum_kernel(pieces_ref, total_ref):
    total = pieces_ref[0]
    for i in range(1, 16):
        total = total + pieces_ref[i]
    total_ref[...] = total


def finish_kernel(pieces_ref, up_ref, down_ref):
    scale = (TOK * 128) ** -0.5
    z = (pieces_ref[0] + pieces_ref[1]) + (pieces_ref[2] + pieces_ref[3])
    z = z * scale
    beta = lax.axis_index("zl")
    sigma = 2 * lax.axis_index("zh") + lax.axis_index("c")
    lane = lax.broadcasted_iota(jnp.int32, (8, 128), 1)
    lane24 = lax.broadcasted_iota(jnp.int32, (24, 128), 1)
    even24 = jnp.full((24, 128), beta, jnp.int32) == 0
    even = jnp.full((8, 128), beta, jnp.int32) == 0
    full, a, b = z[:24], z[24:32], z[32:40]
    turned = pltpu.roll(a, 64, 1)
    half = jnp.concatenate(
        [
            jnp.where(even, a, turned),
            jnp.where(even, turned, a),
            jnp.where(even, b, pltpu.roll(b, 64, 1)),
        ],
        axis=0,
    )
    swapped = pltpu.roll(full, 64, 1)
    up_ref[:, :128] = jnp.where(even24, full, jnp.where(lane24 < 64, half, swapped))
    up_ref[:, 128:] = jnp.where(even24, half, swapped)[:, :64]
    rest = z[40:]
    turned_rest = rest
    for k in range(1, 4):
        chosen = jnp.full((32, 128), sigma, jnp.int32) == k
        turned_rest = jnp.where(chosen, pltpu.roll(rest, 32 * k, 1), turned_rest)
    p0, p1, p2, p3 = [turned_rest[8 * i : 8 * (i + 1)] for i in range(4)]
    segment = lane // 32
    c5 = jnp.where(
        segment == 0,
        pltpu.roll(p0, 32, 1),
        jnp.where(segment == 1, pltpu.roll(p1, 64, 1), pltpu.roll(p2, 96, 1)),
    )
    tail = jnp.where(even, pltpu.roll(b, 96, 1), pltpu.roll(b, 32, 1))
    c4 = jnp.where(segment == 0, pltpu.roll(p3, 32, 1), tail)
    down_ref[...] = jnp.concatenate([p0, p1, p2, p3, c4, c5], axis=0)[:, :96]


def shape(*dims):
    return jax.ShapeDtypeStruct(dims, F32)


def on_device(tokens, nbr_offset, cotangent, conv_weight, w_qkv, w_out, score_bias, w_up, w_down):
    local = tokens[0]
    mates = [(i, i ^ 1) for i in range(SCENE)]
    others = [(i, i + 1) for i in range(1, SCENE - 1, 2)]
    others += [(target, source) for source, target in others]
    even = lax.axis_index("c") == 0
    head, tail = local[:HALO], local[TOK - HALO :]
    other = lax.ppermute(jnp.where(even, head, tail), SCENE_AXES, others)
    mate = lax.ppermute(jnp.where(even, tail, head), SCENE_AXES, mates)

    inner = pl.pallas_call(
        inner_kernel,
        out_shape=shape(128, D),
        in_specs=[VMEM_SPEC] * 3,
        out_specs=VMEM_SPEC,
        compiler_params=params(16),
        cost_estimate=cost(3e9, 1e6),
        name="inner",
    )(local, nbr_offset, conv_weight)
    sent = pl.pallas_call(
        edge_kernel,
        out_shape=shape(3 * TOK, 128),
        in_specs=[VMEM_SPEC] * 6,
        out_specs=VMEM_SPEC,
        compiler_params=params(24),
        cost_estimate=cost(6e9, 2e6),
        name="edges",
    )(local, mate, other, nbr_offset, conv_weight, inner)

    def exchange(values):
        swapped = lax.all_to_all(
            values.reshape(SCENE, 3 * UNITS, 128), SCENE_AXES, split_axis=0, concat_axis=0, tiled=True
        )
        return swapped.reshape(3 * TOK, 128)

    mixed = pl.pallas_call(
        attention_kernel,
        out_shape=shape(3 * TOK, 128),
        in_specs=[VMEM_SPEC] * 4,
        out_specs=VMEM_SPEC,
        scratch_shapes=[pltpu.VMEM((3 * TOK, 128), F32), pltpu.VMEM((TOK, 256), F32)],
        compiler_params=params(24),
        cost_estimate=cost(8e9, 4e6),
        name="attention",
    )(exchange(sent), w_qkv, w_out, score_bias)
    returned = exchange(mixed)

    whole = lambda *dims: pl.BlockSpec(dims, lambda n: (0,) * len(dims))
    pair = jax.ShapeDtypeStruct((2 * TOK, FF), BF16)
    middle, active, d_hidden, keep, send = pl.pallas_call(
        gradient_kernel,
        grid=(2,),
        out_shape=(shape(TOK, D), pair, pair, shape(64, 72, 128), shape(64, 72, 128)),
        in_specs=[
            whole(3 * TOK, 128),
            whole(3 * TOK, 128),
            whole(TOK, D),
            pl.BlockSpec((D, HALF), lambda n: (0, n)),
            pl.BlockSpec((HALF, D), lambda n: (n, 0)),
        ],
        out_specs=(
            whole(TOK, D),
            pl.BlockSpec((2 * TOK, HALF), lambda n: (0, n)),
            pl.BlockSpec((2 * TOK, HALF), lambda n: (0, n)),
            whole(64, 72, 128),
            whole(64, 72, 128),
        ),
        scratch_shapes=[
            pltpu.VMEM((2 * TOK, D), BF16),
            pltpu.VMEM((2 * D, TOK), BF16),
            pltpu.VMEM((2 * TOK, D), BF16),
            pltpu.VMEM((2 * D, TOK), BF16),
            pltpu.VMEM((D, FF), F32),
            pltpu.VMEM((D, FF), F32),
        ],
        compiler_params=params(44),
        cost_estimate=cost(16e9, 16e6),
        name="gradient",
    )(sent, returned, cotangent[0], w_up, w_down)
    got = lax.ppermute(send, "c", [(0, 1), (1, 0)])

    block = FF // 4
    block_out, grad_mid = pl.pallas_call(
        output_kernel,
        grid=(4,),
        out_shape=(shape(TOK, D), shape(TOK, D)),
        in_specs=[
            whole(TOK, D),
            whole(TOK, D),
            pl.BlockSpec((2 * TOK, block), lambda n: (0, n)),
            pl.BlockSpec((2 * TOK, block), lambda n: (0, n)),
            pl.BlockSpec((D, block), lambda n: (0, n)),
            pl.BlockSpec((block, D), lambda n: (n, 0)),
        ],
        out_specs=(whole(TOK, D), whole(TOK, D)),
        compiler_params=params(24),
        cost_estimate=cost(6e9, 11e6),
        name="outputs",
    )(middle, cotangent[0], active, d_hidden, w_up, w_down)

    keep, block_out, grad_mid = lax.optimization_barrier((keep, block_out, grad_mid))
    piece = pl.BlockSpec((8, 72, 128), lambda n: (n, 0, 0))
    chip = pl.pallas_call(
        add_kernel,
        grid=(8,),
        out_shape=pltpu.HBM((64, 72, 128), F32),
        in_specs=[piece, piece],
        out_specs=piece,
        compiler_params=params(16),
        name="add",
    )(keep, got)

    def swap(values, axes, count, rows):
        return lax.all_to_all(
            values.reshape(count, rows, 128), axes, split_axis=0, concat_axis=0, tiled=True
        )

    total = pl.pallas_call(
        sum_kernel,
        out_shape=shape(288, 128),
        in_specs=[VMEM_SPEC],
        out_specs=VMEM_SPEC,
        compiler_params=params(8),
        name="sum",
    )(swap(chip, YZ_AXES, 16, 288))
    grad_up, grad_down = pl.pallas_call(
        finish_kernel,
        out_shape=(shape(24, 192), shape(48, 96)),
        in_specs=[VMEM_SPEC],
        out_specs=(VMEM_SPEC, VMEM_SPEC),
        compiler_params=params(8),
        name="finish",
    )(swap(total, "x", 4, 72))
    grad_down = grad_down.T
    return block_out[None], grad_mid[None], grad_up, grad_down


def solution(mesh):
    fine = Mesh(mesh.devices.reshape(4, 2, 2, 4, 2), (*SCENE_AXES, *BATCH_AXES))
    slab = P(BATCH_AXES, SCENE_AXES, None)
    shard = P(SCENE_AXES, BATCH_AXES)
    return jax.shard_map(
        on_device,
        mesh=fine,
        in_specs=(slab, P(None, BATCH_AXES, SCENE_AXES), slab, P(), P(), P(), P(), P(), P()),
        out_specs=(slab, slab, shard, shard),
        check_vma=False,
    )
```

time: 138 us -> 127 us (0.920)
  blocking collectives: 56.9 us -> 80.1 us
  waiting for transfers between devices: 15.8 us -> 0.01 us
  starting transfers between devices: 17.4 us -> 6.21 us
  local copies, waits for them, and re-layouts: 6.68 us -> 2.68 us
  Pallas kernels: 37.5 us -> 35.6 us
    all_to_all x1 -> x2, blocking collectives: 17.3 us -> 34.5 us  [exchange(): lax.all_to_all(values.reshape(SCENE, 3 * UNITS, 128), SCENE_AXES, split_a...]
    all_to_all x1 -> x0, starting transfers between devices: 13 us -> none  [exchange(): lax.all_to_all(values.reshape(SCENE, 3 * UNITS, 128), SCENE_AXES, split_a...]
    all_to_all x1 -> x0, waiting for transfers between devices: 10.3 us -> none  [exchange(): lax.all_to_all(values.reshape(SCENE, 3 * UNITS, 128), SCENE_AXES, split_a...]
    all_to_all x1 -> x2, blocking collectives: 39.6 us -> 45.6 us  [swap(): lax.all_to_all(values.reshape(count, rows, 128), axes, split_axis=0, conc...]
    ppermute x1, waiting for transfers between devices: 4.63 us -> 0.01 us  [on_device(): got = lax.ppermute(send, 'c', [(0, 1), (1, 0)])]
    pallas_call x1, Pallas kernels: 8.42 us -> 5.71 us  [on_device(): pl.pallas_call(attention_kernel, out_shape=shape(3 * TOK, 128), in_specs=...]
    add x1 -> x0, other arithmetic: 2 us -> none  [on_device(): keep + got]
    ppermute x2, starting transfers between devices: 4.33 us -> 6.09 us  [the longest x1 5.42 us: on_device(): mate = lax.ppermute(jnp.where(even, tail, head), SCENE_AXES, mates)]
  transfers between devices with their start and end apart: 4 -> 3, of which waited for: 3 -> 0; matrix products, arithmetic and copies ran while one was open for 2% -> 0% of each run, Pallas kernels for 0% -> 7%
where the time goes in v2:
time: 127 us; the launch traced here: 126 us
  blocking collectives  80.1 us (63%)
  Pallas kernels  35.6 us (28%)
  starting transfers between devices  6.21 us (5%)
  local copies, waits for them, and re-layouts  2.68 us (2%)
    all_to_all x2, blocking collectives, swap(): lax.all_to_all(values.reshape(count, rows, 128), axes, split_axis=0, conc...  45.6 us
    all_to_all x2, blocking collectives, exchange(): lax.all_to_all(values.reshape(SCENE, 3 * UNITS, 128), SCENE_AXES, split_a...  34.5 us
    pallas_call x1, Pallas kernels, on_device(): pl.pallas_call(gradient_kernel, grid=(2,), out_shape=(shape(TOK, D), pair...  13.5 us
    pallas_call x1, Pallas kernels, on_device(): pl.pallas_call(output_kernel, grid=(4,), out_shape=(shape(TOK, D), shape(...  7.58 us
    pallas_call x1, Pallas kernels, on_device(): pl.pallas_call(attention_kernel, out_shape=shape(3 * TOK, 128), in_specs=...  5.71 us
    ppermute x1, starting transfers between devices, on_device(): mate = lax.ppermute(jnp.where(even, tail, head), SCENE_AXES, mates)  5.42 us
    pallas_call x1, Pallas kernels, on_device(): pl.pallas_call(edge_kernel, out_shape=shape(3 * TOK, 128), in_specs=[VMEM...  3.17 us
    pallas_call x1, Pallas kernels, on_device(): pl.pallas_call(add_kernel, grid=(8,), out_shape=pltpu.HBM((64, 72, 128),...  3.11 us
  transfers between devices with their start and end apart: 3, of which 0 were waited for; matrix products, arithmetic and copies ran while one was open for 0% of the time, Pallas kernels for 7%

profile of v2, /device:TPU:0, one launch (start us, length us, event | category | flops | bytes accessed | tf_op | source)
XLA Modules:
  0.0 126.3 jit_solution(3804244997431340657)
XLA Ops:
  0.6 1.0 select_bitcast_fusion
  1.6 0.7 collective-permute-start.1
  2.3 5.4 %collective-permute-start = (f32[64,384]{1,0:T(8,128)S(1)}, f32[64,384]{1,0:T(8,128)S(1)}, u32[]{:S(2)}, u32[]{:S(2)}) collective-permute-start(f32[64,384]{1,0:T(8,128)S(1)} %get-tuple-element.29), channel_id=1, source_target_pairs={{0,8},{8,0},{16,24},{24,16},{32,40},{40,32},{48,56},{56,48},{64,72... | collective-permute-start | bytes 294920 | tf_op jit(solution)/shard_map/ppermute | solution.py:418
  7.7 0.0 copy-start
  7.7 1.1 copy-done
  8.8 0.0 copy-start.8
  8.8 0.8 copy-done.8
  9.6 0.0 copy-start.10
  9.6 0.8 copy-done.10
  10.3 0.0 copy-start.1
  10.3 0.0 copy-start.9
  10.3 0.0 copy-start.11
  10.3 1.6 %inner.1.inner_ref = f32[128,384]{1,0:T(8,128)S(1)} custom-call(f32[384,384]{1,0:T(8,128)S(1)} %bitcast.20, s32[27,1,384]{2,1,0:T(1,128)S(1)} %copy-done.10, f32[27,384]{1,0:T(8,128)S(1)} %copy-done.8), custom_call_target="tpu_custom_call" | custom-call | flops 3000000000 | bytes 1000000 | tf_op jit(solution)/shard_map/inner/pallas_call | solution.py:420
  12.0 0.0 copy-start.4
  12.0 0.0 copy-start.5
  12.0 0.0 copy-start.7
  12.0 0.0 collective-permute-done.1.other_ref
  12.0 0.0 collective-permute-done.mate_ref
  12.1 0.0 copy-done.1
  12.1 0.0 copy-done.9
  12.1 0.0 copy-done.11
  12.1 3.2 %edges.1.first_ref = f32[1152,128]{1,0:T(8,128)S(1)} custom-call(f32[384,384]{1,0:T(8,128)S(1)} %bitcast.21, f32[64,384]{1,0:T(8,128)S(1)} %collective-permute-done.mate_ref, f32[64,384]{1,0:T(8,128)S(1)} %collective-permute-done.1.other_ref, s32[27,1,384]{2,1,0:T(1,128)S(1)} %copy-done.11, f32[27,384]{1,0:T(8,128)S(1)} %copy-done.9, ...), custom_call_target="tpu_custom_call" | custom-call | flops 6000000000 | bytes 2000000 | tf_op jit(solution)/shard_map/edges/pallas_call | solution.py:429
  15.3 18.9 %all_to_all.20 = f32[16,72,128]{2,1,0:T(8,128)S(1)} all-to-all(f32[16,72,128]{2,1,0:T(8,128)S(1)} %bitcast.16), channel_id=1, replica_groups=mesh['y'=4,'zh'=2,'c'=2,'x'=4,'zl'=2] {'y','zh','c'}, dimensions={0} | all-to-all | bytes 1179648 | tf_op jit(solution)/shard_map/all_to_all | solution.py:440
  34.2 0.0 copy-done.4
  34.2 0.0 copy-done.5
  34.2 0.0 copy-done.7
  34.2 0.0 copy-start.6
  34.2 5.7 %attention.1 = f32[1152,128]{1,0:T(8,128)S(1)} custom-call(f32[1152,128]{1,0:T(8,128)S(1)} %bitcast.19, f32[384,1152]{1,0:T(8,128)S(1)} %copy-done.4, f32[384,384]{1,0:T(8,128)S(1)} %copy-done.5, f32[24,32,32]{2,1,0:T(8,128)S(1)} %copy-done.7), custom_call_target="tpu_custom_call" | custom-call | flops 8000000000 | bytes 4000000 | tf_op jit(solution)/shard_map/attention/pallas_call | solution.py:445
  39.9 15.6 %all_to_all.21 = f32[16,72,128]{2,1,0:T(8,128)S(1)} all-to-all(f32[16,72,128]{2,1,0:T(8,128)S(1)} %bitcast.18), channel_id=1, replica_groups=mesh['y'=4,'zh'=2,'c'=2,'x'=4,'zl'=2] {'y','zh','c'}, dimensions={0} | all-to-all | bytes 1179648 | tf_op jit(solution)/shard_map/all_to_all | solution.py:440
  55.5 0.0 copy-done.6
  55.5 0.0 copy-start.2
  55.5 0.0 copy-start.3
  55.5 13.5 %gradient.1 = (f32[384,384]{1,0:T(8,128)S(1)}, bf16[768,1536]{1,0:T(8,128)(2,1)S(1)}, bf16[768,1536]{1,0:T(8,128)(2,1)S(1)}, f32[64,72,128]{2,1,0:T(8,128)S(1)}, f32[64,72,128]{2,1,0:T(8,128)}) custom-call(f32[1152,128]{1,0:T(8,128)S(1)} %edges.1.first_ref, f32[1152,128]{1,0:T(8,128)S(1)} %bitcast.17, f32[384,384]{1,0:T(8,128)S(1)} %bitcast.22, ...), custom_call_target="tpu_custom_call" | custom-call | flops 16000000000 | bytes 16000000 | tf_op jit(solution)/shard_map/gradient/pallas_call | solution.py:459
  69.0 0.1 collective-permute-start.2
  69.1 0.0 copy-done.2
  69.1 0.0 copy-done.3
  69.1 7.6 %outputs.1 = (f32[384,384]{1,0:T(8,128)}, f32[384,384]{1,0:T(8,128)}) custom-call(f32[384,384]{1,0:T(8,128)S(1)} %get-tuple-element.17.mid_ref, f32[384,384]{1,0:T(8,128)S(1)} %bitcast.23, bf16[768,1536]{1,0:T(8,128)(2,1)S(1)} %get-tuple-element.18.act_ref, bf16[768,1536]{1,0:T(8,128)(2,1)S(1)} %get-tuple-element.19.dh_ref, f32[384,1536]{1,0:T(8,128)S(1)} %copy-done.2, ...), custom_call_target="tpu_custom_call" | custom-call | flops 6000000000 | bytes 11000000 | tf_op jit(solution)/shard_map/outputs/pallas_call | solution.py:492
  76.7 0.0 collective-permute-done.2.b_ref
  76.7 3.1 %add.1 = f32[64,72,128]{2,1,0:T(8,128)} custom-call(f32[64,72,128]{2,1,0:T(8,128)S(1)} %get-tuple-element.24.a_ref, f32[64,72,128]{2,1,0:T(8,128)S(1)} %collective-permute-done.2.b_ref), custom_call_target="tpu_custom_call" | custom-call | tf_op jit(solution)/shard_map/add/pallas_call | solution.py:512
  79.8 35.5 %all_to_all.22.pieces_ref = f32[16,288,128]{2,1,0:T(8,128)S(1)} all-to-all(f32[16,288,128]{2,1,0:T(8,128)} %bitcast.24), channel_id=1, replica_groups=mesh['y'=4,'zh'=2,'c'=2,'x'=4,'zl'=2] {'y','zh','zl'}, dimensions={0} | all-to-all | bytes 4718592 | tf_op jit(solution)/shard_map/all_to_all | solution.py:523
  115.3 0.1 sum.1
  115.4 10.2 %all_to_all.23.pieces_ref = f32[4,72,128]{2,1,0:T(8,128)S(1)} all-to-all(f32[4,72,128]{2,1,0:T(8,128)S(1)} %bitcast.15), channel_id=1, replica_groups=mesh['y'=4,'zh'=2,'c'=2,'x'=4,'zl'=2] {'x'}, dimensions={0} | all-to-all | bytes 294912 | tf_op jit(solution)/shard_map/all_to_all | solution.py:523
  125.6 0.8 finish.1
Async XLA Ops:
  1.6 10.4 %collective-permute-start.1 = (f32[64,384]{1,0:T(8,128)S(1)}, f32[64,384]{1,0:T(8,128)S(1)}, u32[]{:S(2)}, u32[]{:S(2)}) collective-permute-start(f32[64,384]{1,0:T(8,128)S(1)} %get-tuple-element.28), channel_id=1, source_target_pairs={{8,16},{24,32},{40,48},{56,64},{72,80},{88,96},{104,112},{16,8},{3... | collective-permute-start | bytes 294920 | tf_op jit(solution)/shard_map/ppermute | solution.py:417
  2.3 9.8 %collective-permute-start = (f32[64,384]{1,0:T(8,128)S(1)}, f32[64,384]{1,0:T(8,128)S(1)}, u32[]{:S(2)}, u32[]{:S(2)}) collective-permute-start(f32[64,384]{1,0:T(8,128)S(1)} %get-tuple-element.29), channel_id=1, source_target_pairs={{0,8},{8,0},{16,24},{24,16},{32,40},{40,32},{48,56},{56,48},{64,72... | collective-permute-start | bytes 294920 | tf_op jit(solution)/shard_map/ppermute | solution.py:418
  7.7 1.1 copy-start
  8.8 0.8 copy-start.8
  9.6 0.8 copy-start.10
  10.3 1.7 %copy-start.1 = (f32[1,384,384]{2,1,0:T(8,128)S(1)}, f32[1,384,384]{2,1,0:T(8,128)}, u32[]{:S(2)}) copy-start(f32[1,384,384]{2,1,0:T(8,128)} %param.9) | copy-start | bytes 1769476
  10.3 1.7 %copy-start.9 = (f32[27,384]{1,0:T(8,128)S(1)}, f32[27,384]{1,0:T(8,128)}, u32[]{:S(2)}) copy-start(f32[27,384]{1,0:T(8,128)} %weight_ref.3) | copy-start | bytes 124420
  10.3 1.7 %copy-start.11 = (s32[27,1,384]{2,1,0:T(1,128)S(1)}, s32[27,1,384]{2,1,0:T(1,128)}, u32[]{:S(2)}) copy-start(s32[27,1,384]{2,1,0:T(1,128)} %nbr_ref.3) | copy-start | bytes 124420
  12.0 22.2 %copy-start.4 = (f32[384,1152]{1,0:T(8,128)S(1)}, f32[384,1152]{1,0:T(8,128)}, u32[]{:S(2)}) copy-start(f32[384,1152]{1,0:T(8,128)} %qkv_ref.1) | copy-start | bytes 5308420
  12.0 22.1 %copy-start.5 = (f32[384,384]{1,0:T(8,128)S(1)}, f32[384,384]{1,0:T(8,128)}, u32[]{:S(2)}) copy-start(f32[384,384]{1,0:T(8,128)} %wout_ref.1) | copy-start | bytes 1769476
  12.0 22.1 %copy-start.7 = (f32[24,32,32]{2,1,0:T(8,128)S(1)}, f32[24,32,32]{2,1,0:T(8,128)}, u32[]{:S(2)}) copy-start(f32[24,32,32]{2,1,0:T(8,128)} %bias_ref.1) | copy-start | bytes 294916
  34.2 21.4 %copy-start.6 = (f32[1,384,384]{2,1,0:T(8,128)S(1)}, f32[1,384,384]{2,1,0:T(8,128)}, u32[]{:S(2)}) copy-start(f32[1,384,384]{2,1,0:T(8,128)} %param.11) | copy-start | bytes 1769476
  55.5 13.6 %copy-start.2 = (f32[384,1536]{1,0:T(8,128)S(1)}, f32[384,1536]{1,0:T(8,128)}, u32[]{:S(2)}) copy-start(f32[384,1536]{1,0:T(8,128)} %up_ref.3) | copy-start | bytes 7077892
  55.5 13.6 %copy-start.3 = (f32[1536,384]{1,0:T(8,128)S(1)}, f32[1536,384]{1,0:T(8,128)}, u32[]{:S(2)}) copy-start(f32[1536,384]{1,0:T(8,128)} %down_ref.3) | copy-start | bytes 7077892
  69.0 7.7 %collective-permute-start.2 = (f32[64,72,128]{2,1,0:T(8,128)}, f32[64,72,128]{2,1,0:T(8,128)S(1)}, u32[]{:S(2)}, u32[]{:S(2)}) collective-permute-start(f32[64,72,128]{2,1,0:T(8,128)} %get-tuple-element.25), channel_id=1, source_target_pairs={{0,8},{8,0},{1,9},{9,1},{2,10},{10,2},{3,11},{11,3},{4,12},{12,4},... | collective-permute-start | bytes 7077896 | tf_op jit(solution)/shard_map/ppermute | solution.py:489

commit v3 on v2

--- a/solution.py
+++ b/solution.py
@@ -18,7 +18,7 @@
 HALF = FF // 2
 SCENE_AXES = ("y", "zh", "c")
 BATCH_AXES = ("x", "zl")
-YZ_AXES = ("y", "zh", "zl")
+CHIP_AXES = ("y", "zh", "x", "zl")
 F32 = jnp.float32
 BF16 = jnp.bfloat16
 NN = (((1,), (0,)), ((), ()))
@@ -112,9 +112,18 @@
     return jnp.concatenate([rows, jnp.zeros((5, 128), jnp.int32)], axis=0).T
 
 
-def inner_kernel(tok_ref, nbr_ref, weight_ref, out_ref):
+def inner_kernel(tok_hbm, nbr_hbm, weight_hbm, out_ref, tok_ref, nbr_ref, weight_ref, done):
+    copies = [
+        pltpu.make_async_copy(tok_hbm.at[pl.ds(HALO, 2 * 128), :], tok_ref, done.at[0]),
+        pltpu.make_async_copy(nbr_hbm, nbr_ref, done.at[1]),
+        pltpu.make_async_copy(weight_hbm, weight_ref, done.at[2]),
+    ]
+    for copy in copies:
+        copy.start()
+    for copy in copies:
+        copy.wait()
     out_ref[...] = convolve(
-        tok_ref[128:256, :], tok_ref[64:320, :], offsets_of(nbr_ref, 1), weight_ref
+        tok_ref[HALO : HALO + 128, :], tok_ref[...], offsets_of(nbr_ref, 1), weight_ref
     )
 
 
@@ -300,10 +309,8 @@
     lane = lax.broadcasted_iota(jnp.int32, (8, 128), 1)
     left = lane < 64
     segment = lane // 32
-    first_core = jnp.full((72, 128), core, jnp.int32) == 0
-
-    def piece(quarter, sigma, b):
-        g, beta = b // 2, b % 2
+
+    def piece(quarter, sigma, g, beta):
         row = pl.multiple_of((4 * quarter + sigma) * 24, 8)
 
         def up_tile(i, t):
@@ -311,7 +318,8 @@
 
         def down_tile(i, t):
             col = pl.multiple_of(384 * quarter + 128 * t, 128)
-            return grad_down_ref[48 * b + 8 * i : 48 * b + 8 * (i + 1), pl.ds(col, 128)]
+            start = 96 * g + 48 * beta + 8 * i
+            return grad_down_ref[start : start + 8, pl.ds(col, 128)]
 
         full = [up_tile(i, 2 * beta) for i in range(3)]
         m0, m1, m2 = [up_tile(i, 1) for i in range(3)]
@@ -329,7 +337,7 @@
         start = 2 if beta == 0 else 0
         turn = 32 * ((start - (free + 2)) % 4)
         extra = pltpu.roll(c[4], turn, 1) if turn else c[4]
-        rows = full + [
+        return full + [
             jnp.where(own, m0, pltpu.roll(m1, 64, 1)),
             jnp.where(own, m2, extra),
             jnp.where(hole, pltpu.roll(c[5], 96, 1), c[0]),
@@ -337,35 +345,38 @@
             jnp.where(hole, pltpu.roll(c[5], 32, 1), c[2]),
             jnp.where(hole, pltpu.roll(c[4], 96, 1), c[3]),
         ]
-        return jnp.concatenate(rows, axis=0)
-
-    def quarter_body(quarter, carry):
-        for pair in range(2):
-            for b in range(8):
-                even = piece(quarter, 2 * pair, b)
-                odd = piece(quarter, 2 * pair + 1, b)
-                where = (2 * quarter + pair) * 8 + (b % 2) * 4 + b // 2
-                keep_ref[where] = jnp.where(first_core, even, odd)
-                send_ref[where] = jnp.where(first_core, odd, even)
-        return carry
-
-    lax.fori_loop(0, 4, quarter_body, 0)
-
-
-def add_kernel(a_ref, b_ref, out_ref):
-    out_ref[...] = a_ref[...] + b_ref[...]
-
-
-def sum_kernel(pieces_ref, total_ref):
-    total = pieces_ref[0]
-    for i in range(1, 16):
-        total = total + pieces_ref[i]
-    total_ref[...] = total
+
+    def lay(even_ref, odd_ref):
+        def body(quarter, carry):
+            for g in range(4):
+                for sigma in range(4):
+                    for beta in range(2):
+                        ref = odd_ref if sigma % 2 else even_ref
+                        where = (2 * quarter + sigma // 2) * 8 + 2 * g + beta
+                        for i, rows in enumerate(piece(quarter, sigma, g, beta)):
+                            ref[where, 8 * i : 8 * (i + 1), :] = rows
+            return carry
+
+        lax.fori_loop(0, 4, body, 0)
+
+    @pl.when(core == 0)
+    def _():
+        lay(keep_ref, send_ref)
+
+    @pl.when(core == 1)
+    def _():
+        lay(send_ref, keep_ref)
 
 
 def finish_kernel(pieces_ref, up_ref, down_ref):
     scale = (TOK * 128) ** -0.5
-    z = (pieces_ref[0] + pieces_ref[1]) + (pieces_ref[2] + pieces_ref[3])
+    sums = []
+    for k in range(4):
+        total = pieces_ref[16 * k]
+        for i in range(1, 16):
+            total = total + pieces_ref[16 * k + i]
+        sums.append(total)
+    z = (sums[0] + sums[1]) + (sums[2] + sums[3])
     z = z * scale
     beta = lax.axis_index("zl")
     sigma = 2 * lax.axis_index("zh") + lax.axis_index("c")
@@ -420,12 +431,18 @@
     inner = pl.pallas_call(
         inner_kernel,
         out_shape=shape(128, D),
-        in_specs=[VMEM_SPEC] * 3,
+        in_specs=[pl.BlockSpec(memory_space=pltpu.HBM)] * 3,
         out_specs=VMEM_SPEC,
+        scratch_shapes=[
+            pltpu.VMEM((2 * 128, D), F32),
+            pltpu.VMEM((TAPS, 1, TOK), jnp.int32),
+            pltpu.VMEM((TAPS, D), F32),
+            pltpu.SemaphoreType.DMA((3,)),
+        ],
         compiler_params=params(16),
         cost_estimate=cost(3e9, 1e6),
         name="inner",
-    )(local, nbr_offset, conv_weight)
+    )(*(pltpu.with_memory_space_constraint(a, pltpu.HBM) for a in (local, nbr_offset, conv_weight)))
     sent = pl.pallas_call(
         edge_kernel,
         out_shape=shape(3 * TOK, 128),
@@ -455,7 +472,7 @@
     returned = exchange(mixed)
 
     whole = lambda *dims: pl.BlockSpec(dims, lambda n: (0,) * len(dims))
-    pair = jax.ShapeDtypeStruct((2 * TOK, FF), BF16)
+    pair = pltpu.HBM((2 * TOK, FF), BF16)
     middle, active, d_hidden, keep, send = pl.pallas_call(
         gradient_kernel,
         grid=(2,),
@@ -507,31 +524,7 @@
         name="outputs",
     )(middle, cotangent[0], active, d_hidden, w_up, w_down)
 
-    keep, block_out, grad_mid = lax.optimization_barrier((keep, block_out, grad_mid))
-    piece = pl.BlockSpec((8, 72, 128), lambda n: (n, 0, 0))
-    chip = pl.pallas_call(
-        add_kernel,
-        grid=(8,),
-        out_shape=pltpu.HBM((64, 72, 128), F32),
-        in_specs=[piece, piece],
-        out_specs=piece,
-        compiler_params=params(16),
-        name="add",
-    )(keep, got)
-
-    def swap(values, axes, count, rows):
-        return lax.all_to_all(
-            values.reshape(count, rows, 128), axes, split_axis=0, concat_axis=0, tiled=True
-        )
-
-    total = pl.pallas_call(
-        sum_kernel,
-        out_shape=shape(288, 128),
-        in_specs=[VMEM_SPEC],
-        out_specs=VMEM_SPEC,
-        compiler_params=params(8),
-        name="sum",
-    )(swap(chip, YZ_AXES, 16, 288))
+    pieces = lax.all_to_all(keep + got, CHIP_AXES, split_axis=0, concat_axis=0, tiled=True)
     grad_up, grad_down = pl.pallas_call(
         finish_kernel,
         out_shape=(shape(24, 192), shape(48, 96)),
@@ -539,7 +532,7 @@
         out_specs=(VMEM_SPEC, VMEM_SPEC),
         compiler_params=params(8),
         name="finish",
-    )(swap(total, "x", 4, 72))
+    )(pieces)
     grad_down = grad_down.T
     return block_out[None], grad_mid[None], grad_up, grad_down
 

time: 127 us -> 116 us (0.913)
  blocking collectives: 80.1 us -> 36.1 us
  waiting for transfers between devices: 0.01 us -> 23.4 us
  starting transfers between devices: 6.21 us -> 12.6 us
  local copies, waits for them, and re-layouts: 2.68 us -> 6.7 us
  Pallas kernels: 35.6 us -> 32.8 us
  other arithmetic: 0.96 us -> 2.65 us
    all_to_all x2 -> x0, blocking collectives: 45.6 us -> none  [swap(): lax.all_to_all(values.reshape(count, rows, 128), axes, split_axis=0, conc...]
    all_to_all x0 -> x1, waiting for transfers between devices: none -> 19 us  [on_device(): lax.all_to_all(keep + got, CHIP_AXES, split_axis=0, concat_axis=0, tiled=...]
    all_to_all x0 -> x1, starting transfers between devices: none -> 6.44 us  [on_device(): lax.all_to_all(keep + got, CHIP_AXES, split_axis=0, concat_axis=0, tiled=...]
    ppermute x1, waiting for transfers between devices: 0.01 us -> 4.42 us  [on_device(): got = lax.ppermute(send, 'c', [(0, 1), (1, 0)])]
    unnamed x24, local copies, waits for them, and re-layouts: 2.68 us -> 6.7 us
    pallas_call x3 -> x1, Pallas kernels: 4.87 us -> 2.75 us  [on_device(): pl.pallas_call(inner_kernel, out_shape=shape(128, D), in_specs=[pl.BlockS...]
    add x0 -> x1, other arithmetic: none -> 1.69 us  [on_device(): keep + got]
    all_to_all x2, blocking collectives: 34.5 us -> 36.1 us  [exchange(): lax.all_to_all(values.reshape(SCENE, 3 * UNITS, 128), SCENE_AXES, split_a...]
  transfers between devices with their start and end apart: 3 -> 4, of which waited for: 0 -> 2; matrix products, arithmetic and copies ran while one was open for 0% -> 0% of each run, Pallas kernels for 7% -> 9%
where the time goes in v3:
time: 116 us; the launch traced here: 115 us
  blocking collectives  36.1 us (31%)
  Pallas kernels  32.8 us (28%)
  waiting for transfers between devices  23.4 us (20%)
  starting transfers between devices  12.6 us (11%)
  local copies, waits for them, and re-layouts  6.7 us (6%)
  other arithmetic  2.65 us (2%)
    all_to_all x2, blocking collectives, exchange(): lax.all_to_all(values.reshape(SCENE, 3 * UNITS, 128), SCENE_AXES, split_a...  36.1 us
    all_to_all x1, waiting for transfers between devices, on_device(): lax.all_to_all(keep + got, CHIP_AXES, split_axis=0, concat_axis=0, tiled=...  19 us
    pallas_call x1, Pallas kernels, on_device(): pl.pallas_call(gradient_kernel, grid=(2,), out_shape=(shape(TOK, D), pair...  12.8 us
    pallas_call x1, Pallas kernels, on_device(): pl.pallas_call(output_kernel, grid=(4,), out_shape=(shape(TOK, D), shape(...  7.58 us
    unnamed x24, local copies, waits for them, and re-layouts  6.7 us
    all_to_all x1, starting transfers between devices, on_device(): lax.all_to_all(keep + got, CHIP_AXES, split_axis=0, concat_axis=0, tiled=...  6.44 us
    pallas_call x1, Pallas kernels, on_device(): pl.pallas_call(attention_kernel, out_shape=shape(3 * TOK, 128), in_specs=...  5.71 us
    ppermute x1, starting transfers between devices, on_device(): mate = lax.ppermute(jnp.where(even, tail, head), SCENE_AXES, mates)  5.42 us
  transfers between devices with their start and end apart: 4, of which 2 were waited for; matrix products, arithmetic and copies ran while one was open for 0% of the time, Pallas kernels for 9%

profile of v3, /device:TPU:0, one launch (start us, length us, event | category | flops | bytes accessed | tf_op | source)
XLA Modules:
  0.0 115.1 jit_solution(9394042073481999769)
XLA Ops:
  0.6 1.0 select_bitcast_fusion
  1.6 0.7 collective-permute-start.1
  2.3 5.4 %collective-permute-start = (f32[64,384]{1,0:T(8,128)S(1)}, f32[64,384]{1,0:T(8,128)S(1)}, u32[]{:S(2)}, u32[]{:S(2)}) collective-permute-start(f32[64,384]{1,0:T(8,128)S(1)} %get-tuple-element.23), channel_id=1, source_target_pairs={{0,8},{8,0},{16,24},{24,16},{32,40},{40,32},{48,56},{56,48},{64,72... | collective-permute-start | bytes 294920 | tf_op jit(solution)/shard_map/ppermute | solution.py:429
  7.7 0.0 copy-start
  7.7 0.0 copy-start.8
  7.7 0.0 copy-start.9
  7.7 2.7 %inner.1.inner_ref = f32[128,384]{1,0:T(8,128)S(1)} custom-call(f32[384,384]{1,0:T(8,128)} %bitcast.17, s32[27,1,384]{2,1,0:T(1,128)} %nbr_ref.1, f32[27,384]{1,0:T(8,128)} %weight_ref.1), custom_call_target="tpu_custom_call" | custom-call | flops 3000000000 | bytes 1000000 | tf_op jit(solution)/shard_map/inner/pallas_call | solution.py:431
  10.5 0.0 copy-start.4
  10.5 0.0 copy-start.5
  10.5 0.0 copy-start.7
  10.5 0.0 collective-permute-done.1.other_ref
  10.5 0.0 collective-permute-done.mate_ref
  10.5 0.0 copy-done
  10.5 0.0 copy-done.8
  10.5 0.0 copy-done.9
  10.5 3.2 %edges.1.first_ref = f32[1152,128]{1,0:T(8,128)S(1)} custom-call(f32[384,384]{1,0:T(8,128)S(1)} %bitcast.18, f32[64,384]{1,0:T(8,128)S(1)} %collective-permute-done.mate_ref, f32[64,384]{1,0:T(8,128)S(1)} %collective-permute-done.1.other_ref, s32[27,1,384]{2,1,0:T(1,128)S(1)} %copy-done.9, f32[27,384]{1,0:T(8,128)S(1)} %copy-done.8, ...), custom_call_target="tpu_custom_call" | custom-call | flops 6000000000 | bytes 2000000 | tf_op jit(solution)/shard_map/edges/pallas_call | solution.py:446
  13.7 20.4 %all_to_all.15 = f32[16,72,128]{2,1,0:T(8,128)S(1)} all-to-all(f32[16,72,128]{2,1,0:T(8,128)S(1)} %bitcast.13), channel_id=1, replica_groups=mesh['y'=4,'zh'=2,'c'=2,'x'=4,'zl'=2] {'y','zh','c'}, dimensions={0} | all-to-all | bytes 1179648 | tf_op jit(solution)/shard_map/all_to_all | solution.py:457
  34.1 0.0 copy-done.4
  34.1 0.0 copy-done.5
  34.1 0.0 copy-done.7
  34.1 0.0 copy-start.1
  34.2 0.0 copy-start.6
  34.2 5.7 %attention.1 = f32[1152,128]{1,0:T(8,128)S(1)} custom-call(f32[1152,128]{1,0:T(8,128)S(1)} %bitcast.16, f32[384,1152]{1,0:T(8,128)S(1)} %copy-done.4, f32[384,384]{1,0:T(8,128)S(1)} %copy-done.5, f32[24,32,32]{2,1,0:T(8,128)S(1)} %copy-done.7), custom_call_target="tpu_custom_call" | custom-call | flops 8000000000 | bytes 4000000 | tf_op jit(solution)/shard_map/attention/pallas_call | solution.py:462
  39.9 15.6 %all_to_all.16 = f32[16,72,128]{2,1,0:T(8,128)S(1)} all-to-all(f32[16,72,128]{2,1,0:T(8,128)S(1)} %bitcast.15), channel_id=1, replica_groups=mesh['y'=4,'zh'=2,'c'=2,'x'=4,'zl'=2] {'y','zh','c'}, dimensions={0} | all-to-all | bytes 1179648 | tf_op jit(solution)/shard_map/all_to_all | solution.py:457
  55.5 0.0 copy-done.1
  55.5 0.0 copy-done.6
  55.5 12.8 %gradient.1 = (f32[384,384]{1,0:T(8,128)S(1)}, bf16[768,1536]{1,0:T(8,128)(2,1)}, bf16[768,1536]{1,0:T(8,128)(2,1)}, f32[64,72,128]{2,1,0:T(8,128)S(1)}, f32[64,72,128]{2,1,0:T(8,128)S(1)}) custom-call(f32[1152,128]{1,0:T(8,128)S(1)} %edges.1.first_ref, f32[1152,128]{1,0:T(8,128)S(1)} %bitcast.14, f32[384,384]{1,0:T(8,128)S(1)} %bitcast.19, ...), custom_call_target="tpu_custom_call" | custom-call | flops 16000000000 | bytes 16000000 | tf_op jit(solution)/shard_map/gradient/pallas_call | solution.py:476
  68.4 0.1 collective-permute-start.2
  68.5 4.4 %collective-permute-done.2 = f32[64,72,128]{2,1,0:T(8,128)S(1)} collective-permute-done((f32[64,72,128]{2,1,0:T(8,128)S(1)}, f32[64,72,128]{2,1,0:T(8,128)S(1)}, u32[]{:S(2)}, u32[]{:S(2)}) %collective-permute-start.2) | collective-permute-done | bytes 2359328 | tf_op jit(solution)/shard_map/ppermute | solution.py:506
  72.9 1.7 %add.3 = f32[64,72,128]{2,1,0:T(8,128)} add(f32[64,72,128]{2,1,0:T(8,128)S(1)} %get-tuple-element.18, f32[64,72,128]{2,1,0:T(8,128)S(1)} %collective-permute-done.2) | non-fusion elementwise | flops 589824 | bytes 7077888 | tf_op jit(solution)/shard_map/add | solution.py:527
  74.6 6.4 %all-to-all-start.2 = ((f32[64,72,128]{2,1,0:T(8,128)}), f32[64,72,128]{2,1,0:T(8,128)S(1)}, u32[]{:S(2)}, u32[]{:S(2)}) async-start(f32[64,72,128]{2,1,0:T(8,128)} %add.3), calls=%async_computation.2 | async-start | bytes 4718592 | tf_op jit(solution)/shard_map/all_to_all | solution.py:527
  81.0 0.0 copy-start.2
  81.0 1.7 %copy-done.2 = f32[384,1536]{1,0:T(8,128)S(1)} copy-done((f32[384,1536]{1,0:T(8,128)S(1)}, f32[384,1536]{1,0:T(8,128)}, u32[]{:S(2)}) %copy-start.2) | copy-done | bytes 2359320
  82.7 0.0 copy-start.3
  82.7 1.7 %copy-done.3 = f32[1536,384]{1,0:T(8,128)S(1)} copy-done((f32[1536,384]{1,0:T(8,128)S(1)}, f32[1536,384]{1,0:T(8,128)}, u32[]{:S(2)}) %copy-start.3) | copy-done | bytes 2359320
  84.4 0.0 copy-start.10
  84.4 1.7 %copy-done.10 = bf16[768,1536]{1,0:T(8,128)(2,1)S(1)} copy-done((bf16[768,1536]{1,0:T(8,128)(2,1)S(1)}, bf16[768,1536]{1,0:T(8,128)(2,1)}, u32[]{:S(2)}) %copy-start.10) | copy-done | bytes 2359320
  86.0 0.0 copy-start.11
  86.0 1.7 %copy-done.11 = bf16[768,1536]{1,0:T(8,128)(2,1)S(1)} copy-done((bf16[768,1536]{1,0:T(8,128)(2,1)S(1)}, bf16[768,1536]{1,0:T(8,128)(2,1)}, u32[]{:S(2)}) %copy-start.11) | copy-done | bytes 2359320
  87.7 7.6 %outputs.1 = (f32[384,384]{1,0:T(8,128)}, f32[384,384]{1,0:T(8,128)}) custom-call(f32[384,384]{1,0:T(8,128)S(1)} %get-tuple-element.13.mid_ref, f32[384,384]{1,0:T(8,128)S(1)} %bitcast.20, bf16[768,1536]{1,0:T(8,128)(2,1)S(1)} %copy-done.10, bf16[768,1536]{1,0:T(8,128)(2,1)S(1)} %copy-done.11, f32[384,1536]{1,0:T(8,128)S(1)} %copy-done.2, ...), custom_call_target="tpu_custom_call" | custom-call | flops 6000000000 | bytes 11000000 | tf_op jit(solution)/shard_map/outputs/pallas_call | solution.py:509
  95.3 19.0 %all-to-all-done.2.pieces_ref = f32[64,72,128]{2,1,0:T(8,128)S(1)} async-done(((f32[64,72,128]{2,1,0:T(8,128)}), f32[64,72,128]{2,1,0:T(8,128)S(1)}, u32[]{:S(2)}, u32[]{:S(2)}) %all-to-all-start.2) | async-done | bytes 2359328 | tf_op jit(solution)/shard_map/all_to_all | solution.py:527
  114.3 0.8 finish.1
Async XLA Ops:
  1.6 8.9 %collective-permute-start.1 = (f32[64,384]{1,0:T(8,128)S(1)}, f32[64,384]{1,0:T(8,128)S(1)}, u32[]{:S(2)}, u32[]{:S(2)}) collective-permute-start(f32[64,384]{1,0:T(8,128)S(1)} %get-tuple-element.22), channel_id=1, source_target_pairs={{8,16},{24,32},{40,48},{56,64},{72,80},{88,96},{104,112},{16,8},{3... | collective-permute-start | bytes 294920 | tf_op jit(solution)/shard_map/ppermute | solution.py:428
  2.3 8.2 %collective-permute-start = (f32[64,384]{1,0:T(8,128)S(1)}, f32[64,384]{1,0:T(8,128)S(1)}, u32[]{:S(2)}, u32[]{:S(2)}) collective-permute-start(f32[64,384]{1,0:T(8,128)S(1)} %get-tuple-element.23), channel_id=1, source_target_pairs={{0,8},{8,0},{16,24},{24,16},{32,40},{40,32},{48,56},{56,48},{64,72... | collective-permute-start | bytes 294920 | tf_op jit(solution)/shard_map/ppermute | solution.py:429
  7.7 2.8 %copy-start = (f32[1,384,384]{2,1,0:T(8,128)S(1)}, f32[1,384,384]{2,1,0:T(8,128)}, u32[]{:S(2)}) copy-start(f32[1,384,384]{2,1,0:T(8,128)} %param.9) | copy-start | bytes 1769476
  7.7 2.8 %copy-start.8 = (f32[27,384]{1,0:T(8,128)S(1)}, f32[27,384]{1,0:T(8,128)}, u32[]{:S(2)}) copy-start(f32[27,384]{1,0:T(8,128)} %weight_ref.1) | copy-start | bytes 124420
  7.7 2.8 %copy-start.9 = (s32[27,1,384]{2,1,0:T(1,128)S(1)}, s32[27,1,384]{2,1,0:T(1,128)}, u32[]{:S(2)}) copy-start(s32[27,1,384]{2,1,0:T(1,128)} %nbr_ref.1) | copy-start | bytes 124420
  10.5 23.7 %copy-start.4 = (f32[384,1152]{1,0:T(8,128)S(1)}, f32[384,1152]{1,0:T(8,128)}, u32[]{:S(2)}) copy-start(f32[384,1152]{1,0:T(8,128)} %qkv_ref.1) | copy-start | bytes 5308420
  10.5 23.7 %copy-start.5 = (f32[384,384]{1,0:T(8,128)S(1)}, f32[384,384]{1,0:T(8,128)}, u32[]{:S(2)}) copy-start(f32[384,384]{1,0:T(8,128)} %wout_ref.1) | copy-start | bytes 1769476
  10.5 23.7 %copy-start.7 = (f32[24,32,32]{2,1,0:T(8,128)S(1)}, f32[24,32,32]{2,1,0:T(8,128)}, u32[]{:S(2)}) copy-start(f32[24,32,32]{2,1,0:T(8,128)} %bias_ref.1) | copy-start | bytes 294916
  34.1 21.4 %copy-start.1 = (f32[384,1536]{1,0:T(8,128)S(1)}, f32[384,1536]{1,0:T(8,128)}, u32[]{:S(2)}) copy-start(f32[384,1536]{1,0:T(8,128)} %up_ref.3) | copy-start | bytes 7077892
  34.2 21.4 %copy-start.6 = (f32[1,384,384]{2,1,0:T(8,128)S(1)}, f32[1,384,384]{2,1,0:T(8,128)}, u32[]{:S(2)}) copy-start(f32[1,384,384]{2,1,0:T(8,128)} %param.11) | copy-start | bytes 1769476
  68.4 4.5 %collective-permute-start.2 = (f32[64,72,128]{2,1,0:T(8,128)S(1)}, f32[64,72,128]{2,1,0:T(8,128)S(1)}, u32[]{:S(2)}, u32[]{:S(2)}) collective-permute-start(f32[64,72,128]{2,1,0:T(8,128)S(1)} %get-tuple-element.19), channel_id=1, source_target_pairs={{0,8},{8,0},{1,9},{9,1},{2,10},{10,2},{3,11},{11,3},{4,12},{12,4},... | collective-permute-start | bytes 7077896 | tf_op jit(solution)/shard_map/ppermute | solution.py:506
  74.6 39.7 %all-to-all-start.2 = ((f32[64,72,128]{2,1,0:T(8,128)}), f32[64,72,128]{2,1,0:T(8,128)S(1)}, u32[]{:S(2)}, u32[]{:S(2)}) async-start(f32[64,72,128]{2,1,0:T(8,128)} %add.3), calls=%async_computation.2 | async-start | bytes 4718592 | tf_op jit(solution)/shard_map/all_to_all | solution.py:527
  81.0 1.7 %copy-start.2 = (f32[384,1536]{1,0:T(8,128)S(1)}, f32[384,1536]{1,0:T(8,128)}, u32[]{:S(2)}) copy-start(f32[384,1536]{1,0:T(8,128)} %up_ref.3) | copy-start | bytes 7077892
  82.7 1.7 %copy-start.3 = (f32[1536,384]{1,0:T(8,128)S(1)}, f32[1536,384]{1,0:T(8,128)}, u32[]{:S(2)}) copy-start(f32[1536,384]{1,0:T(8,128)} %down_ref.3) | copy-start | bytes 7077892
  84.4 1.7 %copy-start.10 = (bf16[768,1536]{1,0:T(8,128)(2,1)S(1)}, bf16[768,1536]{1,0:T(8,128)(2,1)}, u32[]{:S(2)}) copy-start(bf16[768,1536]{1,0:T(8,128)(2,1)} %get-tuple-element.14.act_ref) | copy-start | bytes 7077892
  86.0 1.7 %copy-start.11 = (bf16[768,1536]{1,0:T(8,128)(2,1)S(1)}, bf16[768,1536]{1,0:T(8,128)(2,1)}, u32[]{:S(2)}) copy-start(bf16[768,1536]{1,0:T(8,128)(2,1)} %get-tuple-element.15.dh_ref) | copy-start | bytes 7077892

commit v4 on v3

--- a/solution.py
+++ b/solution.py
@@ -15,7 +15,6 @@
 TOK = 384
 SCENE = 16
 UNITS = 24
-HALF = FF // 2
 SCENE_AXES = ("y", "zh", "c")
 BATCH_AXES = ("x", "zl")
 CHIP_AXES = ("y", "zh", "x", "zl")
@@ -90,8 +89,9 @@
     middle_tap = TAPS // 2
     taps = [a for a in range(TAPS) if a != middle_tap]
     chunk = 13
-    row = lax.broadcasted_iota(jnp.int32, (128, 32), 0)
-    lanes = lax.broadcasted_iota(jnp.int32, (128, 256), 1)
+    count = tok.shape[0]
+    row = lax.broadcasted_iota(jnp.int32, (count, 32), 0)
+    lanes = lax.broadcasted_iota(jnp.int32, (count, ext.shape[0]), 1)
     table = jnp.concatenate(parts_of(ext), axis=1)
     index = jnp.where(offsets > HALO, -1, offsets + row + HALO)
     acc = tok + tok * weight_ref[middle_tap : middle_tap + 1, :]
@@ -102,19 +102,18 @@
         ]
         picked = dot(jnp.concatenate(hits, axis=0), table)
         for i, a in enumerate(taps[start : start + chunk]):
-            piece = picked[128 * i : 128 * (i + 1)]
+            piece = picked[count * i : count * (i + 1)]
             acc = acc + (piece[:, :D] + piece[:, D:]) * weight_ref[a : a + 1, :]
     return acc
 
 
-def offsets_of(nbr_ref, block):
-    rows = nbr_ref[:, 0, 128 * block : 128 * (block + 1)]
-    return jnp.concatenate([rows, jnp.zeros((5, 128), jnp.int32)], axis=0).T
+def offsets_of(nbr_ref):
+    return jnp.concatenate([nbr_ref[:, 0, :], jnp.zeros((5, TOK), jnp.int32)], axis=0).T
 
 
 def inner_kernel(tok_hbm, nbr_hbm, weight_hbm, out_ref, tok_ref, nbr_ref, weight_ref, done):
     copies = [
-        pltpu.make_async_copy(tok_hbm.at[pl.ds(HALO, 2 * 128), :], tok_ref, done.at[0]),
+        pltpu.make_async_copy(tok_hbm, tok_ref, done.at[0]),
         pltpu.make_async_copy(nbr_hbm, nbr_ref, done.at[1]),
         pltpu.make_async_copy(weight_hbm, weight_ref, done.at[2]),
     ]
@@ -122,25 +121,32 @@
         copy.start()
     for copy in copies:
         copy.wait()
-    out_ref[...] = convolve(
-        tok_ref[HALO : HALO + 128, :], tok_ref[...], offsets_of(nbr_ref, 1), weight_ref
-    )
+    offsets = offsets_of(nbr_ref)
+    for start in (HALO, HALO + 128):
+        out_ref[start - HALO : start - HALO + 128, :] = convolve(
+            tok_ref[start : start + 128, :],
+            tok_ref[start - HALO : start + 128 + HALO, :],
+            offsets[start : start + 128],
+            weight_ref,
+        )
 
 
 def edge_kernel(tok_ref, mate_ref, other_ref, nbr_ref, weight_ref, inner_ref, sent_ref):
     even = jnp.full((HALO, D), lax.axis_index("c"), jnp.int32) == 0
     low = jnp.where(even, other_ref[...], mate_ref[...])
     high = jnp.where(even, mate_ref[...], other_ref[...])
+    offsets = offsets_of(nbr_ref)
+    blank = jnp.zeros((HALO, D), F32)
     head = convolve(
-        tok_ref[:128, :],
-        jnp.concatenate([low, tok_ref[:192, :]], axis=0),
-        offsets_of(nbr_ref, 0),
+        tok_ref[:HALO, :],
+        jnp.concatenate([low, tok_ref[: 2 * HALO, :], blank], axis=0),
+        offsets[:HALO],
         weight_ref,
     )
     tail = convolve(
-        tok_ref[256:, :],
-        jnp.concatenate([tok_ref[192:, :], high], axis=0),
-        offsets_of(nbr_ref, 2),
+        tok_ref[TOK - HALO :, :],
+        jnp.concatenate([tok_ref[TOK - 2 * HALO :, :], high, blank], axis=0),
+        offsets[TOK - HALO :],
         weight_ref,
     )
     to_members(sent_ref, jnp.concatenate([head, inner_ref[...], tail], axis=0))
@@ -236,54 +242,73 @@
     return 0.5 + 0.5 * (z * top / low), 0.3989422804014327 * jnp.exp(-0.5 * (x * x))
 
 
+def prepare_kernel(cot_ref, up_ref, down_ref, d_active_ref, up_high_ref, up_low_ref, ct_ref):
+    @pl.when(pl.program_id(0) == 0)
+    def _():
+        ct_ref[...] = stack(cot_ref[...].T)
+
+    d_active_ref[...] = dot_stacked(stack(cot_ref[...]), parts_of(down_ref[...]), NT)
+    up_high_ref[...], up_low_ref[...] = parts_of(up_ref[...])
+
+
 def gradient_kernel(
-    first_ref, ret_ref, cot_ref, up_ref, down_ref,
-    mid_ref, act_ref, dh_ref, keep_ref, send_ref,
-    normed_ref, nt_ref, cot_pair_ref, ct_ref, grad_up_ref, grad_down_ref,
+    first_ref, ret_ref, d_active_hbm, up_high_hbm, up_low_hbm, ct_hbm,
+    mid_hbm, act_hbm, dh_hbm, keep_ref, send_ref,
+    d_active_ref, up_high_ref, up_low_ref, ct_ref, mid_ref, act_ref, dh_ref,
+    normed_ref, nt_ref, grad_up_ref, grad_down_ref, came, left,
 ):
-    step = pl.program_id(0)
-
-    @pl.when(step == 0)
-    def _():
-        mid = from_members(first_ref) + from_members(ret_ref)
-        mid_ref[...] = mid
-        normed, _ = normalise(mid)
-        cot = cot_ref[...]
-        normed_ref[...] = stack(normed)
-        nt_ref[...] = stack(normed.T)
-        cot_pair_ref[...] = stack(cot)
-        ct_ref[...] = stack(cot.T)
+    pairs = (
+        (up_high_hbm, up_high_ref),
+        (up_low_hbm, up_low_ref),
+        (d_active_hbm, d_active_ref),
+        (ct_hbm, ct_ref),
+    )
+    loads = [pltpu.make_async_copy(src, dst, came.at[i]) for i, (src, dst) in enumerate(pairs)]
+    for load in loads:
+        load.start()
+    mid = from_members(first_ref) + from_members(ret_ref)
+    mid_ref[...] = mid
+    stores = [pltpu.make_async_copy(mid_ref, mid_hbm, left.at[0])]
+    stores[0].start()
+    normed, _ = normalise(mid)
+    normed_ref[...] = stack(normed)
+    nt_ref[...] = stack(normed.T)
 
     def enter(i):
         cols = slice(SUB * i, SUB * (i + 1))
-        hidden = dot_stacked(normed_ref[...], parts_of(up_ref[:, cols]))
-        return hidden, dot_stacked(cot_pair_ref[...], parts_of(down_ref[cols, :]), NT)
-
-    count = HALF // SUB
+        return dot_stacked(normed_ref[...], (up_high_ref[:, cols], up_low_ref[:, cols]))
+
+    loads[0].wait()
+    loads[1].wait()
+    count = FF // SUB
     ahead = enter(0)
+    loads[2].wait()
+    loads[3].wait()
     for i in range(count):
-        hidden, d_active = ahead
+        hidden = ahead
         if i + 1 < count:
             ahead = enter(i + 1)
+        here = slice(SUB * i, SUB * (i + 1))
         chance, density = gauss(hidden)
         active = parts_of(hidden * chance)
-        d_hidden = parts_of(d_active * (chance + hidden * density))
-        here = slice(SUB * i, SUB * (i + 1))
-        act_ref[:TOK, here], act_ref[TOK:, here] = active
-        dh_ref[:TOK, here], dh_ref[TOK:, here] = d_hidden
-        cols = pl.ds(pl.multiple_of(step * HALF + SUB * i, SUB), SUB)
-        grad_down_ref[:, cols] = dot_stacked(ct_ref[...], active)
-        grad_up_ref[:, cols] = dot_stacked(nt_ref[...], d_hidden)
-
-    @pl.when(step == 1)
-    def _():
-        pack(grad_up_ref, grad_down_ref, keep_ref, send_ref)
+        d_hidden = parts_of(d_active_ref[:, here] * (chance + hidden * density))
+        act_ref[i, :TOK, :], act_ref[i, TOK:, :] = active
+        dh_ref[i, :TOK, :], dh_ref[i, TOK:, :] = d_hidden
+        grad_down_ref[:, here] = dot_stacked(ct_ref[...], active)
+        grad_up_ref[:, here] = dot_stacked(nt_ref[...], d_hidden)
+    stores.append(pltpu.make_async_copy(act_ref, act_hbm, left.at[1]))
+    stores.append(pltpu.make_async_copy(dh_ref, dh_hbm, left.at[2]))
+    stores[1].start()
+    stores[2].start()
+    pack(grad_up_ref, grad_down_ref, keep_ref, send_ref)
+    for store in stores:
+        store.wait()
 
 
 def output_kernel(mid_ref, cot_ref, act_ref, dh_ref, up_ref, down_ref, out_ref, mid_grad_ref):
     step = pl.program_id(0)
-    out_part = dot_stacked(act_ref[...], parts_of(down_ref[...]))
-    norm_part = dot_stacked(dh_ref[...], parts_of(up_ref[...]), NT)
+    out_part = dot_stacked(act_ref[0], parts_of(down_ref[...]))
+    norm_part = dot_stacked(dh_ref[0], parts_of(up_ref[...]), NT)
 
     @pl.when(step == 0)
     def _():
@@ -430,11 +455,11 @@
 
     inner = pl.pallas_call(
         inner_kernel,
-        out_shape=shape(128, D),
+        out_shape=shape(256, D),
         in_specs=[pl.BlockSpec(memory_space=pltpu.HBM)] * 3,
         out_specs=VMEM_SPEC,
         scratch_shapes=[
-            pltpu.VMEM((2 * 128, D), F32),
+            pltpu.VMEM((TOK, D), F32),
             pltpu.VMEM((TAPS, 1, TOK), jnp.int32),
             pltpu.VMEM((TAPS, D), F32),
             pltpu.SemaphoreType.DMA((3,)),
@@ -453,6 +478,32 @@
         name="edges",
     )(local, mate, other, nbr_offset, conv_weight, inner)
 
+    whole = lambda *dims: pl.BlockSpec(dims, lambda n: (0,) * len(dims))
+    d_active, up_high, up_low, cot_turned = pl.pallas_call(
+        prepare_kernel,
+        grid=(4,),
+        out_shape=(
+            pltpu.HBM((TOK, FF), F32),
+            pltpu.HBM((D, FF), BF16),
+            pltpu.HBM((D, FF), BF16),
+            pltpu.HBM((2 * D, TOK), BF16),
+        ),
+        in_specs=[
+            whole(TOK, D),
+            pl.BlockSpec((D, FF // 4), lambda n: (0, n)),
+            pl.BlockSpec((FF // 4, D), lambda n: (n, 0)),
+        ],
+        out_specs=(
+            pl.BlockSpec((TOK, FF // 4), lambda n: (0, n)),
+            pl.BlockSpec((D, FF // 4), lambda n: (0, n)),
+            pl.BlockSpec((D, FF // 4), lambda n: (0, n)),
+            whole(2 * D, TOK),
+        ),
+        compiler_params=params(20),
+        cost_estimate=cost(4e9, 12e6),
+        name="prepare",
+    )(cotangent[0], w_up, w_down)
+
     def exchange(values):
         swapped = lax.all_to_all(
             values.reshape(SCENE, 3 * UNITS, 128), SCENE_AXES, split_axis=0, concat_axis=0, tiled=True
@@ -471,50 +522,51 @@
     )(exchange(sent), w_qkv, w_out, score_bias)
     returned = exchange(mixed)
 
-    whole = lambda *dims: pl.BlockSpec(dims, lambda n: (0,) * len(dims))
-    pair = pltpu.HBM((2 * TOK, FF), BF16)
+    pair = pltpu.HBM((FF // SUB, 2 * TOK, SUB), BF16)
+    hbm = pl.BlockSpec(memory_space=pltpu.HBM)
     middle, active, d_hidden, keep, send = pl.pallas_call(
         gradient_kernel,
-        grid=(2,),
-        out_shape=(shape(TOK, D), pair, pair, shape(64, 72, 128), shape(64, 72, 128)),
-        in_specs=[
-            whole(3 * TOK, 128),
-            whole(3 * TOK, 128),
-            whole(TOK, D),
-            pl.BlockSpec((D, HALF), lambda n: (0, n)),
-            pl.BlockSpec((HALF, D), lambda n: (n, 0)),
-        ],
-        out_specs=(
-            whole(TOK, D),
-            pl.BlockSpec((2 * TOK, HALF), lambda n: (0, n)),
-            pl.BlockSpec((2 * TOK, HALF), lambda n: (0, n)),
-            whole(64, 72, 128),
-            whole(64, 72, 128),
-        ),
+        out_shape=(pltpu.HBM((TOK, D), F32), pair, pair, shape(64, 72, 128), shape(64, 72, 128)),
+        in_specs=[VMEM_SPEC] * 2 + [hbm] * 4,
+        out_specs=(hbm, hbm, hbm, VMEM_SPEC, VMEM_SPEC),
         scratch_shapes=[
-            pltpu.VMEM((2 * TOK, D), BF16),
+            pltpu.VMEM((TOK, FF), F32),
+            pltpu.VMEM((D, FF), BF16),
+            pltpu.VMEM((D, FF), BF16),
             pltpu.VMEM((2 * D, TOK), BF16),
+            pltpu.VMEM((TOK, D), F32),
+            pltpu.VMEM((FF // SUB, 2 * TOK, SUB), BF16),
+            pltpu.VMEM((FF // SUB, 2 * TOK, SUB), BF16),
             pltpu.VMEM((2 * TOK, D), BF16),
             pltpu.VMEM((2 * D, TOK), BF16),
             pltpu.VMEM((D, FF), F32),
             pltpu.VMEM((D, FF), F32),
+            pltpu.SemaphoreType.DMA((4,)),
+            pltpu.SemaphoreType.DMA((3,)),
         ],
         compiler_params=params(44),
-        cost_estimate=cost(16e9, 16e6),
+        cost_estimate=cost(12e9, 16e6),
         name="gradient",
-    )(sent, returned, cotangent[0], w_up, w_down)
+    )(
+        sent,
+        returned,
+        *(
+            pltpu.with_memory_space_constraint(a, pltpu.HBM)
+            for a in (d_active, up_high, up_low, cot_turned)
+        ),
+    )
     got = lax.ppermute(send, "c", [(0, 1), (1, 0)])
 
-    block = FF // 4
+    block = SUB
     block_out, grad_mid = pl.pallas_call(
         output_kernel,
-        grid=(4,),
+        grid=(FF // SUB,),
         out_shape=(shape(TOK, D), shape(TOK, D)),
         in_specs=[
             whole(TOK, D),
             whole(TOK, D),
-            pl.BlockSpec((2 * TOK, block), lambda n: (0, n)),
-            pl.BlockSpec((2 * TOK, block), lambda n: (0, n)),
+            pl.BlockSpec((1, 2 * TOK, block), lambda n: (n, 0, 0)),
+            pl.BlockSpec((1, 2 * TOK, block), lambda n: (n, 0, 0)),
             pl.BlockSpec((D, block), lambda n: (0, n)),
             pl.BlockSpec((block, D), lambda n: (n, 0)),
         ],

time: 116 us -> 114 us (0.983)
  blocking collectives: 36.1 us -> 19 us
  waiting for transfers between devices: 23.4 us -> 29.1 us
  Pallas kernels: 32.8 us -> 36.6 us
  starting transfers between devices: 12.6 us -> 16.2 us
  local copies, waits for them, and re-layouts: 6.7 us -> 9.42 us
    all_to_all x2 -> x1, blocking collectives: 36.1 us -> 19 us  [exchange(): lax.all_to_all(values.reshape(SCENE, 3 * UNITS, 128), SCENE_AXES, split_a...]
    all_to_all x0 -> x1, waiting for transfers between devices: none -> 4.95 us  [exchange(): lax.all_to_all(values.reshape(SCENE, 3 * UNITS, 128), SCENE_AXES, split_a...]
    pallas_call x3 -> x4, Pallas kernels: 23.2 us -> 27.5 us  [the longest x1 11.2 us: on_device(): pl.pallas_call(gradient_kernel, out_shape=(pltpu.HBM((TOK, D), F32), pair...]
    all_to_all x0 -> x1, starting transfers between devices: none -> 3.76 us  [exchange(): lax.all_to_all(values.reshape(SCENE, 3 * UNITS, 128), SCENE_AXES, split_a...]
    unnamed x24 -> x30, local copies, waits for them, and re-layouts: 6.7 us -> 9.42 us
    pallas_call x1, Pallas kernels: 3.15 us -> 1.77 us  [on_device(): pl.pallas_call(edge_kernel, out_shape=shape(3 * TOK, 128), in_specs=[VMEM...]
  transfers between devices with their start and end apart: 4 -> 5, of which waited for: 2 -> 3; matrix products, arithmetic and copies ran while one was open for 0% -> 0% of each run, Pallas kernels for 9% -> 14%
where the time goes in v4:
time: 114 us
  Pallas kernels  36.6 us (32%)
  waiting for transfers between devices  29.1 us (26%)
  blocking collectives  19 us (17%)
  starting transfers between devices  16.2 us (14%)
  local copies, waits for them, and re-layouts  9.42 us (8%)
  other arithmetic  2.72 us (2%)
    all_to_all x1, waiting for transfers between devices, on_device(): lax.all_to_all(keep + got, CHIP_AXES, split_axis=0, concat_axis=0, tiled=...  19.6 us
    all_to_all x1, blocking collectives, exchange(): lax.all_to_all(values.reshape(SCENE, 3 * UNITS, 128), SCENE_AXES, split_a...  19 us
    pallas_call x1, Pallas kernels, on_device(): pl.pallas_call(gradient_kernel, out_shape=(pltpu.HBM((TOK, D), F32), pair...  11.2 us
    unnamed x30, local copies, waits for them, and re-layouts  9.42 us
    pallas_call x1, Pallas kernels, on_device(): pl.pallas_call(output_kernel, grid=(FF // SUB,), out_shape=(shape(TOK, D)...  6.98 us
    pallas_call x1, Pallas kernels, on_device(): pl.pallas_call(attention_kernel, out_shape=shape(3 * TOK, 128), in_specs=...  6.53 us
    all_to_all x1, starting transfers between devices, on_device(): lax.all_to_all(keep + got, CHIP_AXES, split_axis=0, concat_axis=0, tiled=...  6.29 us
    ppermute x1, starting transfers between devices, on_device(): mate = lax.ppermute(jnp.where(even, tail, head), SCENE_AXES, mates)  5.42 us
  transfers between devices with their start and end apart: 5, of which 3 were waited for; matrix products, arithmetic and copies ran while one was open for 0% of the time, Pallas kernels for 14%

profile of v4, /device:TPU:0, one launch (start us, length us, event | category | flops | bytes accessed | tf_op | source)
XLA Modules:
  0.0 113.8 jit_solution(7251943967838798878)
XLA Ops:
  0.6 1.0 select_bitcast_fusion
  1.6 0.7 collective-permute-start.1
  2.3 5.4 %collective-permute-start = (f32[64,384]{1,0:T(8,128)S(1)}, f32[64,384]{1,0:T(8,128)S(1)}, u32[]{:S(2)}, u32[]{:S(2)}) collective-permute-start(f32[64,384]{1,0:T(8,128)S(1)} %get-tuple-element.31), channel_id=1, source_target_pairs={{0,8},{8,0},{16,24},{24,16},{32,40},{40,32},{48,56},{56,48},{64,72... | collective-permute-start | bytes 294920 | tf_op jit(solution)/shard_map/ppermute | solution.py:454
  7.7 0.0 copy-start
  7.7 0.0 copy-start.10
  7.7 0.0 copy-start.11
  7.7 4.2 %inner.1.inner_ref = f32[256,384]{1,0:T(8,128)S(1)} custom-call(f32[384,384]{1,0:T(8,128)} %bitcast.16, s32[27,1,384]{2,1,0:T(1,128)} %nbr_ref.1, f32[27,384]{1,0:T(8,128)} %weight_ref.1), custom_call_target="tpu_custom_call" | custom-call | flops 3000000000 | bytes 1000000 | tf_op jit(solution)/shard_map/inner/pallas_call | solution.py:456
  11.9 0.0 copy-start.5
  11.9 0.0 copy-start.6
  11.9 0.0 copy-start.9
  11.9 0.0 collective-permute-done.1.other_ref
  11.9 0.0 collective-permute-done.mate_ref
  12.0 0.0 copy-done
  12.0 0.0 copy-done.10
  12.0 0.0 copy-done.11
  12.0 1.8 %edges.1.first_ref = f32[1152,128]{1,0:T(8,128)S(1)} custom-call(f32[384,384]{1,0:T(8,128)S(1)} %bitcast.17, f32[64,384]{1,0:T(8,128)S(1)} %collective-permute-done.mate_ref, f32[64,384]{1,0:T(8,128)S(1)} %collective-permute-done.1.other_ref, s32[27,1,384]{2,1,0:T(1,128)S(1)} %copy-done.11, f32[27,384]{1,0:T(8,128)S(1)} %copy-done.10, ...), custom_call_target="tpu_custom_call" | custom-call | flops 6000000000 | bytes 2000000 | tf_op jit(solution)/shard_map/edges/pallas_call | solution.py:471
  13.8 19.0 %all_to_all.15 = f32[16,72,128]{2,1,0:T(8,128)S(1)} all-to-all(f32[16,72,128]{2,1,0:T(8,128)S(1)} %bitcast.13), channel_id=1, replica_groups=mesh['y'=4,'zh'=2,'c'=2,'x'=4,'zl'=2] {'y','zh','c'}, dimensions={0} | all-to-all | bytes 1179648 | tf_op jit(solution)/shard_map/all_to_all | solution.py:508
  32.8 0.0 copy-done.5
  32.8 0.0 copy-done.6
  32.8 0.0 copy-done.9
  32.8 0.0 copy-start.1
  32.8 6.5 %attention.1 = f32[1152,128]{1,0:T(8,128)} custom-call(f32[1152,128]{1,0:T(8,128)S(1)} %bitcast.15, f32[384,1152]{1,0:T(8,128)S(1)} %copy-done.5, f32[384,384]{1,0:T(8,128)S(1)} %copy-done.6, f32[24,32,32]{2,1,0:T(8,128)S(1)} %copy-done.9), custom_call_target="tpu_custom_call" | custom-call | flops 8000000000 | bytes 4000000 | tf_op jit(solution)/shard_map/attention/pallas_call | solution.py:513
  39.3 3.8 %all-to-all-start.1 = ((f32[16,72,128]{2,1,0:T(8,128)}), f32[16,72,128]{2,1,0:T(8,128)S(1)}, u32[]{:S(2)}, u32[]{:S(2)}) async-start(f32[16,72,128]{2,1,0:T(8,128)} %bitcast.5), calls=%async_computation.1 | async-start | bytes 1179648 | tf_op jit(solution)/shard_map/all_to_all | solution.py:508
  43.1 0.0 copy-done.1
  43.1 0.0 copy-start.3
  43.1 1.7 %copy-done.3 = f32[1536,384]{1,0:T(8,128)S(1)} copy-done((f32[1536,384]{1,0:T(8,128)S(1)}, f32[1536,384]{1,0:T(8,128)}, u32[]{:S(2)}) %copy-start.3) | copy-done | bytes 2359320
  44.8 0.0 copy-start.7
  44.8 1.1 copy-done.7
  45.8 5.1 %prepare.1 = (f32[384,1536]{1,0:T(8,128)}, bf16[384,1536]{1,0:T(8,128)(2,1)}, bf16[384,1536]{1,0:T(8,128)(2,1)}, bf16[768,384]{1,0:T(8,128)(2,1)}) custom-call(f32[384,384]{1,0:T(8,128)S(1)} %bitcast.18, f32[384,1536]{1,0:T(8,128)S(1)} %copy-done.1, f32[1536,384]{1,0:T(8,128)S(1)} %copy-done.3), custom_call_target="tpu_custom_call" | custom-call | flops 4000000000 | bytes 12000000 | tf_op jit(solution)/shard_map/prepare/pallas_call | solution.py:482
  50.9 4.9 %all-to-all-done.1 = f32[16,72,128]{2,1,0:T(8,128)S(1)} async-done(((f32[16,72,128]{2,1,0:T(8,128)}), f32[16,72,128]{2,1,0:T(8,128)S(1)}, u32[]{:S(2)}, u32[]{:S(2)}) %all-to-all-start.1) | async-done | bytes 589856 | tf_op jit(solution)/shard_map/all_to_all | solution.py:508
  55.9 11.2 %gradient.1 = (f32[384,384]{1,0:T(8,128)}, bf16[6,768,256]{2,1,0:T(8,128)(2,1)}, bf16[6,768,256]{2,1,0:T(8,128)(2,1)}, f32[64,72,128]{2,1,0:T(8,128)S(1)}, f32[64,72,128]{2,1,0:T(8,128)S(1)}) custom-call(f32[1152,128]{1,0:T(8,128)S(1)} %edges.1.first_ref, f32[1152,128]{1,0:T(8,128)S(1)} %bitcast.14, f32[384,1536]{1,0:T(8,128)} %get-tuple-element.17.d_active_hbm, ...), custom_call_target="tpu_custom_call" | custom-call | flops 12000000000 | bytes 16000000 | tf_op jit(solution)/shard_map/gradient/pallas_call | solution.py:527
  67.1 0.1 collective-permute-start.2
  67.2 4.5 %collective-permute-done.2 = f32[64,72,128]{2,1,0:T(8,128)S(1)} collective-permute-done((f32[64,72,128]{2,1,0:T(8,128)S(1)}, f32[64,72,128]{2,1,0:T(8,128)S(1)}, u32[]{:S(2)}, u32[]{:S(2)}) %collective-permute-start.2) | collective-permute-done | bytes 2359328 | tf_op jit(solution)/shard_map/ppermute | solution.py:558
  71.7 1.8 %add.3 = f32[64,72,128]{2,1,0:T(8,128)} add(f32[64,72,128]{2,1,0:T(8,128)S(1)} %get-tuple-element.26, f32[64,72,128]{2,1,0:T(8,128)S(1)} %collective-permute-done.2) | non-fusion elementwise | flops 589824 | bytes 7077888 | tf_op jit(solution)/shard_map/add | solution.py:579
  73.5 0.0 copy-start.8
  73.5 0.0 copy-start.14
  73.5 6.3 %all-to-all-start.2 = ((f32[64,72,128]{2,1,0:T(8,128)}), f32[64,72,128]{2,1,0:T(8,128)S(1)}, u32[]{:S(2)}, u32[]{:S(2)}) async-start(f32[64,72,128]{2,1,0:T(8,128)} %add.3), calls=%async_computation.2 | async-start | bytes 4718592 | tf_op jit(solution)/shard_map/all_to_all | solution.py:579
  79.8 0.0 copy-done.8
  79.8 0.0 copy-done.14
  79.8 0.0 copy-start.2
  79.8 1.7 %copy-done.2 = f32[384,1536]{1,0:T(8,128)S(1)} copy-done((f32[384,1536]{1,0:T(8,128)S(1)}, f32[384,1536]{1,0:T(8,128)}, u32[]{:S(2)}) %copy-start.2) | copy-done | bytes 2359320
  81.4 0.0 copy-start.4
  81.4 1.7 %copy-done.4 = f32[1536,384]{1,0:T(8,128)S(1)} copy-done((f32[1536,384]{1,0:T(8,128)S(1)}, f32[1536,384]{1,0:T(8,128)}, u32[]{:S(2)}) %copy-start.4) | copy-done | bytes 2359320
  83.1 0.0 copy-start.12
  83.1 1.7 %copy-done.12 = bf16[6,768,256]{2,1,0:T(8,128)(2,1)S(1)} copy-done((bf16[6,768,256]{2,1,0:T(8,128)(2,1)S(1)}, bf16[6,768,256]{2,1,0:T(8,128)(2,1)}, u32[]{:S(2)}) %copy-start.12) | copy-done | bytes 2359320
  84.8 0.0 copy-start.13
  84.8 1.7 %copy-done.13 = bf16[6,768,256]{2,1,0:T(8,128)(2,1)S(1)} copy-done((bf16[6,768,256]{2,1,0:T(8,128)(2,1)S(1)}, bf16[6,768,256]{2,1,0:T(8,128)(2,1)}, u32[]{:S(2)}) %copy-start.13) | copy-done | bytes 2359320
  86.4 7.0 %outputs.1 = (f32[384,384]{1,0:T(8,128)}, f32[384,384]{1,0:T(8,128)}) custom-call(f32[384,384]{1,0:T(8,128)S(1)} %copy-done.14, f32[384,384]{1,0:T(8,128)S(1)} %bitcast.19, bf16[6,768,256]{2,1,0:T(8,128)(2,1)S(1)} %copy-done.12, bf16[6,768,256]{2,1,0:T(8,128)(2,1)S(1)} %copy-done.13, f32[384,1536]{1,0:T(8,128)S(1)} %copy-done.2, f32[1536,384]{1,0:T(8,128)S(1)} %copy-done.4), custom_call_target="tpu_custom_call" | custom-call | flops 6000000000 | bytes 11000000 | tf_op jit(solution)/shard_map/outputs/pallas_call | solution.py:561
  93.4 19.6 %all-to-all-done.2.pieces_ref = f32[64,72,128]{2,1,0:T(8,128)S(1)} async-done(((f32[64,72,128]{2,1,0:T(8,128)}), f32[64,72,128]{2,1,0:T(8,128)S(1)}, u32[]{:S(2)}, u32[]{:S(2)}) %all-to-all-start.2) | async-done | bytes 2359328 | tf_op jit(solution)/shard_map/all_to_all | solution.py:579
  113.0 0.8 finish.1
Async XLA Ops:
  1.6 10.3 %collective-permute-start.1 = (f32[64,384]{1,0:T(8,128)S(1)}, f32[64,384]{1,0:T(8,128)S(1)}, u32[]{:S(2)}, u32[]{:S(2)}) collective-permute-start(f32[64,384]{1,0:T(8,128)S(1)} %get-tuple-element.30), channel_id=1, source_target_pairs={{8,16},{24,32},{40,48},{56,64},{72,80},{88,96},{104,112},{16,8},{3... | collective-permute-start | bytes 294920 | tf_op jit(solution)/shard_map/ppermute | solution.py:453
  2.3 9.7 %collective-permute-start = (f32[64,384]{1,0:T(8,128)S(1)}, f32[64,384]{1,0:T(8,128)S(1)}, u32[]{:S(2)}, u32[]{:S(2)}) collective-permute-start(f32[64,384]{1,0:T(8,128)S(1)} %get-tuple-element.31), channel_id=1, source_target_pairs={{0,8},{8,0},{16,24},{24,16},{32,40},{40,32},{48,56},{56,48},{64,72... | collective-permute-start | bytes 294920 | tf_op jit(solution)/shard_map/ppermute | solution.py:454
  7.7 4.3 %copy-start = (f32[1,384,384]{2,1,0:T(8,128)S(1)}, f32[1,384,384]{2,1,0:T(8,128)}, u32[]{:S(2)}) copy-start(f32[1,384,384]{2,1,0:T(8,128)} %param.9) | copy-start | bytes 1769476
  7.7 4.3 %copy-start.10 = (f32[27,384]{1,0:T(8,128)S(1)}, f32[27,384]{1,0:T(8,128)}, u32[]{:S(2)}) copy-start(f32[27,384]{1,0:T(8,128)} %weight_ref.1) | copy-start | bytes 124420
  7.7 4.3 %copy-start.11 = (s32[27,1,384]{2,1,0:T(1,128)S(1)}, s32[27,1,384]{2,1,0:T(1,128)}, u32[]{:S(2)}) copy-start(s32[27,1,384]{2,1,0:T(1,128)} %nbr_ref.1) | copy-start | bytes 124420
  11.9 20.9 %copy-start.5 = (f32[384,1152]{1,0:T(8,128)S(1)}, f32[384,1152]{1,0:T(8,128)}, u32[]{:S(2)}) copy-start(f32[384,1152]{1,0:T(8,128)} %qkv_ref.1) | copy-start | bytes 5308420
  11.9 20.8 %copy-start.6 = (f32[384,384]{1,0:T(8,128)S(1)}, f32[384,384]{1,0:T(8,128)}, u32[]{:S(2)}) copy-start(f32[384,384]{1,0:T(8,128)} %wout_ref.1) | copy-start | bytes 1769476
  11.9 20.8 %copy-start.9 = (f32[24,32,32]{2,1,0:T(8,128)S(1)}, f32[24,32,32]{2,1,0:T(8,128)}, u32[]{:S(2)}) copy-start(f32[24,32,32]{2,1,0:T(8,128)} %bias_ref.1) | copy-start | bytes 294916
  32.8 10.3 %copy-start.1 = (f32[384,1536]{1,0:T(8,128)S(1)}, f32[384,1536]{1,0:T(8,128)}, u32[]{:S(2)}) copy-start(f32[384,1536]{1,0:T(8,128)} %up_ref.3) | copy-start | bytes 7077892
  39.3 16.6 %all-to-all-start.1 = ((f32[16,72,128]{2,1,0:T(8,128)}), f32[16,72,128]{2,1,0:T(8,128)S(1)}, u32[]{:S(2)}, u32[]{:S(2)}) async-start(f32[16,72,128]{2,1,0:T(8,128)} %bitcast.5), calls=%async_computation.1 | async-start | bytes 1179648 | tf_op jit(solution)/shard_map/all_to_all | solution.py:508
  43.1 1.7 %copy-start.3 = (f32[1536,384]{1,0:T(8,128)S(1)}, f32[1536,384]{1,0:T(8,128)}, u32[]{:S(2)}) copy-start(f32[1536,384]{1,0:T(8,128)} %down_ref.3) | copy-start | bytes 7077892
  44.8 1.1 copy-start.7
  67.1 4.6 %collective-permute-start.2 = (f32[64,72,128]{2,1,0:T(8,128)S(1)}, f32[64,72,128]{2,1,0:T(8,128)S(1)}, u32[]{:S(2)}, u32[]{:S(2)}) collective-permute-start(f32[64,72,128]{2,1,0:T(8,128)S(1)} %get-tuple-element.27), channel_id=1, source_target_pairs={{0,8},{8,0},{1,9},{9,1},{2,10},{10,2},{3,11},{11,3},{4,12},{12,4},... | collective-permute-start | bytes 7077896 | tf_op jit(solution)/shard_map/ppermute | solution.py:558
  73.5 6.3 %copy-start.8 = (f32[1,384,384]{2,1,0:T(8,128)S(1)}, f32[1,384,384]{2,1,0:T(8,128)}, u32[]{:S(2)}) copy-start(f32[1,384,384]{2,1,0:T(8,128)} %param.11) | copy-start | bytes 1769476
  73.5 6.3 %copy-start.14 = (f32[384,384]{1,0:T(8,128)S(1)}, f32[384,384]{1,0:T(8,128)}, u32[]{:S(2)}) copy-start(f32[384,384]{1,0:T(8,128)} %get-tuple-element.21.mid_ref) | copy-start | bytes 1769476
  73.5 39.6 %all-to-all-start.2 = ((f32[64,72,128]{2,1,0:T(8,128)}), f32[64,72,128]{2,1,0:T(8,128)S(1)}, u32[]{:S(2)}, u32[]{:S(2)}) async-start(f32[64,72,128]{2,1,0:T(8,128)} %add.3), calls=%async_computation.2 | async-start | bytes 4718592 | tf_op jit(solution)/shard_map/all_to_all | solution.py:579
  79.8 1.7 %copy-start.2 = (f32[384,1536]{1,0:T(8,128)S(1)}, f32[384,1536]{1,0:T(8,128)}, u32[]{:S(2)}) copy-start(f32[384,1536]{1,0:T(8,128)} %up_ref.3) | copy-start | bytes 7077892
  81.4 1.7 %copy-start.4 = (f32[1536,384]{1,0:T(8,128)S(1)}, f32[1536,384]{1,0:T(8,128)}, u32[]{:S(2)}) copy-start(f32[1536,384]{1,0:T(8,128)} %down_ref.3) | copy-start | bytes 7077892
  83.1 1.7 %copy-start.12 = (bf16[6,768,256]{2,1,0:T(8,128)(2,1)S(1)}, bf16[6,768,256]{2,1,0:T(8,128)(2,1)}, u32[]{:S(2)}) copy-start(bf16[6,768,256]{2,1,0:T(8,128)(2,1)} %get-tuple-element.22.act_ref) | copy-start | bytes 7077892
  84.8 1.7 %copy-start.13 = (bf16[6,768,256]{2,1,0:T(8,128)(2,1)S(1)}, bf16[6,768,256]{2,1,0:T(8,128)(2,1)}, u32[]{:S(2)}) copy-start(bf16[6,768,256]{2,1,0:T(8,128)(2,1)} %get-tuple-element.23.dh_ref) | copy-start | bytes 7077892

commit v5 on v4

--- a/solution.py
+++ b/solution.py
@@ -164,53 +164,60 @@
     )
     qkv = dot_stacked(stack(normed), parts_of(qkv_ref[...]))
     head_of = lax.broadcasted_iota(jnp.int32, (16, 128), 1) // 16
+    masks = [jnp.where(head_of == h, 1.0, 0.0).astype(BF16) for h in range(8)]
     row_head = (lax.broadcasted_iota(jnp.int32, (256, 128), 0) // 16) % 8
     ones = jnp.where(
         row_head == lax.broadcasted_iota(jnp.int32, (256, 128), 1) // 16, 1.0, 0.0
     ).astype(BF16)
-    lane_all = lax.broadcasted_iota(jnp.int32, (TOK, 128), 1)
+    lane = lax.broadcasted_iota(jnp.int32, (32, 128), 1)
+    lowers = [(shift, lane % (2 * shift) < shift) for shift in (8, 4, 2, 1)]
 
     def spread(values, group):
         pieces = []
         for half in range(2):
             piece = values[32 * group + 16 * half : 32 * group + 16 * half + 16]
-            pieces += [jnp.where(head_of == h, piece, 0.0) for h in range(8)]
-        return parts_of(jnp.concatenate(pieces, axis=0))
-
-    attended = []
-    for t in range(3):
+            pieces += [piece * mask for mask in masks]
+        return jnp.concatenate(pieces, axis=0)
+
+    def score(t):
         cols = slice(128 * t, 128 * (t + 1))
-        query = qkv[:, :D][:, cols] * 0.25
-        keys = qkv[:, D : 2 * D][:, cols]
-        vals = qkv[:, 2 * D :][:, cols]
+        q_high, q_low = parts_of(qkv[:, :D][:, cols] * 0.25)
+        keys = parts_of(qkv[:, D : 2 * D][:, cols])
         bias = jnp.concatenate(
             [bias_ref[8 * t + h][:, 16 * half : 16 * half + 16] for half in range(2) for h in range(8)],
             axis=1,
         )
         for g in range(12):
             rows = slice(32 * g, 32 * g + 32)
-            scores_ref[rows, :] = dot_stacked(stack(query[rows]), spread(keys, g), NT) + bias
-        score = scores_ref[...]
-        top = jnp.maximum(score[:, :128], score[:, 128:])
-        for shift in (8, 4, 2, 1):
-            other = jnp.where(
-                lane_all % (2 * shift) < shift,
-                pltpu.roll(top, 128 - shift, 1),
-                pltpu.roll(top, shift, 1),
-            )
-            top = jnp.maximum(top, other)
-        weight = jnp.exp(score - jnp.concatenate([top, top], axis=1))
-        w_high, w_low = parts_of(weight)
+            query = jnp.concatenate([q_high[rows], q_low[rows]], axis=0)
+            spread_keys = tuple(spread(part, g) for part in keys)
+            scores_ref[t, rows, :] = dot_stacked(query, spread_keys, NT) + bias
+
+    def attend(t):
+        vals = parts_of(qkv[:, 2 * D :][:, 128 * t : 128 * (t + 1)])
         pieces = []
         for g in range(12):
-            v_high, v_low = spread(vals, g)
+            rows = slice(32 * g, 32 * g + 32)
+            scores = scores_ref[t, rows, :]
+            top = jnp.maximum(scores[:, :128], scores[:, 128:])
+            for shift, lower in lowers:
+                other = jnp.where(lower, pltpu.roll(top, 128 - shift, 1), pltpu.roll(top, shift, 1))
+                top = jnp.maximum(top, other)
+            weight = jnp.exp(scores - jnp.concatenate([top, top], axis=1))
+            w_high, w_low = parts_of(weight)
+            v_high, v_low = (spread(part, g) for part in vals)
             wide = jnp.concatenate([v_high, ones], axis=1)
-            rows = slice(32 * g, 32 * g + 32)
-            both = dot(jnp.concatenate([w_high[rows], w_low[rows]], axis=0), wide)
+            both = dot(jnp.concatenate([w_high, w_low], axis=0), wide)
             total = both[:32] + both[32:]
-            mixed = total[:, :128] + dot(w_high[rows], v_low)
+            mixed = total[:, :128] + dot(w_high, v_low)
             pieces.append(mixed / total[:, 128:])
-        attended.append(jnp.concatenate(pieces, axis=0))
+        return jnp.concatenate(pieces, axis=0)
+
+    score(0)
+    score(1)
+    attended = [attend(0)]
+    score(2)
+    attended += [attend(1), attend(2)]
     attended = jnp.concatenate(attended, axis=1)
     mixed = dot_stacked(stack(attended), parts_of(wout_ref[...]))
     for t in range(3):
@@ -335,7 +342,7 @@
     left = lane < 64
     segment = lane // 32
 
-    def piece(quarter, sigma, g, beta):
+    def piece(quarter, sigma, g, beta, turned):
         row = pl.multiple_of((4 * quarter + sigma) * 24, 8)
 
         def up_tile(i, t):
@@ -347,7 +354,7 @@
             return grad_down_ref[start : start + 8, pl.ds(col, 128)]
 
         full = [up_tile(i, 2 * beta) for i in range(3)]
-        m0, m1, m2 = [up_tile(i, 1) for i in range(3)]
+        m0, m2 = up_tile(0, 1), up_tile(2, 1)
         own = left if beta == 0 else jnp.logical_not(left)
         if sigma == 0:
             c = [down_tile(i, 0) for i in range(6)]
@@ -363,7 +370,7 @@
         turn = 32 * ((start - (free + 2)) % 4)
         extra = pltpu.roll(c[4], turn, 1) if turn else c[4]
         return full + [
-            jnp.where(own, m0, pltpu.roll(m1, 64, 1)),
+            jnp.where(own, m0, turned),
             jnp.where(own, m2, extra),
             jnp.where(hole, pltpu.roll(c[5], 96, 1), c[0]),
             jnp.where(hole, pltpu.roll(c[5], 64, 1), c[1]),
@@ -375,10 +382,14 @@
         def body(quarter, carry):
             for g in range(4):
                 for sigma in range(4):
+                    row = pl.multiple_of((4 * quarter + sigma) * 24 + 8, 8)
+                    turned = pltpu.roll(
+                        grad_up_ref[pl.ds(row, 8), 384 * g + 128 : 384 * g + 256], 64, 1
+                    )
                     for beta in range(2):
                         ref = odd_ref if sigma % 2 else even_ref
                         where = (2 * quarter + sigma // 2) * 8 + 2 * g + beta
-                        for i, rows in enumerate(piece(quarter, sigma, g, beta)):
+                        for i, rows in enumerate(piece(quarter, sigma, g, beta, turned)):
                             ref[where, 8 * i : 8 * (i + 1), :] = rows
             return carry
 
@@ -515,7 +526,7 @@
         out_shape=shape(3 * TOK, 128),
         in_specs=[VMEM_SPEC] * 4,
         out_specs=VMEM_SPEC,
-        scratch_shapes=[pltpu.VMEM((3 * TOK, 128), F32), pltpu.VMEM((TOK, 256), F32)],
+        scratch_shapes=[pltpu.VMEM((3 * TOK, 128), F32), pltpu.VMEM((3, TOK, 256), F32)],
         compiler_params=params(24),
         cost_estimate=cost(8e9, 4e6),
         name="attention",

time: 114 us -> 114 us (level)
  no operation moved by 1% of the time
where the time goes in v5:
time: 114 us; the launch traced here: 113 us
  Pallas kernels  36 us (32%)
  waiting for transfers between devices  29.1 us (26%)
  blocking collectives  19 us (17%)
  starting transfers between devices  16.2 us (14%)
  local copies, waits for them, and re-layouts  9.42 us (8%)
  other arithmetic  2.72 us (2%)
    all_to_all x1, waiting for transfers between devices, on_device(): lax.all_to_all(keep + got, CHIP_AXES, split_axis=0, concat_axis=0, tiled=...  19.6 us
    all_to_all x1, blocking collectives, exchange(): lax.all_to_all(values.reshape(SCENE, 3 * UNITS, 128), SCENE_AXES, split_a...  19 us
    pallas_call x1, Pallas kernels, on_device(): pl.pallas_call(gradient_kernel, out_shape=(pltpu.HBM((TOK, D), F32), pair...  11.2 us
    unnamed x30, local copies, waits for them, and re-layouts  9.42 us
    pallas_call x1, Pallas kernels, on_device(): pl.pallas_call(output_kernel, grid=(FF // SUB,), out_shape=(shape(TOK, D)...  6.97 us
    all_to_all x1, starting transfers between devices, on_device(): lax.all_to_all(keep + got, CHIP_AXES, split_axis=0, concat_axis=0, tiled=...  6.27 us
    pallas_call x1, Pallas kernels, on_device(): pl.pallas_call(attention_kernel, out_shape=shape(3 * TOK, 128), in_specs=...  5.93 us
    ppermute x1, starting transfers between devices, on_device(): mate = lax.ppermute(jnp.where(even, tail, head), SCENE_AXES, mates)  5.42 us
  transfers between devices with their start and end apart: 5, of which 3 were waited for; matrix products, arithmetic and copies ran while one was open for 0% of the time, Pallas kernels for 14%

profile of v5, /device:TPU:0, one launch (start us, length us, event | category | flops | bytes accessed | tf_op | source)
XLA Modules:
  0.0 113.2 jit_solution(1600986746741721045)
XLA Ops:
  0.6 1.0 select_bitcast_fusion
  1.6 0.7 collective-permute-start.1
  2.3 5.4 %collective-permute-start = (f32[64,384]{1,0:T(8,128)S(1)}, f32[64,384]{1,0:T(8,128)S(1)}, u32[]{:S(2)}, u32[]{:S(2)}) collective-permute-start(f32[64,384]{1,0:T(8,128)S(1)} %get-tuple-element.31), channel_id=1, source_target_pairs={{0,8},{8,0},{16,24},{24,16},{32,40},{40,32},{48,56},{56,48},{64,72... | collective-permute-start | bytes 294920 | tf_op jit(solution)/shard_map/ppermute | solution.py:465
  7.7 0.0 copy-start
  7.7 0.0 copy-start.10
  7.7 0.0 copy-start.11
  7.7 4.2 %inner.1.inner_ref = f32[256,384]{1,0:T(8,128)S(1)} custom-call(f32[384,384]{1,0:T(8,128)} %bitcast.16, s32[27,1,384]{2,1,0:T(1,128)} %nbr_ref.1, f32[27,384]{1,0:T(8,128)} %weight_ref.1), custom_call_target="tpu_custom_call" | custom-call | flops 3000000000 | bytes 1000000 | tf_op jit(solution)/shard_map/inner/pallas_call | solution.py:467
  11.9 0.0 copy-start.5
  11.9 0.0 copy-start.6
  11.9 0.0 copy-start.9
  11.9 0.0 collective-permute-done.1.other_ref
  11.9 0.0 collective-permute-done.mate_ref
  12.0 0.0 copy-done
  12.0 0.0 copy-done.10
  12.0 0.0 copy-done.11
  12.0 1.8 %edges.1.first_ref = f32[1152,128]{1,0:T(8,128)S(1)} custom-call(f32[384,384]{1,0:T(8,128)S(1)} %bitcast.17, f32[64,384]{1,0:T(8,128)S(1)} %collective-permute-done.mate_ref, f32[64,384]{1,0:T(8,128)S(1)} %collective-permute-done.1.other_ref, s32[27,1,384]{2,1,0:T(1,128)S(1)} %copy-done.11, f32[27,384]{1,0:T(8,128)S(1)} %copy-done.10, ...), custom_call_target="tpu_custom_call" | custom-call | flops 6000000000 | bytes 2000000 | tf_op jit(solution)/shard_map/edges/pallas_call | solution.py:482
  13.8 19.0 %all_to_all.15 = f32[16,72,128]{2,1,0:T(8,128)S(1)} all-to-all(f32[16,72,128]{2,1,0:T(8,128)S(1)} %bitcast.13), channel_id=1, replica_groups=mesh['y'=4,'zh'=2,'c'=2,'x'=4,'zl'=2] {'y','zh','c'}, dimensions={0} | all-to-all | bytes 1179648 | tf_op jit(solution)/shard_map/all_to_all | solution.py:519
  32.8 0.0 copy-done.5
  32.8 0.0 copy-done.6
  32.8 0.0 copy-done.9
  32.8 0.0 copy-start.1
  32.8 5.9 %attention.1 = f32[1152,128]{1,0:T(8,128)} custom-call(f32[1152,128]{1,0:T(8,128)S(1)} %bitcast.15, f32[384,1152]{1,0:T(8,128)S(1)} %copy-done.5, f32[384,384]{1,0:T(8,128)S(1)} %copy-done.6, f32[24,32,32]{2,1,0:T(8,128)S(1)} %copy-done.9), custom_call_target="tpu_custom_call" | custom-call | flops 8000000000 | bytes 4000000 | tf_op jit(solution)/shard_map/attention/pallas_call | solution.py:524
  38.7 3.8 %all-to-all-start.1 = ((f32[16,72,128]{2,1,0:T(8,128)}), f32[16,72,128]{2,1,0:T(8,128)S(1)}, u32[]{:S(2)}, u32[]{:S(2)}) async-start(f32[16,72,128]{2,1,0:T(8,128)} %bitcast.5), calls=%async_computation.1 | async-start | bytes 1179648 | tf_op jit(solution)/shard_map/all_to_all | solution.py:519
  42.5 0.0 copy-done.1
  42.5 0.0 copy-start.3
  42.5 1.7 %copy-done.3 = f32[1536,384]{1,0:T(8,128)S(1)} copy-done((f32[1536,384]{1,0:T(8,128)S(1)}, f32[1536,384]{1,0:T(8,128)}, u32[]{:S(2)}) %copy-start.3) | copy-done | bytes 2359320
  44.2 0.0 copy-start.7
  44.2 1.1 copy-done.7
  45.2 5.1 %prepare.1 = (f32[384,1536]{1,0:T(8,128)}, bf16[384,1536]{1,0:T(8,128)(2,1)}, bf16[384,1536]{1,0:T(8,128)(2,1)}, bf16[768,384]{1,0:T(8,128)(2,1)}) custom-call(f32[384,384]{1,0:T(8,128)S(1)} %bitcast.18, f32[384,1536]{1,0:T(8,128)S(1)} %copy-done.1, f32[1536,384]{1,0:T(8,128)S(1)} %copy-done.3), custom_call_target="tpu_custom_call" | custom-call | flops 4000000000 | bytes 12000000 | tf_op jit(solution)/shard_map/prepare/pallas_call | solution.py:493
  50.3 5.0 %all-to-all-done.1 = f32[16,72,128]{2,1,0:T(8,128)S(1)} async-done(((f32[16,72,128]{2,1,0:T(8,128)}), f32[16,72,128]{2,1,0:T(8,128)S(1)}, u32[]{:S(2)}, u32[]{:S(2)}) %all-to-all-start.1) | async-done | bytes 589856 | tf_op jit(solution)/shard_map/all_to_all | solution.py:519
  55.3 11.2 %gradient.1 = (f32[384,384]{1,0:T(8,128)}, bf16[6,768,256]{2,1,0:T(8,128)(2,1)}, bf16[6,768,256]{2,1,0:T(8,128)(2,1)}, f32[64,72,128]{2,1,0:T(8,128)S(1)}, f32[64,72,128]{2,1,0:T(8,128)S(1)}) custom-call(f32[1152,128]{1,0:T(8,128)S(1)} %edges.1.first_ref, f32[1152,128]{1,0:T(8,128)S(1)} %bitcast.14, f32[384,1536]{1,0:T(8,128)} %get-tuple-element.17.d_active_hbm, ...), custom_call_target="tpu_custom_call" | custom-call | flops 12000000000 | bytes 16000000 | tf_op jit(solution)/shard_map/gradient/pallas_call | solution.py:538
  66.5 0.1 collective-permute-start.2
  66.6 4.5 %collective-permute-done.2 = f32[64,72,128]{2,1,0:T(8,128)S(1)} collective-permute-done((f32[64,72,128]{2,1,0:T(8,128)S(1)}, f32[64,72,128]{2,1,0:T(8,128)S(1)}, u32[]{:S(2)}, u32[]{:S(2)}) %collective-permute-start.2) | collective-permute-done | bytes 2359328 | tf_op jit(solution)/shard_map/ppermute | solution.py:569
  71.1 1.8 %add.3 = f32[64,72,128]{2,1,0:T(8,128)} add(f32[64,72,128]{2,1,0:T(8,128)S(1)} %get-tuple-element.26, f32[64,72,128]{2,1,0:T(8,128)S(1)} %collective-permute-done.2) | non-fusion elementwise | flops 589824 | bytes 7077888 | tf_op jit(solution)/shard_map/add | solution.py:590
  72.9 0.0 copy-start.8
  72.9 0.0 copy-start.14
  72.9 6.3 %all-to-all-start.2 = ((f32[64,72,128]{2,1,0:T(8,128)}), f32[64,72,128]{2,1,0:T(8,128)S(1)}, u32[]{:S(2)}, u32[]{:S(2)}) async-start(f32[64,72,128]{2,1,0:T(8,128)} %add.3), calls=%async_computation.2 | async-start | bytes 4718592 | tf_op jit(solution)/shard_map/all_to_all | solution.py:590
  79.1 0.0 copy-done.8
  79.2 0.0 copy-done.14
  79.2 0.0 copy-start.2
  79.2 1.7 %copy-done.2 = f32[384,1536]{1,0:T(8,128)S(1)} copy-done((f32[384,1536]{1,0:T(8,128)S(1)}, f32[384,1536]{1,0:T(8,128)}, u32[]{:S(2)}) %copy-start.2) | copy-done | bytes 2359320
  80.8 0.0 copy-start.4
  80.8 1.7 %copy-done.4 = f32[1536,384]{1,0:T(8,128)S(1)} copy-done((f32[1536,384]{1,0:T(8,128)S(1)}, f32[1536,384]{1,0:T(8,128)}, u32[]{:S(2)}) %copy-start.4) | copy-done | bytes 2359320
  82.5 0.0 copy-start.12
  82.5 1.7 %copy-done.12 = bf16[6,768,256]{2,1,0:T(8,128)(2,1)S(1)} copy-done((bf16[6,768,256]{2,1,0:T(8,128)(2,1)S(1)}, bf16[6,768,256]{2,1,0:T(8,128)(2,1)}, u32[]{:S(2)}) %copy-start.12) | copy-done | bytes 2359320
  84.2 0.0 copy-start.13
  84.2 1.7 %copy-done.13 = bf16[6,768,256]{2,1,0:T(8,128)(2,1)S(1)} copy-done((bf16[6,768,256]{2,1,0:T(8,128)(2,1)S(1)}, bf16[6,768,256]{2,1,0:T(8,128)(2,1)}, u32[]{:S(2)}) %copy-start.13) | copy-done | bytes 2359320
  85.8 7.0 %outputs.1 = (f32[384,384]{1,0:T(8,128)}, f32[384,384]{1,0:T(8,128)}) custom-call(f32[384,384]{1,0:T(8,128)S(1)} %copy-done.14, f32[384,384]{1,0:T(8,128)S(1)} %bitcast.19, bf16[6,768,256]{2,1,0:T(8,128)(2,1)S(1)} %copy-done.12, bf16[6,768,256]{2,1,0:T(8,128)(2,1)S(1)} %copy-done.13, f32[384,1536]{1,0:T(8,128)S(1)} %copy-done.2, f32[1536,384]{1,0:T(8,128)S(1)} %copy-done.4), custom_call_target="tpu_custom_call" | custom-call | flops 6000000000 | bytes 11000000 | tf_op jit(solution)/shard_map/outputs/pallas_call | solution.py:572
  92.8 19.6 %all-to-all-done.2.pieces_ref = f32[64,72,128]{2,1,0:T(8,128)S(1)} async-done(((f32[64,72,128]{2,1,0:T(8,128)}), f32[64,72,128]{2,1,0:T(8,128)S(1)}, u32[]{:S(2)}, u32[]{:S(2)}) %all-to-all-start.2) | async-done | bytes 2359328 | tf_op jit(solution)/shard_map/all_to_all | solution.py:590
  112.4 0.8 finish.1
Async XLA Ops:
  1.6 10.3 %collective-permute-start.1 = (f32[64,384]{1,0:T(8,128)S(1)}, f32[64,384]{1,0:T(8,128)S(1)}, u32[]{:S(2)}, u32[]{:S(2)}) collective-permute-start(f32[64,384]{1,0:T(8,128)S(1)} %get-tuple-element.30), channel_id=1, source_target_pairs={{8,16},{24,32},{40,48},{56,64},{72,80},{88,96},{104,112},{16,8},{3... | collective-permute-start | bytes 294920 | tf_op jit(solution)/shard_map/ppermute | solution.py:464
  2.3 9.7 %collective-permute-start = (f32[64,384]{1,0:T(8,128)S(1)}, f32[64,384]{1,0:T(8,128)S(1)}, u32[]{:S(2)}, u32[]{:S(2)}) collective-permute-start(f32[64,384]{1,0:T(8,128)S(1)} %get-tuple-element.31), channel_id=1, source_target_pairs={{0,8},{8,0},{16,24},{24,16},{32,40},{40,32},{48,56},{56,48},{64,72... | collective-permute-start | bytes 294920 | tf_op jit(solution)/shard_map/ppermute | solution.py:465
  7.7 4.3 %copy-start = (f32[1,384,384]{2,1,0:T(8,128)S(1)}, f32[1,384,384]{2,1,0:T(8,128)}, u32[]{:S(2)}) copy-start(f32[1,384,384]{2,1,0:T(8,128)} %param.9) | copy-start | bytes 1769476
  7.7 4.3 %copy-start.10 = (f32[27,384]{1,0:T(8,128)S(1)}, f32[27,384]{1,0:T(8,128)}, u32[]{:S(2)}) copy-start(f32[27,384]{1,0:T(8,128)} %weight_ref.1) | copy-start | bytes 124420
  7.7 4.3 %copy-start.11 = (s32[27,1,384]{2,1,0:T(1,128)S(1)}, s32[27,1,384]{2,1,0:T(1,128)}, u32[]{:S(2)}) copy-start(s32[27,1,384]{2,1,0:T(1,128)} %nbr_ref.1) | copy-start | bytes 124420
  11.9 20.9 %copy-start.5 = (f32[384,1152]{1,0:T(8,128)S(1)}, f32[384,1152]{1,0:T(8,128)}, u32[]{:S(2)}) copy-start(f32[384,1152]{1,0:T(8,128)} %qkv_ref.1) | copy-start | bytes 5308420
  11.9 20.8 %copy-start.6 = (f32[384,384]{1,0:T(8,128)S(1)}, f32[384,384]{1,0:T(8,128)}, u32[]{:S(2)}) copy-start(f32[384,384]{1,0:T(8,128)} %wout_ref.1) | copy-start | bytes 1769476
  11.9 20.8 %copy-start.9 = (f32[24,32,32]{2,1,0:T(8,128)S(1)}, f32[24,32,32]{2,1,0:T(8,128)}, u32[]{:S(2)}) copy-start(f32[24,32,32]{2,1,0:T(8,128)} %bias_ref.1) | copy-start | bytes 294916
  32.8 9.7 %copy-start.1 = (f32[384,1536]{1,0:T(8,128)S(1)}, f32[384,1536]{1,0:T(8,128)}, u32[]{:S(2)}) copy-start(f32[384,1536]{1,0:T(8,128)} %up_ref.3) | copy-start | bytes 7077892
  38.7 16.6 %all-to-all-start.1 = ((f32[16,72,128]{2,1,0:T(8,128)}), f32[16,72,128]{2,1,0:T(8,128)S(1)}, u32[]{:S(2)}, u32[]{:S(2)}) async-start(f32[16,72,128]{2,1,0:T(8,128)} %bitcast.5), calls=%async_computation.1 | async-start | bytes 1179648 | tf_op jit(solution)/shard_map/all_to_all | solution.py:519
  42.5 1.7 %copy-start.3 = (f32[1536,384]{1,0:T(8,128)S(1)}, f32[1536,384]{1,0:T(8,128)}, u32[]{:S(2)}) copy-start(f32[1536,384]{1,0:T(8,128)} %down_ref.3) | copy-start | bytes 7077892
  44.2 1.1 copy-start.7
  66.5 4.6 %collective-permute-start.2 = (f32[64,72,128]{2,1,0:T(8,128)S(1)}, f32[64,72,128]{2,1,0:T(8,128)S(1)}, u32[]{:S(2)}, u32[]{:S(2)}) collective-permute-start(f32[64,72,128]{2,1,0:T(8,128)S(1)} %get-tuple-element.27), channel_id=1, source_target_pairs={{0,8},{8,0},{1,9},{9,1},{2,10},{10,2},{3,11},{11,3},{4,12},{12,4},... | collective-permute-start | bytes 7077896 | tf_op jit(solution)/shard_map/ppermute | solution.py:569
  72.9 6.3 %copy-start.8 = (f32[1,384,384]{2,1,0:T(8,128)S(1)}, f32[1,384,384]{2,1,0:T(8,128)}, u32[]{:S(2)}) copy-start(f32[1,384,384]{2,1,0:T(8,128)} %param.11) | copy-start | bytes 1769476
  72.9 6.3 %copy-start.14 = (f32[384,384]{1,0:T(8,128)S(1)}, f32[384,384]{1,0:T(8,128)}, u32[]{:S(2)}) copy-start(f32[384,384]{1,0:T(8,128)} %get-tuple-element.21.mid_ref) | copy-start | bytes 1769476
  72.9 39.5 %all-to-all-start.2 = ((f32[64,72,128]{2,1,0:T(8,128)}), f32[64,72,128]{2,1,0:T(8,128)S(1)}, u32[]{:S(2)}, u32[]{:S(2)}) async-start(f32[64,72,128]{2,1,0:T(8,128)} %add.3), calls=%async_computation.2 | async-start | bytes 4718592 | tf_op jit(solution)/shard_map/all_to_all | solution.py:590
  79.2 1.7 %copy-start.2 = (f32[384,1536]{1,0:T(8,128)S(1)}, f32[384,1536]{1,0:T(8,128)}, u32[]{:S(2)}) copy-start(f32[384,1536]{1,0:T(8,128)} %up_ref.3) | copy-start | bytes 7077892
  80.8 1.7 %copy-start.4 = (f32[1536,384]{1,0:T(8,128)S(1)}, f32[1536,384]{1,0:T(8,128)}, u32[]{:S(2)}) copy-start(f32[1536,384]{1,0:T(8,128)} %down_ref.3) | copy-start | bytes 7077892
  82.5 1.7 %copy-start.12 = (bf16[6,768,256]{2,1,0:T(8,128)(2,1)S(1)}, bf16[6,768,256]{2,1,0:T(8,128)(2,1)}, u32[]{:S(2)}) copy-start(bf16[6,768,256]{2,1,0:T(8,128)(2,1)} %get-tuple-element.22.act_ref) | copy-start | bytes 7077892
  84.2 1.7 %copy-start.13 = (bf16[6,768,256]{2,1,0:T(8,128)(2,1)S(1)}, bf16[6,768,256]{2,1,0:T(8,128)(2,1)}, u32[]{:S(2)}) copy-start(bf16[6,768,256]{2,1,0:T(8,128)(2,1)} %get-tuple-element.23.dh_ref) | copy-start | bytes 7077892

commit v6 on v5

--- a/solution.py
+++ b/solution.py
@@ -23,7 +23,7 @@
 NN = (((1,), (0,)), ((), ()))
 NT = (((1,), (1,)), ((), ()))
 VMEM_SPEC = pl.BlockSpec(memory_space=pltpu.VMEM)
-SUB = 256
+SUB = 512
 
 
 def params(mebibytes):

time: 114 us -> 113 us (level)
  Pallas kernels: 36 us -> 34 us
where the time goes in v6:
time: 113 us; the launch traced here: 112 us
  Pallas kernels  34 us (30%)
  waiting for transfers between devices  30 us (27%)
  blocking collectives  19 us (17%)
  starting transfers between devices  16.2 us (14%)
  local copies, waits for them, and re-layouts  9.42 us (8%)
  other arithmetic  2.72 us (2%)
    all_to_all x1, waiting for transfers between devices, on_device(): lax.all_to_all(keep + got, CHIP_AXES, split_axis=0, concat_axis=0, tiled=...  20.5 us
    all_to_all x1, blocking collectives, exchange(): lax.all_to_all(values.reshape(SCENE, 3 * UNITS, 128), SCENE_AXES, split_a...  19 us
    pallas_call x1, Pallas kernels, on_device(): pl.pallas_call(gradient_kernel, out_shape=(pltpu.HBM((TOK, D), F32), pair...  10.2 us
    unnamed x30, local copies, waits for them, and re-layouts  9.42 us
    all_to_all x1, starting transfers between devices, on_device(): lax.all_to_all(keep + got, CHIP_AXES, split_axis=0, concat_axis=0, tiled=...  6.28 us
    pallas_call x1, Pallas kernels, on_device(): pl.pallas_call(output_kernel, grid=(FF // SUB,), out_shape=(shape(TOK, D)...  6.06 us
    pallas_call x1, Pallas kernels, on_device(): pl.pallas_call(attention_kernel, out_shape=shape(3 * TOK, 128), in_specs=...  5.93 us
    ppermute x1, starting transfers between devices, on_device(): mate = lax.ppermute(jnp.where(even, tail, head), SCENE_AXES, mates)  5.42 us
  transfers between devices with their start and end apart: 5, of which 3 were waited for; matrix products, arithmetic and copies ran while one was open for 0% of the time, Pallas kernels for 14%

profile of v6, /device:TPU:0, one launch (start us, length us, event | category | flops | bytes accessed | tf_op | source)
XLA Modules:
  0.0 112.2 jit_solution(16241873752441110566)
XLA Ops:
  0.6 1.0 select_bitcast_fusion
  1.6 0.7 collective-permute-start.1
  2.3 5.4 %collective-permute-start = (f32[64,384]{1,0:T(8,128)S(1)}, f32[64,384]{1,0:T(8,128)S(1)}, u32[]{:S(2)}, u32[]{:S(2)}) collective-permute-start(f32[64,384]{1,0:T(8,128)S(1)} %get-tuple-element.31), channel_id=1, source_target_pairs={{0,8},{8,0},{16,24},{24,16},{32,40},{40,32},{48,56},{56,48},{64,72... | collective-permute-start | bytes 294920 | tf_op jit(solution)/shard_map/ppermute | solution.py:465
  7.7 0.0 copy-start
  7.7 0.0 copy-start.10
  7.7 0.0 copy-start.11
  7.7 4.2 %inner.1.inner_ref = f32[256,384]{1,0:T(8,128)S(1)} custom-call(f32[384,384]{1,0:T(8,128)} %bitcast.16, s32[27,1,384]{2,1,0:T(1,128)} %nbr_ref.1, f32[27,384]{1,0:T(8,128)} %weight_ref.1), custom_call_target="tpu_custom_call" | custom-call | flops 3000000000 | bytes 1000000 | tf_op jit(solution)/shard_map/inner/pallas_call | solution.py:467
  11.9 0.0 copy-start.5
  11.9 0.0 copy-start.6
  11.9 0.0 copy-start.9
  11.9 0.0 collective-permute-done.1.other_ref
  11.9 0.0 collective-permute-done.mate_ref
  12.0 0.0 copy-done
  12.0 0.0 copy-done.10
  12.0 0.0 copy-done.11
  12.0 1.8 %edges.1.first_ref = f32[1152,128]{1,0:T(8,128)S(1)} custom-call(f32[384,384]{1,0:T(8,128)S(1)} %bitcast.17, f32[64,384]{1,0:T(8,128)S(1)} %collective-permute-done.mate_ref, f32[64,384]{1,0:T(8,128)S(1)} %collective-permute-done.1.other_ref, s32[27,1,384]{2,1,0:T(1,128)S(1)} %copy-done.11, f32[27,384]{1,0:T(8,128)S(1)} %copy-done.10, ...), custom_call_target="tpu_custom_call" | custom-call | flops 6000000000 | bytes 2000000 | tf_op jit(solution)/shard_map/edges/pallas_call | solution.py:482
  13.8 19.0 %all_to_all.15 = f32[16,72,128]{2,1,0:T(8,128)S(1)} all-to-all(f32[16,72,128]{2,1,0:T(8,128)S(1)} %bitcast.13), channel_id=1, replica_groups=mesh['y'=4,'zh'=2,'c'=2,'x'=4,'zl'=2] {'y','zh','c'}, dimensions={0} | all-to-all | bytes 1179648 | tf_op jit(solution)/shard_map/all_to_all | solution.py:519
  32.8 0.0 copy-done.5
  32.8 0.0 copy-done.6
  32.8 0.0 copy-done.9
  32.8 0.0 copy-start.1
  32.8 5.9 %attention.1 = f32[1152,128]{1,0:T(8,128)} custom-call(f32[1152,128]{1,0:T(8,128)S(1)} %bitcast.15, f32[384,1152]{1,0:T(8,128)S(1)} %copy-done.5, f32[384,384]{1,0:T(8,128)S(1)} %copy-done.6, f32[24,32,32]{2,1,0:T(8,128)S(1)} %copy-done.9), custom_call_target="tpu_custom_call" | custom-call | flops 8000000000 | bytes 4000000 | tf_op jit(solution)/shard_map/attention/pallas_call | solution.py:524
  38.7 3.8 %all-to-all-start.1 = ((f32[16,72,128]{2,1,0:T(8,128)}), f32[16,72,128]{2,1,0:T(8,128)S(1)}, u32[]{:S(2)}, u32[]{:S(2)}) async-start(f32[16,72,128]{2,1,0:T(8,128)} %bitcast.5), calls=%async_computation.1 | async-start | bytes 1179648 | tf_op jit(solution)/shard_map/all_to_all | solution.py:519
  42.5 0.0 copy-done.1
  42.5 0.0 copy-start.3
  42.5 1.7 %copy-done.3 = f32[1536,384]{1,0:T(8,128)S(1)} copy-done((f32[1536,384]{1,0:T(8,128)S(1)}, f32[1536,384]{1,0:T(8,128)}, u32[]{:S(2)}) %copy-start.3) | copy-done | bytes 2359320
  44.2 0.0 copy-start.7
  44.2 1.1 copy-done.7
  45.2 5.1 %prepare.1 = (f32[384,1536]{1,0:T(8,128)}, bf16[384,1536]{1,0:T(8,128)(2,1)}, bf16[384,1536]{1,0:T(8,128)(2,1)}, bf16[768,384]{1,0:T(8,128)(2,1)}) custom-call(f32[384,384]{1,0:T(8,128)S(1)} %bitcast.18, f32[384,1536]{1,0:T(8,128)S(1)} %copy-done.1, f32[1536,384]{1,0:T(8,128)S(1)} %copy-done.3), custom_call_target="tpu_custom_call" | custom-call | flops 4000000000 | bytes 12000000 | tf_op jit(solution)/shard_map/prepare/pallas_call | solution.py:493
  50.3 5.0 %all-to-all-done.1 = f32[16,72,128]{2,1,0:T(8,128)S(1)} async-done(((f32[16,72,128]{2,1,0:T(8,128)}), f32[16,72,128]{2,1,0:T(8,128)S(1)}, u32[]{:S(2)}, u32[]{:S(2)}) %all-to-all-start.1) | async-done | bytes 589856 | tf_op jit(solution)/shard_map/all_to_all | solution.py:519
  55.3 10.2 %gradient.1 = (f32[384,384]{1,0:T(8,128)}, bf16[3,768,512]{2,1,0:T(8,128)(2,1)}, bf16[3,768,512]{2,1,0:T(8,128)(2,1)}, f32[64,72,128]{2,1,0:T(8,128)S(1)}, f32[64,72,128]{2,1,0:T(8,128)S(1)}) custom-call(f32[1152,128]{1,0:T(8,128)S(1)} %edges.1.first_ref, f32[1152,128]{1,0:T(8,128)S(1)} %bitcast.14, f32[384,1536]{1,0:T(8,128)} %get-tuple-element.17.d_active_hbm, ...), custom_call_target="tpu_custom_call" | custom-call | flops 12000000000 | bytes 16000000 | tf_op jit(solution)/shard_map/gradient/pallas_call | solution.py:538
  65.5 0.1 collective-permute-start.2
  65.6 4.5 %collective-permute-done.2 = f32[64,72,128]{2,1,0:T(8,128)S(1)} collective-permute-done((f32[64,72,128]{2,1,0:T(8,128)S(1)}, f32[64,72,128]{2,1,0:T(8,128)S(1)}, u32[]{:S(2)}, u32[]{:S(2)}) %collective-permute-start.2) | collective-permute-done | bytes 2359328 | tf_op jit(solution)/shard_map/ppermute | solution.py:569
  70.1 1.8 %add.3 = f32[64,72,128]{2,1,0:T(8,128)} add(f32[64,72,128]{2,1,0:T(8,128)S(1)} %get-tuple-element.26, f32[64,72,128]{2,1,0:T(8,128)S(1)} %collective-permute-done.2) | non-fusion elementwise | flops 589824 | bytes 7077888 | tf_op jit(solution)/shard_map/add | solution.py:590
  71.8 0.0 copy-start.8
  71.8 0.0 copy-start.14
  71.8 6.3 %all-to-all-start.2 = ((f32[64,72,128]{2,1,0:T(8,128)}), f32[64,72,128]{2,1,0:T(8,128)S(1)}, u32[]{:S(2)}, u32[]{:S(2)}) async-start(f32[64,72,128]{2,1,0:T(8,128)} %add.3), calls=%async_computation.2 | async-start | bytes 4718592 | tf_op jit(solution)/shard_map/all_to_all | solution.py:590
  78.1 0.0 copy-done.8
  78.1 0.0 copy-done.14
  78.2 0.0 copy-start.2
  78.2 1.7 %copy-done.2 = f32[384,1536]{1,0:T(8,128)S(1)} copy-done((f32[384,1536]{1,0:T(8,128)S(1)}, f32[384,1536]{1,0:T(8,128)}, u32[]{:S(2)}) %copy-start.2) | copy-done | bytes 2359320
  79.8 0.0 copy-start.4
  79.8 1.7 %copy-done.4 = f32[1536,384]{1,0:T(8,128)S(1)} copy-done((f32[1536,384]{1,0:T(8,128)S(1)}, f32[1536,384]{1,0:T(8,128)}, u32[]{:S(2)}) %copy-start.4) | copy-done | bytes 2359320
  81.5 0.0 copy-start.12
  81.5 1.7 %copy-done.12 = bf16[3,768,512]{2,1,0:T(8,128)(2,1)S(1)} copy-done((bf16[3,768,512]{2,1,0:T(8,128)(2,1)S(1)}, bf16[3,768,512]{2,1,0:T(8,128)(2,1)}, u32[]{:S(2)}) %copy-start.12) | copy-done | bytes 2359320
  83.2 0.0 copy-start.13
  83.2 1.7 %copy-done.13 = bf16[3,768,512]{2,1,0:T(8,128)(2,1)S(1)} copy-done((bf16[3,768,512]{2,1,0:T(8,128)(2,1)S(1)}, bf16[3,768,512]{2,1,0:T(8,128)(2,1)}, u32[]{:S(2)}) %copy-start.13) | copy-done | bytes 2359320
  84.8 6.1 %outputs.1 = (f32[384,384]{1,0:T(8,128)}, f32[384,384]{1,0:T(8,128)}) custom-call(f32[384,384]{1,0:T(8,128)S(1)} %copy-done.14, f32[384,384]{1,0:T(8,128)S(1)} %bitcast.19, bf16[3,768,512]{2,1,0:T(8,128)(2,1)S(1)} %copy-done.12, bf16[3,768,512]{2,1,0:T(8,128)(2,1)S(1)} %copy-done.13, f32[384,1536]{1,0:T(8,128)S(1)} %copy-done.2, f32[1536,384]{1,0:T(8,128)S(1)} %copy-done.4), custom_call_target="tpu_custom_call" | custom-call | flops 6000000000 | bytes 11000000 | tf_op jit(solution)/shard_map/outputs/pallas_call | solution.py:572
  90.9 20.5 %all-to-all-done.2.pieces_ref = f32[64,72,128]{2,1,0:T(8,128)S(1)} async-done(((f32[64,72,128]{2,1,0:T(8,128)}), f32[64,72,128]{2,1,0:T(8,128)S(1)}, u32[]{:S(2)}, u32[]{:S(2)}) %all-to-all-start.2) | async-done | bytes 2359328 | tf_op jit(solution)/shard_map/all_to_all | solution.py:590
  111.4 0.8 finish.1
Async XLA Ops:
  1.6 10.3 %collective-permute-start.1 = (f32[64,384]{1,0:T(8,128)S(1)}, f32[64,384]{1,0:T(8,128)S(1)}, u32[]{:S(2)}, u32[]{:S(2)}) collective-permute-start(f32[64,384]{1,0:T(8,128)S(1)} %get-tuple-element.30), channel_id=1, source_target_pairs={{8,16},{24,32},{40,48},{56,64},{72,80},{88,96},{104,112},{16,8},{3... | collective-permute-start | bytes 294920 | tf_op jit(solution)/shard_map/ppermute | solution.py:464
  2.3 9.7 %collective-permute-start = (f32[64,384]{1,0:T(8,128)S(1)}, f32[64,384]{1,0:T(8,128)S(1)}, u32[]{:S(2)}, u32[]{:S(2)}) collective-permute-start(f32[64,384]{1,0:T(8,128)S(1)} %get-tuple-element.31), channel_id=1, source_target_pairs={{0,8},{8,0},{16,24},{24,16},{32,40},{40,32},{48,56},{56,48},{64,72... | collective-permute-start | bytes 294920 | tf_op jit(solution)/shard_map/ppermute | solution.py:465
  7.7 4.3 %copy-start = (f32[1,384,384]{2,1,0:T(8,128)S(1)}, f32[1,384,384]{2,1,0:T(8,128)}, u32[]{:S(2)}) copy-start(f32[1,384,384]{2,1,0:T(8,128)} %param.9) | copy-start | bytes 1769476
  7.7 4.3 %copy-start.10 = (f32[27,384]{1,0:T(8,128)S(1)}, f32[27,384]{1,0:T(8,128)}, u32[]{:S(2)}) copy-start(f32[27,384]{1,0:T(8,128)} %weight_ref.1) | copy-start | bytes 124420
  7.7 4.3 %copy-start.11 = (s32[27,1,384]{2,1,0:T(1,128)S(1)}, s32[27,1,384]{2,1,0:T(1,128)}, u32[]{:S(2)}) copy-start(s32[27,1,384]{2,1,0:T(1,128)} %nbr_ref.1) | copy-start | bytes 124420
  11.9 20.9 %copy-start.5 = (f32[384,1152]{1,0:T(8,128)S(1)}, f32[384,1152]{1,0:T(8,128)}, u32[]{:S(2)}) copy-start(f32[384,1152]{1,0:T(8,128)} %qkv_ref.1) | copy-start | bytes 5308420
  11.9 20.8 %copy-start.6 = (f32[384,384]{1,0:T(8,128)S(1)}, f32[384,384]{1,0:T(8,128)}, u32[]{:S(2)}) copy-start(f32[384,384]{1,0:T(8,128)} %wout_ref.1) | copy-start | bytes 1769476
  11.9 20.8 %copy-start.9 = (f32[24,32,32]{2,1,0:T(8,128)S(1)}, f32[24,32,32]{2,1,0:T(8,128)}, u32[]{:S(2)}) copy-start(f32[24,32,32]{2,1,0:T(8,128)} %bias_ref.1) | copy-start | bytes 294916
  32.8 9.7 %copy-start.1 = (f32[384,1536]{1,0:T(8,128)S(1)}, f32[384,1536]{1,0:T(8,128)}, u32[]{:S(2)}) copy-start(f32[384,1536]{1,0:T(8,128)} %up_ref.3) | copy-start | bytes 7077892
  38.7 16.6 %all-to-all-start.1 = ((f32[16,72,128]{2,1,0:T(8,128)}), f32[16,72,128]{2,1,0:T(8,128)S(1)}, u32[]{:S(2)}, u32[]{:S(2)}) async-start(f32[16,72,128]{2,1,0:T(8,128)} %bitcast.5), calls=%async_computation.1 | async-start | bytes 1179648 | tf_op jit(solution)/shard_map/all_to_all | solution.py:519
  42.5 1.7 %copy-start.3 = (f32[1536,384]{1,0:T(8,128)S(1)}, f32[1536,384]{1,0:T(8,128)}, u32[]{:S(2)}) copy-start(f32[1536,384]{1,0:T(8,128)} %down_ref.3) | copy-start | bytes 7077892
  44.2 1.1 copy-start.7
  65.5 4.6 %collective-permute-start.2 = (f32[64,72,128]{2,1,0:T(8,128)S(1)}, f32[64,72,128]{2,1,0:T(8,128)S(1)}, u32[]{:S(2)}, u32[]{:S(2)}) collective-permute-start(f32[64,72,128]{2,1,0:T(8,128)S(1)} %get-tuple-element.27), channel_id=1, source_target_pairs={{0,8},{8,0},{1,9},{9,1},{2,10},{10,2},{3,11},{11,3},{4,12},{12,4},... | collective-permute-start | bytes 7077896 | tf_op jit(solution)/shard_map/ppermute | solution.py:569
  71.8 6.3 %copy-start.8 = (f32[1,384,384]{2,1,0:T(8,128)S(1)}, f32[1,384,384]{2,1,0:T(8,128)}, u32[]{:S(2)}) copy-start(f32[1,384,384]{2,1,0:T(8,128)} %param.11) | copy-start | bytes 1769476
  71.8 6.3 %copy-start.14 = (f32[384,384]{1,0:T(8,128)S(1)}, f32[384,384]{1,0:T(8,128)}, u32[]{:S(2)}) copy-start(f32[384,384]{1,0:T(8,128)} %get-tuple-element.21.mid_ref) | copy-start | bytes 1769476
  71.8 39.5 %all-to-all-start.2 = ((f32[64,72,128]{2,1,0:T(8,128)}), f32[64,72,128]{2,1,0:T(8,128)S(1)}, u32[]{:S(2)}, u32[]{:S(2)}) async-start(f32[64,72,128]{2,1,0:T(8,128)} %add.3), calls=%async_computation.2 | async-start | bytes 4718592 | tf_op jit(solution)/shard_map/all_to_all | solution.py:590
  78.2 1.7 %copy-start.2 = (f32[384,1536]{1,0:T(8,128)S(1)}, f32[384,1536]{1,0:T(8,128)}, u32[]{:S(2)}) copy-start(f32[384,1536]{1,0:T(8,128)} %up_ref.3) | copy-start | bytes 7077892
  79.8 1.7 %copy-start.4 = (f32[1536,384]{1,0:T(8,128)S(1)}, f32[1536,384]{1,0:T(8,128)}, u32[]{:S(2)}) copy-start(f32[1536,384]{1,0:T(8,128)} %down_ref.3) | copy-start | bytes 7077892
  81.5 1.7 %copy-start.12 = (bf16[3,768,512]{2,1,0:T(8,128)(2,1)S(1)}, bf16[3,768,512]{2,1,0:T(8,128)(2,1)}, u32[]{:S(2)}) copy-start(bf16[3,768,512]{2,1,0:T(8,128)(2,1)} %get-tuple-element.22.act_ref) | copy-start | bytes 7077892
  83.2 1.7 %copy-start.13 = (bf16[3,768,512]{2,1,0:T(8,128)(2,1)S(1)}, bf16[3,768,512]{2,1,0:T(8,128)(2,1)}, u32[]{:S(2)}) copy-start(bf16[3,768,512]{2,1,0:T(8,128)(2,1)} %get-tuple-element.23.dh_ref) | copy-start | bytes 7077892

commit v7 on v6

--- a/solution.py
+++ b/solution.py
@@ -303,10 +303,9 @@
         dh_ref[i, :TOK, :], dh_ref[i, TOK:, :] = d_hidden
         grad_down_ref[:, here] = dot_stacked(ct_ref[...], active)
         grad_up_ref[:, here] = dot_stacked(nt_ref[...], d_hidden)
-    stores.append(pltpu.make_async_copy(act_ref, act_hbm, left.at[1]))
-    stores.append(pltpu.make_async_copy(dh_ref, dh_hbm, left.at[2]))
-    stores[1].start()
-    stores[2].start()
+        for ref, hbm, k in ((act_ref, act_hbm, 1 + 2 * i), (dh_ref, dh_hbm, 2 + 2 * i)):
+            stores.append(pltpu.make_async_copy(ref.at[i], hbm.at[i], left.at[k]))
+            stores[-1].start()
     pack(grad_up_ref, grad_down_ref, keep_ref, send_ref)
     for store in stores:
         store.wait()
@@ -553,7 +552,7 @@
             pltpu.VMEM((D, FF), F32),
             pltpu.VMEM((D, FF), F32),
             pltpu.SemaphoreType.DMA((4,)),
-            pltpu.SemaphoreType.DMA((3,)),
+            pltpu.SemaphoreType.DMA((1 + 2 * (FF // SUB),)),
         ],
         compiler_params=params(44),
         cost_estimate=cost(12e9, 16e6),

time: 113 us -> 113 us (level)
  no operation moved by 1% of the time
where the time goes in v7:
time: 113 us
  Pallas kernels  34.6 us (31%)
  waiting for transfers between devices  30 us (27%)
  blocking collectives  19 us (17%)
  starting transfers between devices  16.2 us (14%)
  local copies, waits for them, and re-layouts  9.42 us (8%)
  other arithmetic  2.72 us (2%)
    all_to_all x1, waiting for transfers between devices, on_device(): lax.all_to_all(keep + got, CHIP_AXES, split_axis=0, concat_axis=0, tiled=...  20.5 us
    all_to_all x1, blocking collectives, exchange(): lax.all_to_all(values.reshape(SCENE, 3 * UNITS, 128), SCENE_AXES, split_a...  19 us
    pallas_call x1, Pallas kernels, on_device(): pl.pallas_call(gradient_kernel, out_shape=(pltpu.HBM((TOK, D), F32), pair...  10.8 us
    unnamed x30, local copies, waits for them, and re-layouts  9.42 us
    all_to_all x1, starting transfers between devices, on_device(): lax.all_to_all(keep + got, CHIP_AXES, split_axis=0, concat_axis=0, tiled=...  6.27 us
    pallas_call x1, Pallas kernels, on_device(): pl.pallas_call(output_kernel, grid=(FF // SUB,), out_shape=(shape(TOK, D)...  6.06 us
    pallas_call x1, Pallas kernels, on_device(): pl.pallas_call(attention_kernel, out_shape=shape(3 * TOK, 128), in_specs=...  5.93 us
    ppermute x1, starting transfers between devices, on_device(): mate = lax.ppermute(jnp.where(even, tail, head), SCENE_AXES, mates)  5.42 us
  transfers between devices with their start and end apart: 5, of which 3 were waited for; matrix products, arithmetic and copies ran while one was open for 0% of the time, Pallas kernels for 14%

profile of v7, /device:TPU:0, one launch (start us, length us, event | category | flops | bytes accessed | tf_op | source)
XLA Modules:
  0.0 112.8 jit_solution(5932015112932887100)
XLA Ops:
  0.6 1.0 select_bitcast_fusion
  1.6 0.7 collective-permute-start.1
  2.3 5.4 %collective-permute-start = (f32[64,384]{1,0:T(8,128)S(1)}, f32[64,384]{1,0:T(8,128)S(1)}, u32[]{:S(2)}, u32[]{:S(2)}) collective-permute-start(f32[64,384]{1,0:T(8,128)S(1)} %get-tuple-element.31), channel_id=1, source_target_pairs={{0,8},{8,0},{16,24},{24,16},{32,40},{40,32},{48,56},{56,48},{64,72... | collective-permute-start | bytes 294920 | tf_op jit(solution)/shard_map/ppermute | solution.py:464
  7.7 0.0 copy-start
  7.7 0.0 copy-start.10
  7.7 0.0 copy-start.11
  7.7 4.2 %inner.1.inner_ref = f32[256,384]{1,0:T(8,128)S(1)} custom-call(f32[384,384]{1,0:T(8,128)} %bitcast.16, s32[27,1,384]{2,1,0:T(1,128)} %nbr_ref.1, f32[27,384]{1,0:T(8,128)} %weight_ref.1), custom_call_target="tpu_custom_call" | custom-call | flops 3000000000 | bytes 1000000 | tf_op jit(solution)/shard_map/inner/pallas_call | solution.py:466
  11.9 0.0 copy-start.5
  11.9 0.0 copy-start.6
  11.9 0.0 copy-start.9
  11.9 0.0 collective-permute-done.1.other_ref
  11.9 0.0 collective-permute-done.mate_ref
  12.0 0.0 copy-done
  12.0 0.0 copy-done.10
  12.0 0.0 copy-done.11
  12.0 1.8 %edges.1.first_ref = f32[1152,128]{1,0:T(8,128)S(1)} custom-call(f32[384,384]{1,0:T(8,128)S(1)} %bitcast.17, f32[64,384]{1,0:T(8,128)S(1)} %collective-permute-done.mate_ref, f32[64,384]{1,0:T(8,128)S(1)} %collective-permute-done.1.other_ref, s32[27,1,384]{2,1,0:T(1,128)S(1)} %copy-done.11, f32[27,384]{1,0:T(8,128)S(1)} %copy-done.10, ...), custom_call_target="tpu_custom_call" | custom-call | flops 6000000000 | bytes 2000000 | tf_op jit(solution)/shard_map/edges/pallas_call | solution.py:481
  13.8 19.0 %all_to_all.15 = f32[16,72,128]{2,1,0:T(8,128)S(1)} all-to-all(f32[16,72,128]{2,1,0:T(8,128)S(1)} %bitcast.13), channel_id=1, replica_groups=mesh['y'=4,'zh'=2,'c'=2,'x'=4,'zl'=2] {'y','zh','c'}, dimensions={0} | all-to-all | bytes 1179648 | tf_op jit(solution)/shard_map/all_to_all | solution.py:518
  32.8 0.0 copy-done.5
  32.8 0.0 copy-done.6
  32.8 0.0 copy-done.9
  32.8 0.0 copy-start.1
  32.8 5.9 %attention.1 = f32[1152,128]{1,0:T(8,128)} custom-call(f32[1152,128]{1,0:T(8,128)S(1)} %bitcast.15, f32[384,1152]{1,0:T(8,128)S(1)} %copy-done.5, f32[384,384]{1,0:T(8,128)S(1)} %copy-done.6, f32[24,32,32]{2,1,0:T(8,128)S(1)} %copy-done.9), custom_call_target="tpu_custom_call" | custom-call | flops 8000000000 | bytes 4000000 | tf_op jit(solution)/shard_map/attention/pallas_call | solution.py:523
  38.7 3.8 %all-to-all-start.1 = ((f32[16,72,128]{2,1,0:T(8,128)}), f32[16,72,128]{2,1,0:T(8,128)S(1)}, u32[]{:S(2)}, u32[]{:S(2)}) async-start(f32[16,72,128]{2,1,0:T(8,128)} %bitcast.5), calls=%async_computation.1 | async-start | bytes 1179648 | tf_op jit(solution)/shard_map/all_to_all | solution.py:518
  42.5 0.0 copy-done.1
  42.5 0.0 copy-start.3
  42.5 1.7 %copy-done.3 = f32[1536,384]{1,0:T(8,128)S(1)} copy-done((f32[1536,384]{1,0:T(8,128)S(1)}, f32[1536,384]{1,0:T(8,128)}, u32[]{:S(2)}) %copy-start.3) | copy-done | bytes 2359320
  44.2 0.0 copy-start.7
  44.2 1.1 copy-done.7
  45.2 5.1 %prepare.1 = (f32[384,1536]{1,0:T(8,128)}, bf16[384,1536]{1,0:T(8,128)(2,1)}, bf16[384,1536]{1,0:T(8,128)(2,1)}, bf16[768,384]{1,0:T(8,128)(2,1)}) custom-call(f32[384,384]{1,0:T(8,128)S(1)} %bitcast.18, f32[384,1536]{1,0:T(8,128)S(1)} %copy-done.1, f32[1536,384]{1,0:T(8,128)S(1)} %copy-done.3), custom_call_target="tpu_custom_call" | custom-call | flops 4000000000 | bytes 12000000 | tf_op jit(solution)/shard_map/prepare/pallas_call | solution.py:492
  50.3 5.0 %all-to-all-done.1 = f32[16,72,128]{2,1,0:T(8,128)S(1)} async-done(((f32[16,72,128]{2,1,0:T(8,128)}), f32[16,72,128]{2,1,0:T(8,128)S(1)}, u32[]{:S(2)}, u32[]{:S(2)}) %all-to-all-start.1) | async-done | bytes 589856 | tf_op jit(solution)/shard_map/all_to_all | solution.py:518
  55.3 10.8 %gradient.1 = (f32[384,384]{1,0:T(8,128)}, bf16[3,768,512]{2,1,0:T(8,128)(2,1)}, bf16[3,768,512]{2,1,0:T(8,128)(2,1)}, f32[64,72,128]{2,1,0:T(8,128)S(1)}, f32[64,72,128]{2,1,0:T(8,128)S(1)}) custom-call(f32[1152,128]{1,0:T(8,128)S(1)} %edges.1.first_ref, f32[1152,128]{1,0:T(8,128)S(1)} %bitcast.14, f32[384,1536]{1,0:T(8,128)} %get-tuple-element.17.d_active_hbm, ...), custom_call_target="tpu_custom_call" | custom-call | flops 12000000000 | bytes 16000000 | tf_op jit(solution)/shard_map/gradient/pallas_call | solution.py:537
  66.1 0.1 collective-permute-start.2
  66.2 4.5 %collective-permute-done.2 = f32[64,72,128]{2,1,0:T(8,128)S(1)} collective-permute-done((f32[64,72,128]{2,1,0:T(8,128)S(1)}, f32[64,72,128]{2,1,0:T(8,128)S(1)}, u32[]{:S(2)}, u32[]{:S(2)}) %collective-permute-start.2) | collective-permute-done | bytes 2359328 | tf_op jit(solution)/shard_map/ppermute | solution.py:568
  70.7 1.8 %add.3 = f32[64,72,128]{2,1,0:T(8,128)} add(f32[64,72,128]{2,1,0:T(8,128)S(1)} %get-tuple-element.26, f32[64,72,128]{2,1,0:T(8,128)S(1)} %collective-permute-done.2) | non-fusion elementwise | flops 589824 | bytes 7077888 | tf_op jit(solution)/shard_map/add | solution.py:589
  72.4 0.0 copy-start.8
  72.4 0.0 copy-start.14
  72.4 6.3 %all-to-all-start.2 = ((f32[64,72,128]{2,1,0:T(8,128)}), f32[64,72,128]{2,1,0:T(8,128)S(1)}, u32[]{:S(2)}, u32[]{:S(2)}) async-start(f32[64,72,128]{2,1,0:T(8,128)} %add.3), calls=%async_computation.2 | async-start | bytes 4718592 | tf_op jit(solution)/shard_map/all_to_all | solution.py:589
  78.7 0.0 copy-done.8
  78.7 0.0 copy-done.14
  78.7 0.0 copy-start.2
  78.8 1.7 %copy-done.2 = f32[384,1536]{1,0:T(8,128)S(1)} copy-done((f32[384,1536]{1,0:T(8,128)S(1)}, f32[384,1536]{1,0:T(8,128)}, u32[]{:S(2)}) %copy-start.2) | copy-done | bytes 2359320
  80.4 0.0 copy-start.4
  80.4 1.7 %copy-done.4 = f32[1536,384]{1,0:T(8,128)S(1)} copy-done((f32[1536,384]{1,0:T(8,128)S(1)}, f32[1536,384]{1,0:T(8,128)}, u32[]{:S(2)}) %copy-start.4) | copy-done | bytes 2359320
  82.1 0.0 copy-start.12
  82.1 1.7 %copy-done.12 = bf16[3,768,512]{2,1,0:T(8,128)(2,1)S(1)} copy-done((bf16[3,768,512]{2,1,0:T(8,128)(2,1)S(1)}, bf16[3,768,512]{2,1,0:T(8,128)(2,1)}, u32[]{:S(2)}) %copy-start.12) | copy-done | bytes 2359320
  83.7 0.0 copy-start.13
  83.7 1.7 %copy-done.13 = bf16[3,768,512]{2,1,0:T(8,128)(2,1)S(1)} copy-done((bf16[3,768,512]{2,1,0:T(8,128)(2,1)S(1)}, bf16[3,768,512]{2,1,0:T(8,128)(2,1)}, u32[]{:S(2)}) %copy-start.13) | copy-done | bytes 2359320
  85.4 6.1 %outputs.1 = (f32[384,384]{1,0:T(8,128)}, f32[384,384]{1,0:T(8,128)}) custom-call(f32[384,384]{1,0:T(8,128)S(1)} %copy-done.14, f32[384,384]{1,0:T(8,128)S(1)} %bitcast.19, bf16[3,768,512]{2,1,0:T(8,128)(2,1)S(1)} %copy-done.12, bf16[3,768,512]{2,1,0:T(8,128)(2,1)S(1)} %copy-done.13, f32[384,1536]{1,0:T(8,128)S(1)} %copy-done.2, f32[1536,384]{1,0:T(8,128)S(1)} %copy-done.4), custom_call_target="tpu_custom_call" | custom-call | flops 6000000000 | bytes 11000000 | tf_op jit(solution)/shard_map/outputs/pallas_call | solution.py:571
  91.5 20.5 %all-to-all-done.2.pieces_ref = f32[64,72,128]{2,1,0:T(8,128)S(1)} async-done(((f32[64,72,128]{2,1,0:T(8,128)}), f32[64,72,128]{2,1,0:T(8,128)S(1)}, u32[]{:S(2)}, u32[]{:S(2)}) %all-to-all-start.2) | async-done | bytes 2359328 | tf_op jit(solution)/shard_map/all_to_all | solution.py:589
  112.0 0.8 finish.1
Async XLA Ops:
  1.6 10.3 %collective-permute-start.1 = (f32[64,384]{1,0:T(8,128)S(1)}, f32[64,384]{1,0:T(8,128)S(1)}, u32[]{:S(2)}, u32[]{:S(2)}) collective-permute-start(f32[64,384]{1,0:T(8,128)S(1)} %get-tuple-element.30), channel_id=1, source_target_pairs={{8,16},{24,32},{40,48},{56,64},{72,80},{88,96},{104,112},{16,8},{3... | collective-permute-start | bytes 294920 | tf_op jit(solution)/shard_map/ppermute | solution.py:463
  2.3 9.7 %collective-permute-start = (f32[64,384]{1,0:T(8,128)S(1)}, f32[64,384]{1,0:T(8,128)S(1)}, u32[]{:S(2)}, u32[]{:S(2)}) collective-permute-start(f32[64,384]{1,0:T(8,128)S(1)} %get-tuple-element.31), channel_id=1, source_target_pairs={{0,8},{8,0},{16,24},{24,16},{32,40},{40,32},{48,56},{56,48},{64,72... | collective-permute-start | bytes 294920 | tf_op jit(solution)/shard_map/ppermute | solution.py:464
  7.7 4.3 %copy-start = (f32[1,384,384]{2,1,0:T(8,128)S(1)}, f32[1,384,384]{2,1,0:T(8,128)}, u32[]{:S(2)}) copy-start(f32[1,384,384]{2,1,0:T(8,128)} %param.9) | copy-start | bytes 1769476
  7.7 4.3 %copy-start.10 = (f32[27,384]{1,0:T(8,128)S(1)}, f32[27,384]{1,0:T(8,128)}, u32[]{:S(2)}) copy-start(f32[27,384]{1,0:T(8,128)} %weight_ref.1) | copy-start | bytes 124420
  7.7 4.3 %copy-start.11 = (s32[27,1,384]{2,1,0:T(1,128)S(1)}, s32[27,1,384]{2,1,0:T(1,128)}, u32[]{:S(2)}) copy-start(s32[27,1,384]{2,1,0:T(1,128)} %nbr_ref.1) | copy-start | bytes 124420
  11.9 20.9 %copy-start.5 = (f32[384,1152]{1,0:T(8,128)S(1)}, f32[384,1152]{1,0:T(8,128)}, u32[]{:S(2)}) copy-start(f32[384,1152]{1,0:T(8,128)} %qkv_ref.1) | copy-start | bytes 5308420
  11.9 20.8 %copy-start.6 = (f32[384,384]{1,0:T(8,128)S(1)}, f32[384,384]{1,0:T(8,128)}, u32[]{:S(2)}) copy-start(f32[384,384]{1,0:T(8,128)} %wout_ref.1) | copy-start | bytes 1769476
  11.9 20.8 %copy-start.9 = (f32[24,32,32]{2,1,0:T(8,128)S(1)}, f32[24,32,32]{2,1,0:T(8,128)}, u32[]{:S(2)}) copy-start(f32[24,32,32]{2,1,0:T(8,128)} %bias_ref.1) | copy-start | bytes 294916
  32.8 9.7 %copy-start.1 = (f32[384,1536]{1,0:T(8,128)S(1)}, f32[384,1536]{1,0:T(8,128)}, u32[]{:S(2)}) copy-start(f32[384,1536]{1,0:T(8,128)} %up_ref.3) | copy-start | bytes 7077892
  38.7 16.6 %all-to-all-start.1 = ((f32[16,72,128]{2,1,0:T(8,128)}), f32[16,72,128]{2,1,0:T(8,128)S(1)}, u32[]{:S(2)}, u32[]{:S(2)}) async-start(f32[16,72,128]{2,1,0:T(8,128)} %bitcast.5), calls=%async_computation.1 | async-start | bytes 1179648 | tf_op jit(solution)/shard_map/all_to_all | solution.py:518
  42.5 1.7 %copy-start.3 = (f32[1536,384]{1,0:T(8,128)S(1)}, f32[1536,384]{1,0:T(8,128)}, u32[]{:S(2)}) copy-start(f32[1536,384]{1,0:T(8,128)} %down_ref.3) | copy-start | bytes 7077892
  44.2 1.1 copy-start.7
  66.1 4.6 %collective-permute-start.2 = (f32[64,72,128]{2,1,0:T(8,128)S(1)}, f32[64,72,128]{2,1,0:T(8,128)S(1)}, u32[]{:S(2)}, u32[]{:S(2)}) collective-permute-start(f32[64,72,128]{2,1,0:T(8,128)S(1)} %get-tuple-element.27), channel_id=1, source_target_pairs={{0,8},{8,0},{1,9},{9,1},{2,10},{10,2},{3,11},{11,3},{4,12},{12,4},... | collective-permute-start | bytes 7077896 | tf_op jit(solution)/shard_map/ppermute | solution.py:568
  72.4 6.3 %copy-start.8 = (f32[1,384,384]{2,1,0:T(8,128)S(1)}, f32[1,384,384]{2,1,0:T(8,128)}, u32[]{:S(2)}) copy-start(f32[1,384,384]{2,1,0:T(8,128)} %param.11) | copy-start | bytes 1769476
  72.4 6.3 %copy-start.14 = (f32[384,384]{1,0:T(8,128)S(1)}, f32[384,384]{1,0:T(8,128)}, u32[]{:S(2)}) copy-start(f32[384,384]{1,0:T(8,128)} %get-tuple-element.21.mid_ref) | copy-start | bytes 1769476
  72.4 39.5 %all-to-all-start.2 = ((f32[64,72,128]{2,1,0:T(8,128)}), f32[64,72,128]{2,1,0:T(8,128)S(1)}, u32[]{:S(2)}, u32[]{:S(2)}) async-start(f32[64,72,128]{2,1,0:T(8,128)} %add.3), calls=%async_computation.2 | async-start | bytes 4718592 | tf_op jit(solution)/shard_map/all_to_all | solution.py:589
  78.7 1.7 %copy-start.2 = (f32[384,1536]{1,0:T(8,128)S(1)}, f32[384,1536]{1,0:T(8,128)}, u32[]{:S(2)}) copy-start(f32[384,1536]{1,0:T(8,128)} %up_ref.3) | copy-start | bytes 7077892
  80.4 1.7 %copy-start.4 = (f32[1536,384]{1,0:T(8,128)S(1)}, f32[1536,384]{1,0:T(8,128)}, u32[]{:S(2)}) copy-start(f32[1536,384]{1,0:T(8,128)} %down_ref.3) | copy-start | bytes 7077892
  82.1 1.7 %copy-start.12 = (bf16[3,768,512]{2,1,0:T(8,128)(2,1)S(1)}, bf16[3,768,512]{2,1,0:T(8,128)(2,1)}, u32[]{:S(2)}) copy-start(bf16[3,768,512]{2,1,0:T(8,128)(2,1)} %get-tuple-element.22.act_ref) | copy-start | bytes 7077892
  83.7 1.7 %copy-start.13 = (bf16[3,768,512]{2,1,0:T(8,128)(2,1)S(1)}, bf16[3,768,512]{2,1,0:T(8,128)(2,1)}, u32[]{:S(2)}) copy-start(bf16[3,768,512]{2,1,0:T(8,128)(2,1)} %get-tuple-element.23.dh_ref) | copy-start | bytes 7077892
